TPU v7x, 32 devices: a whole 2x2x4 slice. The times are simulated.
32 devices in a mesh: dp: 8 (over z, x), fsdp: 4 (over y, core).
Axes of the slice: x: 2, y: 2, z: 4, core: 2. Of those that a mesh axis runs over, the one named last changes fastest.
Arguments:
- tokens: bfloat16 [2, 4096, 2048], P(None, ('dp', 'fsdp')), may hold values from -6 to 6
- membership: int32 [8, 2, 16], P('dp'), may hold values from 0 to 4, as said below
- d_output: bfloat16 [2, 4096, 2048], P(None, ('dp', 'fsdp')), may hold values from -6 to 6
- gain_attn: bfloat16 [2048], P(('dp', 'fsdp')), may hold values from 0.25 to 1.75
- w_qa: bfloat16 [2048, 1024], P(('dp', 'fsdp')), may hold values from -0.125 to 0.125
- gain_latent: bfloat16 [1024], P(('dp', 'fsdp')), may hold values from 0.25 to 1.75
- w_qb: bfloat16 [1024, 4096], P('dp', 'fsdp'), may hold values from -0.1875 to 0.1875
- w_key: bfloat16 [2048, 256], P(('dp', 'fsdp')), may hold values from -0.125 to 0.125
- w_value: bfloat16 [2048, 256], P(('dp', 'fsdp')), may hold values from -0.125 to 0.125
- w_out: bfloat16 [2048, 4096], P('dp', 'fsdp'), may hold values from -0.5 to 0.5
- gain_ffn: bfloat16 [2048], P(('dp', 'fsdp')), may hold values from 0.25 to 1.75
- w_gate: bfloat16 [2048, 5632], P('dp', 'fsdp'), may hold values from -0.125 to 0.125
- w_up: bfloat16 [2048, 5632], P('dp', 'fsdp'), may hold values from -0.125 to 0.125
- w_down: bfloat16 [2048, 5632], P('dp', 'fsdp'), may hold values from -0.078125 to 0.078125
Outputs:
- output: bfloat16 [2, 4096, 2048], P(None, ('dp', 'fsdp'))
- input_grad: bfloat16 [2, 4096, 2048], P(None, ('dp', 'fsdp'))
- grad_gain_attn: float32 [2048], P(('dp', 'fsdp'))
- grad_w_qa: float32 [2048, 1024], P(('dp', 'fsdp'))
- grad_gain_latent: float32 [1024], P(('dp', 'fsdp'))
- grad_w_qb: float32 [1024, 4096], P('dp', 'fsdp')
- grad_w_key: float32 [2048, 256], P(('dp', 'fsdp'))
- grad_w_value: float32 [2048, 256], P(('dp', 'fsdp'))
- grad_w_out: float32 [2048, 4096], P('dp', 'fsdp')
- grad_gain_ffn: float32 [2048], P(('dp', 'fsdp'))
- grad_w_gate: float32 [2048, 5632], P('dp', 'fsdp')
- grad_w_up: float32 [2048, 5632], P('dp', 'fsdp')
- grad_w_down: float32 [2048, 5632], P('dp', 'fsdp')
Inputs may be any that keep to these rules, and one draw needn't show every extreme that they name: `membership`: in each group's row the first 8 entries are 0 (the prompt); the last 8 entries name continuations 1 to 4 in increasing order, each a run of whole blocks; the runs have 4, 2, 1 and 1 blocks, in an order drawn for each group.
All inputs are finite; a program needn't handle non-finite values.
Results may differ from a plain program's by a relative error of at most 0.02.
Values may be sent and summed in bfloat16 or wider, within the bound.
A program may use at most 192 MiB of HBM per device.

v0:
```python
import jax
import jax.numpy as jnp
from jax import lax
from jax.sharding import PartitionSpec as P

BLK = 32


EPSILON = 1e-05
ROPE_BASE = 10000.0
MASK_FILL = -1e30


def shortened(x):

    def short(part):
        return part.astype(jnp.bfloat16) if part.dtype == jnp.float32 else part

    return jax.tree.map(short, x)


def layout(member_row, block_len):
    count_blocks = member_row.shape[0]
    block_ids = jnp.arange(count_blocks, dtype=jnp.int32)
    same_run = (member_row[None, :] == member_row[:, None]) & (
        block_ids[None, :] < block_ids[:, None]
    )
    earlier = jnp.sum(same_run.astype(jnp.int32), axis=1)
    prompt_len = jnp.sum((member_row == 0).astype(jnp.int32)) * block_len
    labels = jnp.repeat(member_row, block_len)
    within = jnp.arange(count_blocks * block_len, dtype=jnp.int32) % block_len
    positions = (
        (labels > 0).astype(jnp.int32) * prompt_len
        + jnp.repeat(earlier, block_len) * block_len
        + within
    )
    return (labels, positions)


def rope_tables(positions, head_width):
    half_width = head_width // 2
    frequency = ROPE_BASE ** (-(jnp.arange(half_width, dtype=jnp.float32) * (2.0 / head_width)))
    angles = positions.astype(jnp.float32)[:, None] * frequency[None, :]
    return (jnp.cos(angles), jnp.sin(angles))


def rotate(vector, cos_tab, sin_tab):
    half_width = vector.shape[-1] // 2
    lower_half = vector[..., :half_width]
    upper_half = vector[..., half_width:]
    return jnp.concatenate(
        [lower_half * cos_tab - upper_half * sin_tab, upper_half * cos_tab + lower_half * sin_tab],
        axis=-1,
    )


def unrotate(vector, cos_tab, sin_tab):
    half_width = vector.shape[-1] // 2
    lower_half = vector[..., :half_width]
    upper_half = vector[..., half_width:]
    return jnp.concatenate(
        [lower_half * cos_tab + upper_half * sin_tab, upper_half * cos_tab - lower_half * sin_tab],
        axis=-1,
    )


def norm_back(grad_in, values, inverse, gain):
    scaled = grad_in * gain
    gain_term = jnp.sum(grad_in * values * inverse, axis=0)
    inner_sum = jnp.mean(scaled * values, axis=-1, keepdims=True)
    return (inverse * scaled - values * inverse * inverse * inverse * inner_sum, gain_term)


def masked_scores(query_part, label_part, index_part, keys_all, labels, key_index, scaling):
    scores = (
        jnp.einsum("qhd,kd->qhk", query_part, keys_all, preferred_element_type=jnp.float32)
        * scaling
    )
    allowed = (key_index[None, :] <= index_part[:, None]) & (
        (labels[None, :] == 0) | (labels[None, :] == label_part[:, None])
    )
    return jnp.where(allowed[:, None, :], scores, MASK_FILL)


def micro_forward(tokens_part, member_row, seq_set, head_set):
    qa_full, key_full, value_full, gain_one, gain_lat, gain_two = seq_set
    qb_full, out_full, gate_full, up_full, down_full = head_set
    labels, positions = layout(member_row, BLK)
    group_len = labels.shape[0]
    own_len = tokens_part.shape[0]
    head_width = key_full.shape[1]
    heads_here = qb_full.shape[1] // head_width
    scaling = head_width ** (-0.5)
    cos_all, sin_all = rope_tables(positions, head_width)
    start_own = lax.axis_index("fsdp") * own_len
    cos_own = lax.dynamic_slice_in_dim(cos_all, start_own, own_len, 0)
    sin_own = lax.dynamic_slice_in_dim(sin_all, start_own, own_len, 0)
    inputs = tokens_part.astype(jnp.float32)
    inv_one = lax.rsqrt(jnp.mean(inputs * inputs, axis=-1, keepdims=True) + EPSILON)
    normed = (inputs * inv_one * gain_one).astype(jnp.bfloat16)
    latent = jnp.dot(normed, qa_full, preferred_element_type=jnp.float32)
    inv_lat = lax.rsqrt(jnp.mean(latent * latent, axis=-1, keepdims=True) + EPSILON)
    latent_n = (latent * inv_lat * gain_lat).astype(jnp.bfloat16)
    key_own = rotate(
        jnp.dot(normed, key_full, preferred_element_type=jnp.float32), cos_own, sin_own
    ).astype(jnp.bfloat16)
    value_own = jnp.dot(normed, value_full, preferred_element_type=jnp.float32).astype(jnp.bfloat16)
    latent_all, keys_all, values_all = (
        lax.all_gather(latent_n, "fsdp", axis=0, tiled=True),
        lax.all_gather(key_own, "fsdp", axis=0, tiled=True),
        lax.all_gather(value_own, "fsdp", axis=0, tiled=True),
    )
    queries = jnp.dot(latent_all, qb_full, preferred_element_type=jnp.float32).reshape(
        group_len, heads_here, head_width
    )
    queries = rotate(queries, cos_all[:, None, :], sin_all[:, None, :]).astype(jnp.bfloat16)
    q_block = min(256, group_len)
    n_blocks = group_len // q_block
    key_index = jnp.arange(group_len, dtype=jnp.int32)
    query_blocks = queries.reshape(n_blocks, q_block, heads_here, head_width)
    label_blocks = labels.reshape(n_blocks, q_block)
    index_blocks = key_index.reshape(n_blocks, q_block)

    def attend(block_items):
        query_part, label_part, index_part = block_items
        scores = masked_scores(
            query_part, label_part, index_part, keys_all, labels, key_index, scaling
        )
        row_max = jnp.max(scores, axis=-1, keepdims=True)
        lifted = jnp.exp(scores - row_max)
        row_sum = jnp.sum(lifted, axis=-1, keepdims=True)
        attn_probs = (lifted / row_sum).astype(jnp.bfloat16)
        mixed_part = jnp.einsum(
            "qhk,kd->qhd", attn_probs, values_all, preferred_element_type=jnp.float32
        )
        return (mixed_part, (row_max + jnp.log(row_sum))[..., 0])

    mixed_blocks, log_blocks = lax.map(attend, (query_blocks, label_blocks, index_blocks))
    mixed_rows = mixed_blocks.reshape(group_len, heads_here * head_width).astype(jnp.bfloat16)
    row_part = mixed_rows
    attn_own = lax.psum_scatter(
        jnp.einsum("rc,dc->rd", row_part, out_full, preferred_element_type=jnp.float32),
        "fsdp",
        scatter_dimension=0,
        tiled=True,
    )
    middle = inputs + attn_own
    inv_two = lax.rsqrt(jnp.mean(middle * middle, axis=-1, keepdims=True) + EPSILON)
    normed_two = (middle * inv_two * gain_two).astype(jnp.bfloat16)
    normed_all = lax.all_gather(normed_two, "fsdp", axis=0, tiled=True)
    gate_pre = jnp.dot(normed_all, gate_full, preferred_element_type=jnp.float32)
    up_pre = jnp.dot(normed_all, up_full, preferred_element_type=jnp.float32)
    hidden = (jax.nn.silu(gate_pre) * up_pre).astype(jnp.bfloat16)
    row_part = hidden
    ffn_own = lax.psum_scatter(
        jnp.einsum("rf,df->rd", row_part, down_full, preferred_element_type=jnp.float32).astype(
            jnp.bfloat16
        ),
        "fsdp",
        scatter_dimension=0,
        tiled=True,
    ).astype(jnp.float32)
    output = (middle + ffn_own).astype(jnp.bfloat16)
    kept = (
        inputs,
        inv_one,
        normed,
        latent,
        inv_lat,
        latent_all,
        keys_all,
        values_all,
        query_blocks,
        label_blocks,
        index_blocks,
        log_blocks,
        mixed_rows,
        middle,
        inv_two,
        normed_all,
        gate_pre,
        up_pre,
        hidden,
        cos_own,
        sin_own,
        cos_all,
        sin_all,
        labels,
        key_index,
    )
    return (output, kept)


def micro_backward(dout_part, kept, seq_set, head_set):
    qa_full, key_full, value_full, gain_one, gain_lat, gain_two = seq_set
    qb_back, out_back, gate_back, up_back, down_back = head_set
    (
        inputs,
        inv_one,
        normed,
        latent,
        inv_lat,
        latent_all,
        keys_all,
        values_all,
        query_blocks,
        label_blocks,
        index_blocks,
        log_blocks,
        mixed_rows,
        middle,
        inv_two,
        normed_all,
        gate_pre,
        up_pre,
        hidden,
        cos_own,
        sin_own,
        cos_all,
        sin_all,
        labels,
        key_index,
    ) = kept
    group_len = labels.shape[0]
    n_blocks, q_block, heads_here, head_width = query_blocks.shape
    scaling = head_width ** (-0.5)
    grad_out = dout_part.astype(jnp.float32)
    grad_ffn_all = lax.all_gather(dout_part, "fsdp", axis=0, tiled=True)
    grad_hidden = jnp.dot(grad_ffn_all, down_back, preferred_element_type=jnp.float32)
    grad_wdown = jnp.einsum("gd,gf->df", grad_ffn_all, hidden, preferred_element_type=jnp.float32)
    sigmoid_g = jax.nn.sigmoid(gate_pre)
    grad_gate = (grad_hidden * up_pre * sigmoid_g * (1.0 + gate_pre * (1.0 - sigmoid_g))).astype(
        jnp.bfloat16
    )
    grad_up = (grad_hidden * gate_pre * sigmoid_g).astype(jnp.bfloat16)
    grad_wgate = jnp.einsum("gd,gf->df", normed_all, grad_gate, preferred_element_type=jnp.float32)
    grad_wup = jnp.einsum("gd,gf->df", normed_all, grad_up, preferred_element_type=jnp.float32)
    grad_norm_two = lax.psum_scatter(
        jnp.einsum("rf,df->rd", grad_gate, gate_back, preferred_element_type=jnp.float32)
        + jnp.einsum("rf,df->rd", grad_up, up_back, preferred_element_type=jnp.float32),
        "fsdp",
        scatter_dimension=0,
        tiled=True,
    )
    grad_mid_norm, grad_gain_two = norm_back(grad_norm_two, middle, inv_two, gain_two)
    grad_middle = grad_out + grad_mid_norm
    grad_proj_all = lax.all_gather(grad_middle.astype(jnp.bfloat16), "fsdp", axis=0, tiled=True)
    grad_wout = jnp.einsum(
        "gd,gc->dc", grad_proj_all, mixed_rows, preferred_element_type=jnp.float32
    )
    grad_mixed = jnp.einsum(
        "gd,dc->gc", grad_proj_all, out_back, preferred_element_type=jnp.float32
    ).astype(jnp.bfloat16)
    grad_mixed = grad_mixed.reshape(n_blocks, q_block, heads_here, head_width)

    def attend_back(carried, block_items):
        grad_keys, grad_values = carried
        query_part, label_part, index_part, log_part, grad_part = block_items
        scores = masked_scores(
            query_part, label_part, index_part, keys_all, labels, key_index, scaling
        )
        attn_probs = jnp.exp(scores - log_part[..., None])
        probs_low = attn_probs.astype(jnp.bfloat16)
        grad_probs = jnp.einsum(
            "qhd,kd->qhk", grad_part, values_all, preferred_element_type=jnp.float32
        )
        grad_values = grad_values + jnp.einsum(
            "qhk,qhd->kd", probs_low, grad_part, preferred_element_type=jnp.float32
        )
        inner_sum = jnp.sum(attn_probs * grad_probs, axis=-1, keepdims=True)
        grad_scores = (attn_probs * (grad_probs - inner_sum)).astype(jnp.bfloat16)
        grad_query = (
            jnp.einsum("qhk,kd->qhd", grad_scores, keys_all, preferred_element_type=jnp.float32)
            * scaling
        )
        grad_keys = (
            grad_keys
            + jnp.einsum("qhk,qhd->kd", grad_scores, query_part, preferred_element_type=jnp.float32)
            * scaling
        )
        return ((grad_keys, grad_values), grad_query)

    zero_rows = jnp.zeros((group_len, head_width), jnp.float32)
    (grad_keys_part, grad_values_part), grad_query_blocks = lax.scan(
        attend_back,
        (zero_rows, zero_rows),
        (query_blocks, label_blocks, index_blocks, log_blocks, grad_mixed),
    )
    grad_query = unrotate(
        grad_query_blocks.reshape(group_len, heads_here, head_width),
        cos_all[:, None, :],
        sin_all[:, None, :],
    )
    grad_query = grad_query.astype(jnp.bfloat16).reshape(group_len, heads_here * head_width)
    grad_wqb = jnp.einsum("gr,gc->rc", latent_all, grad_query, preferred_element_type=jnp.float32)
    grad_latent_part = jnp.einsum(
        "gc,rc->gr", grad_query, qb_back, preferred_element_type=jnp.float32
    )
    grad_lat_own, grad_key_own, grad_value_own = (
        lax.psum_scatter(
            grad_latent_part.astype(jnp.bfloat16), "fsdp", scatter_dimension=0, tiled=True
        ).astype(jnp.float32),
        lax.psum_scatter(
            grad_keys_part.astype(jnp.bfloat16), "fsdp", scatter_dimension=0, tiled=True
        ).astype(jnp.float32),
        lax.psum_scatter(
            grad_values_part.astype(jnp.bfloat16), "fsdp", scatter_dimension=0, tiled=True
        ).astype(jnp.float32),
    )
    grad_key_low = unrotate(grad_key_own, cos_own, sin_own).astype(jnp.bfloat16)
    grad_value_low = grad_value_own.astype(jnp.bfloat16)
    grad_latent_raw, grad_gain_lat = norm_back(grad_lat_own, latent, inv_lat, gain_lat)
    grad_latent_low = grad_latent_raw.astype(jnp.bfloat16)
    grad_wqa = jnp.einsum("td,tr->dr", normed, grad_latent_low, preferred_element_type=jnp.float32)
    grad_wkey = jnp.einsum("td,te->de", normed, grad_key_low, preferred_element_type=jnp.float32)
    grad_wvalue = jnp.einsum(
        "td,te->de", normed, grad_value_low, preferred_element_type=jnp.float32
    )
    grad_normed = jnp.einsum(
        "tr,dr->td", grad_latent_low, qa_full, preferred_element_type=jnp.float32
    )
    grad_normed = grad_normed + jnp.einsum(
        "te,de->td", grad_key_low, key_full, preferred_element_type=jnp.float32
    )
    grad_normed = grad_normed + jnp.einsum(
        "te,de->td", grad_value_low, value_full, preferred_element_type=jnp.float32
    )
    grad_in_norm, grad_gain_one = norm_back(grad_normed, inputs, inv_one, gain_one)
    input_grad = (grad_middle + grad_in_norm).astype(jnp.bfloat16)
    head_part = (grad_wqb, grad_wout, grad_wgate, grad_wup, grad_wdown)
    seq_part = (grad_wqa, grad_wkey, grad_wvalue, grad_gain_one, grad_gain_lat, grad_gain_two)
    return (input_grad, head_part, seq_part)


def per_device(
    tokens,
    membership,
    d_output,
    gain_attn,
    w_qa,
    gain_latent,
    w_qb,
    w_key,
    w_value,
    w_out,
    gain_ffn,
    w_gate,
    w_up,
    w_down,
):
    seq_full = (
        lax.all_gather(w_qa, ("dp", "fsdp"), axis=0, tiled=True),
        lax.all_gather(w_key, ("dp", "fsdp"), axis=0, tiled=True),
        lax.all_gather(w_value, ("dp", "fsdp"), axis=0, tiled=True),
        lax.all_gather(gain_attn, ("dp", "fsdp"), axis=0, tiled=True),
        lax.all_gather(gain_latent, ("dp", "fsdp"), axis=0, tiled=True),
        lax.all_gather(gain_ffn, ("dp", "fsdp"), axis=0, tiled=True),
    )
    seq_set = (
        seq_full[0],
        seq_full[1],
        seq_full[2],
        seq_full[3].astype(jnp.float32),
        seq_full[4].astype(jnp.float32),
        seq_full[5].astype(jnp.float32),
    )
    micro_count = tokens.shape[0]
    head_total = None
    seq_total = None
    output_rows = []
    input_rows = []
    for micro in range(micro_count):
        forward_set = (
            lax.all_gather(w_qb, "dp", axis=0, tiled=True),
            lax.all_gather(w_out, "dp", axis=0, tiled=True),
            lax.all_gather(w_gate, "dp", axis=0, tiled=True),
            lax.all_gather(w_up, "dp", axis=0, tiled=True),
            lax.all_gather(w_down, "dp", axis=0, tiled=True),
        )
        output_part, kept = micro_forward(tokens[micro], membership[0, micro], seq_set, forward_set)
        backward_set = (
            lax.all_gather(w_qb, "dp", axis=0, tiled=True),
            lax.all_gather(w_out, "dp", axis=0, tiled=True),
            lax.all_gather(w_gate, "dp", axis=0, tiled=True),
            lax.all_gather(w_up, "dp", axis=0, tiled=True),
            lax.all_gather(w_down, "dp", axis=0, tiled=True),
        )
        input_part, head_part, seq_part = micro_backward(
            d_output[micro], kept, seq_set, backward_set
        )
        head_total = (
            head_part
            if head_total is None
            else tuple((running + latest for running, latest in zip(head_total, head_part)))
        )
        seq_total = (
            seq_part
            if seq_total is None
            else tuple((running + latest for running, latest in zip(seq_total, seq_part)))
        )
        output_rows.append(output_part)
        input_rows.append(input_part)
    head_sums = jax.tree.map(
        lambda part: part.astype(jnp.float32),
        lax.psum_scatter(shortened(head_total), "dp", scatter_dimension=0, tiled=True),
    )
    seq_sums = lax.psum_scatter(seq_total, ("dp", "fsdp"), scatter_dimension=0, tiled=True)
    output = jnp.stack(output_rows, axis=0)
    input_grad = jnp.stack(input_rows, axis=0)
    return (
        output,
        input_grad,
        seq_sums[3],
        seq_sums[0],
        seq_sums[4],
        head_sums[0],
        seq_sums[1],
        seq_sums[2],
        head_sums[1],
        seq_sums[5],
        head_sums[2],
        head_sums[3],
        head_sums[4],
    )


def solution(mesh):
    placed = (
        P(None, ("dp", "fsdp"), None),
        P("dp", None, None),
        P(None, ("dp", "fsdp"), None),
        P(("dp", "fsdp")),
        P(("dp", "fsdp"), None),
        P(("dp", "fsdp")),
        P("dp", "fsdp"),
        P(("dp", "fsdp"), None),
        P(("dp", "fsdp"), None),
        P("dp", "fsdp"),
        P(("dp", "fsdp")),
        P("dp", "fsdp"),
        P("dp", "fsdp"),
        P("dp", "fsdp"),
    )
    return jax.shard_map(
        per_device,
        mesh=mesh,
        in_specs=placed,
        out_specs=(
            P(None, ("dp", "fsdp"), None),
            P(None, ("dp", "fsdp"), None),
            P(("dp", "fsdp")),
            P(("dp", "fsdp"), None),
            P(("dp", "fsdp")),
            P("dp", "fsdp"),
            P(("dp", "fsdp"), None),
            P(("dp", "fsdp"), None),
            P("dp", "fsdp"),
            P(("dp", "fsdp")),
            P("dp", "fsdp"),
            P("dp", "fsdp"),
            P("dp", "fsdp"),
        ),
        check_vma=False,
    )
```

profile of v0, /device:TPU:0, one launch (start us, length us, event | category | flops | bytes accessed | tf_op | source)
XLA Modules:
  0.0 2178.5 jit_solution(5856194676266203782)
XLA Ops:
  12.6 42.3 %all-reduce.7 = (bf16[2048]{0:T(1024)(128)(2,1)S(1)}, bf16[1024]{0:T(1024)(128)(2,1)S(1)}, bf16[2048]{0:T(1024)(128)(2,1)S(1)}) all-reduce(bf16[2048]{0:T(1024)(128)(2,1)S(1)} %dynamic-update-slice, bf16[1024]{0:T(1024)(128)(2,1)S(1)} %dynamic-update-slice.1, ...), channel_id=1, replica_groups=mesh['dp'=8,'fsdp'=4] {'dp','fsdp'}, use_global_device_ids=true, to_apply=%add | all-reduce | flops 5120 | bytes 20480
  56.4 19.4 all-gather.19.cloned.1.call-done
  87.5 43.6 %all-gather.25.cloned.1.call-done = bf16[2048,256]{1,0:T(8,128)(2,1)} async-done(((bf16[64,256]{1,0:T(8,128)(2,1)}), bf16[2048,256]{1,0:T(8,128)(2,1)}) %all-gather.25.cloned.1.call-update) | async-done | bytes 1048592 | tf_op jit(solution)/shard_map/all_gather | solution.py:353
  132.7 5.8 all_gather.90
  138.5 48.1 %all-gather.27.cloned.1.call-done = bf16[2048,256]{1,0:T(8,128)(2,1)} async-done(((bf16[64,256]{1,0:T(8,128)(2,1)}), bf16[2048,256]{1,0:T(8,128)(2,1)}) %all-gather.27.cloned.1.call-update) | async-done | bytes 1048592 | tf_op jit(solution)/shard_map/all_gather | solution.py:354
  188.2 5.8 all_gather.92
  194.3 42.5 %all-gather.23.cloned.1.call-done = bf16[1024,1024]{1,0:T(8,128)(2,1)} async-done(((bf16[128,1024]{1,0:T(8,128)(2,1)}), bf16[1024,1024]{1,0:T(8,128)(2,1)}) %all-gather.23.cloned.1.call-update) | async-done | bytes 2097168 | tf_op jit(solution)/shard_map/all_gather | solution.py:374
  236.8 17.2 all-gather.21.cloned.1.call-done
  265.0 6.9 while.56
  275.7 53.7 %all-gather.29.cloned.1.call-done = bf16[2048,1024]{1,0:T(8,128)(2,1)} async-done(((bf16[256,1024]{1,0:T(8,128)(2,1)}), bf16[2048,1024]{1,0:T(8,128)(2,1)}) %all-gather.29.cloned.1.call-update) | async-done | bytes 4194320 | tf_op jit(solution)/shard_map/all_gather | solution.py:375
  329.4 6.9 fusion.174
  338.8 7.6 all_gather.100
  346.8 6.1 all_gather.101
  352.9 4.5 fusion.177
  364.4 7.0 while.57
  380.4 14.7 reduce-scatter.21.cloned.1.call-done
  395.1 47.2 %reduce-scatter.25.cloned.1.call-done = f32[128,2048]{1,0:T(8,128)} async-done(((f32[512,2048]{1,0:T(8,128)}), f32[128,2048]{1,0:T(8,128)}) %reduce-scatter.25.cloned.1.call-update) | async-done | bytes 1048592 | tf_op jit(solution)/shard_map/reduce_scatter | solution.py:141
  448.0 89.0 %all-gather.33.cloned.1.call-done = bf16[2048,1408]{1,0:T(8,128)(2,1)} async-done(((bf16[256,1408]{1,0:T(8,128)(2,1)}), bf16[2048,1408]{1,0:T(8,128)(2,1)}) %all-gather.33.cloned.1.call-update) | async-done | bytes 5767184 | tf_op jit(solution)/shard_map/all_gather | solution.py:376
  537.1 23.0 %all-gather.31.cloned.1.call-done = bf16[512,2048]{1,0:T(8,128)(2,1)} async-done(((bf16[128,2048]{1,0:T(8,128)(2,1)}), bf16[512,2048]{1,0:T(8,128)(2,1)}) %all-gather.31.cloned.1.call-update) | async-done | bytes 2097168 | tf_op jit(solution)/shard_map/all_gather | solution.py:150
  560.0 8.3 fusion.175
  568.3 86.4 %all-gather.35.cloned.1.call-done = bf16[2048,1408]{1,0:T(8,128)(2,1)} async-done(((bf16[256,1408]{1,0:T(8,128)(2,1)}), bf16[2048,1408]{1,0:T(8,128)(2,1)}) %all-gather.35.cloned.1.call-update) | async-done | bytes 5767184 | tf_op jit(solution)/shard_map/all_gather | solution.py:377
  654.7 8.3 fusion.176
  663.0 14.7 all-gather.47.cloned.1.call-done
  677.7 94.7 %all-gather.37.cloned.1.call-done = bf16[2048,1408]{1,0:T(8,128)(2,1)} async-done(((bf16[256,1408]{1,0:T(8,128)(2,1)}), bf16[2048,1408]{1,0:T(8,128)(2,1)}) %all-gather.37.cloned.1.call-update) | async-done | bytes 5767184 | tf_op jit(solution)/shard_map/all_gather | solution.py:378
  772.4 10.3 multiply_convert_fusion.4
  782.7 6.6 fusion.181
  789.3 5.1 convolution_add_fusion.2
  794.5 42.8 %reduce-scatter.29.cloned.1.call-done = f32[128,2048]{1,0:T(8,128)} async-done(((f32[512,2048]{1,0:T(8,128)}), f32[128,2048]{1,0:T(8,128)}) %reduce-scatter.29.cloned.1.call-update) | async-done | bytes 1048592 | tf_op jit(solution)/shard_map/reduce_scatter | solution.py:238
  841.2 22.0 %all-gather.41.cloned.1.call-done = bf16[512,2048]{1,0:T(8,128)(2,1)} async-done(((bf16[128,2048]{1,0:T(8,128)(2,1)}), bf16[512,2048]{1,0:T(8,128)(2,1)}) %all-gather.41.cloned.1.call-update) | async-done | bytes 2097168 | tf_op jit(solution)/shard_map/all_gather | solution.py:150
  863.1 8.5 fusion.179
  871.6 8.1 fusion.180
  879.6 8.1 all-gather.49.cloned.1.call-done
  887.8 10.3 multiply_convert_fusion.2
  898.1 6.5 fusion.183
  904.7 7.9 convolution_add_fusion.1
  912.6 7.8 convolution_convert_fusion.1
  920.8 8.6 convolution_convert_fusion
  929.4 27.8 %reduce-scatter.37.cloned.1.call-done = f32[128,2048]{1,0:T(8,128)} async-done(((f32[512,2048]{1,0:T(8,128)}), f32[128,2048]{1,0:T(8,128)}) %reduce-scatter.37.cloned.1.call-update) | async-done | bytes 1048592 | tf_op jit(solution)/shard_map/reduce_scatter | solution.py:238
  959.3 31.9 %reduce-scatter.23.cloned.1.call-done = bf16[128,2048]{1,0:T(8,128)(2,1)} async-done(((bf16[512,2048]{1,0:T(8,128)(2,1)}), bf16[128,2048]{1,0:T(8,128)(2,1)}) %reduce-scatter.23.cloned.1.call-update) | async-done | bytes 524304 | tf_op jit(solution)/shard_map/reduce_scatter | solution.py:155
  991.2 34.0 %reduce-scatter.27.cloned.1.call-done = bf16[128,2048]{1,0:T(8,128)(2,1)} async-done(((bf16[512,2048]{1,0:T(8,128)(2,1)}), bf16[128,2048]{1,0:T(8,128)(2,1)}) %reduce-scatter.27.cloned.1.call-update) | async-done | bytes 524304 | tf_op jit(solution)/shard_map/reduce_scatter | solution.py:155
  1030.3 21.9 %all-gather.45.cloned.1.call-done = bf16[512,2048]{1,0:T(8,128)(2,1)} async-done(((bf16[128,2048]{1,0:T(8,128)(2,1)}), bf16[512,2048]{1,0:T(8,128)(2,1)}) %all-gather.45.cloned.1.call-update) | async-done | bytes 2097168 | tf_op jit(solution)/shard_map/all_gather | solution.py:247
  1052.2 5.2 convolution_convert_fusion.4
  1059.7 26.6 %while.59 = (s32[]{:T(128)}, f32[512,256]{1,0:T(8,128)}, f32[512,256]{1,0:T(8,128)}, f32[2,256,4,256]{3,1,0,2:T(8,128)}, s32[2,256]{1,0:T(2,128)S(1)}, /*index=5...) while((s32[]{:T(128)}, f32[512,256]{1,0:T(8,128)}, ...), condition=%wide.region_36.37_spmd.clone, body=%wide.region_34.36_spmd.clone.sunk | while | flops 1348337152 | bytes 73438704 | solution.py:284
  1088.6 5.2 convolution_convert_fusion.5
  1096.2 26.1 %while.58 = (s32[]{:T(128)}, f32[512,256]{1,0:T(8,128)}, f32[512,256]{1,0:T(8,128)S(1)}, f32[2,256,4,256]{3,1,0,2:T(8,128)}, s32[2,256]{1,0:T(2,128)S(1)}, /*ind...) while((s32[]{:T(128)}, f32[512,256]{1,0:T(8,128)}, ...), condition=%wide.region_26.27_spmd.clone, body=%wide.region_24.26_spmd.clone.sunk | while | flops 1348337152 | bytes 69244336 | solution.py:284
  1138.3 5.7 fusion.187
  1144.0 5.5 add_convert_fusion.2
  1149.7 5.7 fusion.188
  1155.4 5.5 add_convert_fusion.1
  1161.2 5.4 fusion.88
  1166.6 5.3 fusion.82
  1183.8 4.6 add_convert_fusion.3
  1198.2 19.8 reduce-scatter.31.cloned.1.call-done
  1218.0 27.6 %reduce-scatter.39.cloned.1.call-done = bf16[128,1024]{1,0:T(8,128)(2,1)} async-done(((bf16[512,1024]{1,0:T(8,128)(2,1)}), bf16[128,1024]{1,0:T(8,128)(2,1)}) %reduce-scatter.39.cloned.1.call-update) | async-done | bytes 262160 | tf_op jit(solution)/shard_map/reduce_scatter | solution.py:300
  1250.3 4.7 convolution_add_fusion
  1257.3 101.9 %reduce-scatter.55.cloned.1.call-done = bf16[256,1408]{1,0:T(8,128)(2,1)} async-done(((bf16[2048,1408]{1,0:T(8,128)(2,1)}), bf16[256,1408]{1,0:T(8,128)(2,1)}) %reduce-scatter.55.cloned.1.call-update) | async-done | bytes 720912 | tf_op jit(solution)/shard_map/reduce_scatter | solution.py:405
  1361.5 111.0 %reduce-scatter.57.cloned.1.call-done = bf16[256,1408]{1,0:T(8,128)(2,1)} async-done(((bf16[2048,1408]{1,0:T(8,128)(2,1)}), bf16[256,1408]{1,0:T(8,128)(2,1)}) %reduce-scatter.57.cloned.1.call-update) | async-done | bytes 720912 | tf_op jit(solution)/shard_map/reduce_scatter | solution.py:405
  1474.8 111.6 %reduce-scatter.59.cloned.1.call-done = bf16[256,1408]{0,1:T(8,128)(2,1)} async-done(((bf16[2048,1408]{0,1:T(8,128)(2,1)}), bf16[256,1408]{0,1:T(8,128)(2,1)}) %reduce-scatter.59.cloned.1.call-update) | async-done | bytes 720912 | tf_op jit(solution)/shard_map/reduce_scatter | solution.py:405
  1596.8 40.8 %all-reduce.6 = (f32[2048]{0:T(1024)S(1)}, f32[1024]{0:T(1024)S(1)}, f32[2048]{0:T(1024)S(1)}) all-reduce(f32[2048]{0:T(1024)S(1)} %add.363, f32[1024]{0:T(1024)S(1)} %add.365, f32[2048]{0:T(1024)S(1)} %add.370), channel_id=16, replica_groups=mesh['dp'=8,'fsdp'=4] {'dp','fsdp'}, use_global_device_ids=true, to_apply=%region_44.45.clone | all-reduce | flops 5120 | bytes 40960
  1642.7 15.6 reduce-scatter.47.cloned.1.call-done
  1660.0 88.8 %reduce-scatter.53.cloned.1.call-done = bf16[256,1024]{1,0:T(8,128)(2,1)} async-done(((bf16[2048,1024]{1,0:T(8,128)(2,1)}), bf16[256,1024]{1,0:T(8,128)(2,1)}) %reduce-scatter.53.cloned.1.call-update) | async-done | bytes 524304 | tf_op jit(solution)/shard_map/reduce_scatter | solution.py:405
  1750.9 137.5 %reduce-scatter.49.cloned.1.call-done = f32[64,256]{1,0:T(8,128)} async-done(((f32[2048,256]{1,0:T(8,128)}), f32[64,256]{1,0:T(8,128)}) %reduce-scatter.49.cloned.1.call-update) | async-done | bytes 65552 | tf_op jit(solution)/shard_map/reduce_scatter | solution.py:407
  1888.4 135.7 %reduce-scatter.51.cloned.1.call-done = f32[64,256]{1,0:T(8,128)} async-done(((f32[2048,256]{1,0:T(8,128)}), f32[64,256]{1,0:T(8,128)}) %reduce-scatter.51.cloned.1.call-update) | async-done | bytes 65552 | tf_op jit(solution)/shard_map/reduce_scatter | solution.py:407
  2024.1 147.5 %reduce-scatter.45.cloned.1.call-done = f32[64,1024]{1,0:T(8,128)} async-done(((f32[2048,1024]{1,0:T(8,128)}), f32[64,1024]{1,0:T(8,128)}) %reduce-scatter.45.cloned.1.call-update) | async-done | bytes 262160 | tf_op jit(solution)/shard_map/reduce_scatter | solution.py:407
  (535 shorter events, 212.3 us)
Async XLA Ops:
  7.2 68.6 %all-gather.19.cloned.1.call-start = ((), (), s32[]{:S(2)}) async-start(), calls=%async_computation.20 | async-start | bytes 4325376 | tf_op jit(solution)/shard_map/all_gather | solution.py:352
  7.9 123.1 %all-gather.25.cloned.1.call-start = ((), (), s32[]{:S(2)}) async-start(), calls=%async_computation.23 | async-start | bytes 1081344 | tf_op jit(solution)/shard_map/all_gather | solution.py:353
  8.7 177.9 %all-gather.27.cloned.1.call-start = ((), (), s32[]{:S(2)}) async-start(), calls=%async_computation.24 | async-start | bytes 1081344 | tf_op jit(solution)/shard_map/all_gather | solution.py:354
  9.4 227.4 %all-gather.23.cloned.1.call-start = ((), (), s32[]{:S(2)}) async-start(), calls=%async_computation.22 | async-start | bytes 2359296 | tf_op jit(solution)/shard_map/all_gather | solution.py:374
  10.0 244.0 %all-gather.21.cloned.1.call-start = ((), (), s32[]{:S(2)}) async-start(), calls=%async_computation.21 | async-start | bytes 1310720 | tf_op jit(solution)/shard_map/all_gather | solution.py:109
  54.9 291.6 %copy-start.53 = (f32[2048]{0:T(1024)}, f32[2048]{0:T(1024)S(1)}, u32[]{:S(2)}) copy-start(f32[2048]{0:T(1024)S(1)} %convert_element_type.256) | copy-start | bytes 24580
  54.9 25.4 %copy-start.68 = (f32[1024]{0:T(1024)}, f32[1024]{0:T(1024)S(1)}, u32[]{:S(2)}) copy-start(f32[1024]{0:T(1024)S(1)} %convert_element_type.258) | copy-start | bytes 12292
  56.4 130.2 %copy-start.72 = (f32[128]{0:T(128)}, f32[128]{0:T(128)S(1)}, u32[]{:S(2)}) copy-start(f32[128]{0:T(128)S(1)} %add_rsqrt_fusion.5) | copy-start | bytes 1540
  56.4 290.0 %copy-start.75 = (f32[128]{0:T(128)}, f32[128]{0:T(128)S(1)}, u32[]{:S(2)}) copy-start(f32[128]{0:T(128)S(1)} %add_rsqrt_fusion.2) | copy-start | bytes 1540
  56.4 22.7 %copy-start.8 = (bf16[2,128,2048]{2,1,0:T(8,128)(2,1)S(1)}, bf16[2,128,2048]{2,1,0:T(8,128)(2,1)}, u32[]{:S(2)}) copy-start(bf16[2,128,2048]{2,1,0:T(8,128)(2,1)} %param.22) | copy-start | bytes 3145732
  81.4 248.0 %all-gather.29.cloned.1.call-start = ((), (), s32[]{:S(2)}) async-start(), calls=%async_computation.25 | async-start | bytes 4718592 | tf_op jit(solution)/shard_map/all_gather | solution.py:375
  81.9 271.0 %all-gather.39.cloned.1.call-start = ((), (), s32[]{:S(2)}) async-start(), calls=%async_computation.32 | async-start | bytes 1310720 | tf_op jit(solution)/shard_map/all_gather | solution.py:109
  87.5 175.9 %copy-start.44 = (f32[512,128]{1,0:T(8,128)}, f32[512,128]{1,0:T(8,128)S(1)}, u32[]{:S(2)}) copy-start(f32[512,128]{1,0:T(8,128)S(1)} %get-tuple-element.833) | copy-start | bytes 786436
  87.5 175.9 %copy-start.46 = (f32[512,128]{1,0:T(8,128)}, f32[512,128]{1,0:T(8,128)S(1)}, u32[]{:S(2)}) copy-start(f32[512,128]{1,0:T(8,128)S(1)} %get-tuple-element.834) | copy-start | bytes 786436
  194.0 201.1 %reduce-scatter.21.cloned.1.call-start = ((), (), s32[]{:S(2)}) async-start(), calls=%async_computation.26 | async-start | bytes 5242880 | tf_op jit(solution)/shard_map/reduce_scatter | solution.py:141
  336.4 10.1 copy-start.37
  336.4 106.0 %reduce-scatter.25.cloned.1.call-start = ((), (), s32[]{:S(2)}) async-start(), calls=%async_computation.33 | async-start | bytes 5242880 | tf_op jit(solution)/shard_map/reduce_scatter | solution.py:141
  379.7 157.3 %all-gather.33.cloned.1.call-start = ((), (), s32[]{:S(2)}) async-start(), calls=%async_computation.28 | async-start | bytes 6488064 | tf_op jit(solution)/shard_map/all_gather | solution.py:376
  380.3 179.7 %all-gather.31.cloned.1.call-start = ((), (), s32[]{:S(2)}) async-start(), calls=%async_computation.27 | async-start | bytes 2621440 | tf_op jit(solution)/shard_map/all_gather | solution.py:150
  445.2 209.5 %all-gather.35.cloned.1.call-start = ((), (), s32[]{:S(2)}) async-start(), calls=%async_computation.29 | async-start | bytes 6488064 | tf_op jit(solution)/shard_map/all_gather | solution.py:377
  445.8 231.9 %all-gather.47.cloned.1.call-start = ((), (), s32[]{:S(2)}) async-start(), calls=%async_computation.54 | async-start | bytes 2621440 | tf_op jit(solution)/shard_map/all_gather | solution.py:228
  446.9 325.4 %all-gather.37.cloned.1.call-start = ((), (), s32[]{:S(2)}) async-start(), calls=%async_computation.30 | async-start | bytes 6488064 | tf_op jit(solution)/shard_map/all_gather | solution.py:378
  447.5 389.8 %reduce-scatter.29.cloned.1.call-start = ((), (), s32[]{:S(2)}) async-start(), calls=%async_computation.36 | async-start | bytes 5242880 | tf_op jit(solution)/shard_map/reduce_scatter | solution.py:238
  782.7 6.6 copy-start.93
  782.7 6.6 copy-start.92
  782.7 6.6 copy-start.85
  794.5 68.6 %all-gather.41.cloned.1.call-start = ((), (), s32[]{:S(2)}) async-start(), calls=%async_computation.34 | async-start | bytes 2621440 | tf_op jit(solution)/shard_map/all_gather | solution.py:150
  840.3 47.4 %all-gather.49.cloned.1.call-start = ((), (), s32[]{:S(2)}) async-start(), calls=%async_computation.55 | async-start | bytes 2621440 | tf_op jit(solution)/shard_map/all_gather | solution.py:228
  840.9 116.3 %reduce-scatter.37.cloned.1.call-start = ((), (), s32[]{:S(2)}) async-start(), calls=%async_computation.41 | async-start | bytes 5242880 | tf_op jit(solution)/shard_map/reduce_scatter | solution.py:238
  863.1 8.5 copy-start.88
  898.1 6.5 copy-start.96
  898.1 6.5 copy-start.94
  912.6 78.7 %reduce-scatter.23.cloned.1.call-start = ((), (), s32[]{:S(2)}) async-start(), calls=%async_computation.31 | async-start | bytes 2621440 | tf_op jit(solution)/shard_map/reduce_scatter | solution.py:155
  920.5 104.7 %reduce-scatter.27.cloned.1.call-start = ((), (), s32[]{:S(2)}) async-start(), calls=%async_computation.35 | async-start | bytes 2621440 | tf_op jit(solution)/shard_map/reduce_scatter | solution.py:155
  929.3 95.9 %copy-start.33 = (f32[128,2048]{1,0:T(8,128)S(1)}, f32[128,2048]{1,0:T(8,128)}, u32[]{:S(2)}) copy-start(f32[128,2048]{1,0:T(8,128)} %reduce-scatter.29.cloned.1.call-done) | copy-start | bytes 3145732
  929.4 122.9 %all-gather.45.cloned.1.call-start = ((), (), s32[]{:S(2)}) async-start(), calls=%async_computation.42 | async-start | bytes 2621440 | tf_op jit(solution)/shard_map/all_gather | solution.py:247
  1029.5 59.1 %all-gather.43.cloned.1.call-start = ((), (), s32[]{:S(2)}) async-start(), calls=%async_computation.37 | async-start | bytes 2621440 | tf_op jit(solution)/shard_map/all_gather | solution.py:247
  1030.3 158.5 %reduce-scatter.41.cloned.1.call-start = ((), (), s32[]{:S(2)}) async-start(), calls=%async_computation.44 | async-start | bytes 327680 | tf_op jit(solution)/shard_map/reduce_scatter | solution.py:303
  1088.2 101.5 %reduce-scatter.33.cloned.1.call-start = ((), (), s32[]{:S(2)}) async-start(), calls=%async_computation.39 | async-start | bytes 327680 | tf_op jit(solution)/shard_map/reduce_scatter | solution.py:303
  1124.3 69.7 %reduce-scatter.35.cloned.1.call-start = ((), (), s32[]{:S(2)}) async-start(), calls=%async_computation.40 | async-start | bytes 327680 | tf_op jit(solution)/shard_map/reduce_scatter | solution.py:306
  1125.1 70.3 %reduce-scatter.43.cloned.1.call-start = ((), (), s32[]{:S(2)}) async-start(), calls=%async_computation.45 | async-start | bytes 327680 | tf_op jit(solution)/shard_map/reduce_scatter | solution.py:306
  1125.9 92.0 %reduce-scatter.31.cloned.1.call-start = ((), (), s32[]{:S(2)}) async-start(), calls=%async_computation.38 | async-start | bytes 1310720 | tf_op jit(solution)/shard_map/reduce_scatter | solution.py:300
  1133.1 112.5 %reduce-scatter.39.cloned.1.call-start = ((), (), s32[]{:S(2)}) async-start(), calls=%async_computation.43 | async-start | bytes 1310720 | tf_op jit(solution)/shard_map/reduce_scatter | solution.py:300
  1138.1 221.1 %reduce-scatter.55.cloned.1.call-start = ((), (), s32[]{:S(2)}) async-start(), calls=%async_computation.51 | async-start | bytes 6488064 | tf_op jit(solution)/shard_map/reduce_scatter | solution.py:405
  1138.3 5.7 copy-start.89
  1138.3 5.7 copy-start.97
  1149.6 323.0 %reduce-scatter.57.cloned.1.call-start = ((), (), s32[]{:S(2)}) async-start(), calls=%async_computation.52 | async-start | bytes 6488064 | tf_op jit(solution)/shard_map/reduce_scatter | solution.py:405
  1149.6 5.7 copy-start.90
  1149.6 5.7 copy-start.95
  1160.9 425.6 %reduce-scatter.59.cloned.1.call-start = ((), (), s32[]{:S(2)}) async-start(), calls=%async_computation.53 | async-start | bytes 6488064 | tf_op jit(solution)/shard_map/reduce_scatter | solution.py:405
  1161.1 5.4 copy-start.87
  1161.1 5.4 copy-start.98
  1171.9 486.3 %reduce-scatter.47.cloned.1.call-start = ((), (), s32[]{:S(2)}) async-start(), calls=%async_computation.47 | async-start | bytes 2359296 | tf_op jit(solution)/shard_map/reduce_scatter | solution.py:405
  1178.5 570.3 %reduce-scatter.53.cloned.1.call-start = ((), (), s32[]{:S(2)}) async-start(), calls=%async_computation.50 | async-start | bytes 4718592 | tf_op jit(solution)/shard_map/reduce_scatter | solution.py:405
  1188.5 700.0 %reduce-scatter.49.cloned.1.call-start = ((), (), s32[]{:S(2)}) async-start(), calls=%async_computation.48 | async-start | bytes 2162688 | tf_op jit(solution)/shard_map/reduce_scatter | solution.py:407
  1193.9 830.2 %reduce-scatter.51.cloned.1.call-start = ((), (), s32[]{:S(2)}) async-start(), calls=%async_computation.49 | async-start | bytes 2162688 | tf_op jit(solution)/shard_map/reduce_scatter | solution.py:407
  1198.1 47.5 %copy-start.30 = (f32[128,1024]{1,0:T(8,128)S(1)}, f32[128,1024]{1,0:T(8,128)}, u32[]{:S(2)}) copy-start(f32[128,1024]{1,0:T(8,128)} %copy-done.29) | copy-start | bytes 1572868
  1198.1 47.5 %copy-start.32 = (f32[128,1024]{1,0:T(8,128)S(1)}, f32[128,1024]{1,0:T(8,128)}, u32[]{:S(2)}) copy-start(f32[128,1024]{1,0:T(8,128)} %copy-done.31) | copy-start | bytes 1572868
  1198.1 47.5 %copy-start.69 = (f32[1024]{0:T(1024)S(1)}, f32[1024]{0:T(1024)}, u32[]{:S(2)}) copy-start(f32[1024]{0:T(1024)} %copy-done.68) | copy-start | bytes 12292
  1198.1 47.5 %copy-start.82 = (f32[128]{0:T(128)S(1)}, f32[128]{0:T(128)}, u32[]{:S(2)}) copy-start(f32[128]{0:T(128)} %copy-done.81) | copy-start | bytes 1540
  1198.1 47.5 %copy-start.84 = (f32[128]{0:T(128)S(1)}, f32[128]{0:T(128)}, u32[]{:S(2)}) copy-start(f32[128]{0:T(128)} %copy-done.83) | copy-start | bytes 1540
  1198.1 973.4 %reduce-scatter.45.cloned.1.call-start = ((), (), s32[]{:S(2)}) async-start(), calls=%async_computation.46 | async-start | bytes 8650752 | tf_op jit(solution)/shard_map/reduce_scatter | solution.py:407
  1361.5 227.4 %copy-start.36 = (bf16[2048,256]{1,0:T(8,128)(2,1)S(1)}, bf16[2048,256]{1,0:T(8,128)(2,1)}, u32[]{:S(2)}) copy-start(bf16[2048,256]{1,0:T(8,128)(2,1)} %all-gather.25.cloned.1.call-done) | copy-start | bytes 3145732
  1593.9 45.4 %copy-start.39 = (f32[128,2048]{1,0:T(8,128)S(1)}, f32[128,2048]{1,0:T(8,128)}, u32[]{:S(2)}) copy-start(f32[128,2048]{1,0:T(8,128)} %get-tuple-element.767) | copy-start | bytes 3145732
  (91 other events, 202.2 us)
Sparse Core Ops, SparseCore 0:
  10.9 64.8 all-gather.18
  78.7 52.3 all-gather.24
  133.9 52.6 all-gather.26
  188.6 48.1 all-gather.22
  238.8 15.2 all-gather.20
  256.0 73.3 all-gather.28
  331.5 16.4 all-gather.38
  350.5 44.5 reduce-scatter.20
  397.8 44.5 reduce-scatter.24
  444.4 92.6 all-gather.32
  539.2 20.7 all-gather.30
  562.0 92.6 all-gather.34
  656.9 20.7 all-gather.46
  679.7 92.6 all-gather.36
  794.6 42.7 reduce-scatter.28
  840.5 22.5 all-gather.40
  865.2 22.5 all-gather.48
  912.7 44.5 reduce-scatter.36
  959.8 31.4 reduce-scatter.22
  993.8 31.4 reduce-scatter.26
  1029.6 22.5 all-gather.44
  1054.4 22.5 all-gather.42
  1088.3 20.0 reduce-scatter.40
  1124.4 20.0 reduce-scatter.32
  1147.5 20.0 reduce-scatter.34
  1170.6 20.0 reduce-scatter.42
  1193.1 24.8 reduce-scatter.30
  1220.7 24.8 reduce-scatter.38
  1249.2 109.9 reduce-scatter.54
  1362.7 109.7 reduce-scatter.56
  1476.2 110.2 reduce-scatter.58
  1590.0 68.1 reduce-scatter.46
  1661.7 87.0 reduce-scatter.52
  1751.7 136.6 reduce-scatter.48
  1891.3 132.7 reduce-scatter.50
  2026.9 144.6 reduce-scatter.44
where the time goes:
time: 2190 us; the launch traced here: 2180 us
  waiting for transfers between devices  1690 us (77%)
  matrix products  244 us (11%)
  blocking collectives  108 us (5%)
  local copies, waits for them, and re-layouts  61.8 us (3%)
  other arithmetic  57.1 us (3%)
    reduce_scatter x5, waiting for transfers between devices, per_device(): lax.psum_scatter(shortened(head_total), 'dp', scatter_dimension=0, tiled=...  429 us
    reduce_scatter x3, waiting for transfers between devices, per_device(): lax.psum_scatter(seq_total, ('dp', 'fsdp'), scatter_dimension=0, tiled=True)  421 us
    all_gather x1, waiting for transfers between devices, per_device(): lax.all_gather(w_down, 'dp', axis=0, tiled=True)  94.7 us
    all_gather x1, waiting for transfers between devices, per_device(): lax.all_gather(w_gate, 'dp', axis=0, tiled=True)  89 us
    all_gather x1, waiting for transfers between devices, per_device(): lax.all_gather(w_up, 'dp', axis=0, tiled=True)  86.4 us
    unnamed x2, blocking collectives  83.1 us
    reduce_scatter x2, waiting for transfers between devices, micro_backward(): lax.psum_scatter(jnp.einsum('rf,df->rd', grad_gate, gate_back, preferred_...  70.6 us
    reduce_scatter x2, waiting for transfers between devices, micro_forward(): lax.psum_scatter(jnp.einsum('rf,df->rd', row_part, down_full, preferred_e...  65.9 us
  transfers between devices with their start and end apart: 36, of which 30 were waited for; matrix products, arithmetic and copies ran while one was open for 13% of the time, Pallas kernels for 0%

commit v1 on v0

v1 whole, which is shorter than its diff:
```python
import functools

import jax
import jax.numpy as jnp
from jax import lax
from jax.experimental import pallas as pl
from jax.experimental.pallas import tpu as pltpu
from jax.sharding import PartitionSpec as P

BLK = 32
PROMPT = 256
EPSILON = 1e-05
ROPE_BASE = 10000.0
MASK_FILL = -1e30
F32 = jnp.float32
BF16 = jnp.bfloat16
MESH = pl.DeviceIdType.MESH
ANY = pl.BlockSpec(memory_space=pl.ANY)
VMEM = pl.BlockSpec(memory_space=pltpu.VMEM)
NF = 4


def layout(member_row, block_len):
    count_blocks = member_row.shape[0]
    block_ids = jnp.arange(count_blocks, dtype=jnp.int32)
    same_run = (member_row[None, :] == member_row[:, None]) & (
        block_ids[None, :] < block_ids[:, None]
    )
    earlier = jnp.sum(same_run.astype(jnp.int32), axis=1)
    prompt_len = jnp.sum((member_row == 0).astype(jnp.int32)) * block_len
    labels = jnp.repeat(member_row, block_len)
    within = jnp.arange(count_blocks * block_len, dtype=jnp.int32) % block_len
    positions = (
        (labels > 0).astype(jnp.int32) * prompt_len
        + jnp.repeat(earlier, block_len) * block_len
        + within
    )
    return (labels, positions)


def rope_tables(positions, head_width):
    half_width = head_width // 2
    frequency = ROPE_BASE ** (-(jnp.arange(half_width, dtype=jnp.float32) * (2.0 / head_width)))
    angles = positions.astype(jnp.float32)[:, None] * frequency[None, :]
    return (jnp.cos(angles), jnp.sin(angles))


def al(x, n):
    return pl.multiple_of(x, n)


def mm(a, b):
    return lax.dot_general(a, b, (((1,), (0,)), ((), ())), preferred_element_type=F32)


def mm_nt(a, b):
    return lax.dot_general(a, b, (((1,), (1,)), ((), ())), preferred_element_type=F32)


def mm_tn(a, b):
    return lax.dot_general(a, b, (((0,), (0,)), ((), ())), preferred_element_type=F32)


class Place:
    def __init__(self, ndp):
        self.ndp = ndp
        self.nz = ndp // 2
        self.me = lax.axis_index("dp")
        self.f = lax.axis_index("fsdp")
        self.z = self.me // 2
        self.x = self.me % 2
        self.pair = self.z * 2 + 1 - self.x
        y, c = self.f // 2, self.f % 2
        self.f_core = y * 2 + 1 - c
        self.f_y = (1 - y) * 2 + c
        self.f_yc = (1 - y) * 2 + 1 - c
        self.to_pair = (self.pair, self.f)
        self.to_core = (self.me, self.f_core)
        self.to_y = (self.me, self.f_y)

    def zidx(self, k):
        return lax.rem(self.z + k + self.nz, self.nz)

    def to_z(self, k):
        return (self.zidx(k) * 2 + self.x, self.f)

    def barrier(self, fsdp=True):
        bar = pltpu.get_barrier_semaphore()
        count = self.nz
        devs = [self.to_pair] + [self.to_z(k) for k in range(1, self.nz)]
        if fsdp:
            devs += [self.to_core, self.to_y]
            count += 2
        for d in devs:
            pl.semaphore_signal(bar, inc=1, device_id=d, device_id_type=MESH)
        pl.semaphore_wait(bar, count)


def rcopy(src, dst, ss, rs, dev):
    return pltpu.make_async_remote_copy(
        src_ref=src, dst_ref=dst, send_sem=ss, recv_sem=rs, device_id=dev, device_id_type=MESH
    )


class DpGather:
    def __init__(self, pos, items, zs, zr, xs, xr):
        self.p, self.items = pos, items
        self.zs, self.zr, self.xs, self.xr = zs, zr, xs, xr

    def zcopy(self, i, k):
        src, dst = self.items[i]
        return rcopy(
            src, dst(self.p.me), self.zs.at[i, k - 1], self.zr.at[i, k - 1], self.p.to_z(k)
        )

    def zarrive(self, i, k):
        src, dst = self.items[i]
        j = self.p.zidx(-k) * 2 + self.p.x
        return rcopy(src, dst(j), self.zs.at[i, k - 1], self.zr.at[i, k - 1], self.p.to_z(-k))

    def xcopy(self, i, k):
        src, dst = self.items[i]
        j = self.p.zidx(-k) * 2 + self.p.x
        return rcopy(
            src if k == 0 else dst(j), dst(j), self.xs.at[i, k], self.xr.at[i, k], self.p.to_pair
        )

    def xarrive(self, i, k):
        src, dst = self.items[i]
        j = self.p.zidx(-k) * 2 + 1 - self.p.x
        return rcopy(src, dst(j), self.xs.at[i, k], self.xr.at[i, k], self.p.to_pair)

    def start_z(self, i):
        for k in range(1, self.p.nz):
            self.zcopy(i, k).start()

    def start_x(self, i):
        self.xcopy(i, 0).start()

    def forward(self, i, k):
        self.zarrive(i, k).wait_recv()
        self.xcopy(i, k).start()

    def wait_x(self, i):
        for k in range(self.p.nz):
            self.xarrive(i, k).wait_recv()

    def wait_sends(self, i):
        for k in range(self.p.nz):
            self.xcopy(i, k).wait_send()
        for k in range(1, self.p.nz):
            self.zcopy(i, k).wait_send()


class FsGather:
    def __init__(self, pos, blocks, ss, rs):
        self.p, self.b, self.ss, self.rs = pos, blocks, ss, rs

    def copy(self, n, fb, dev):
        return rcopy(self.b(fb), self.b(fb), self.ss.at[n], self.rs.at[n], dev)

    def start(self):
        self.copy(1, self.p.f, self.p.to_y).start()
        self.copy(0, self.p.f, self.p.to_core).start()

    def mid(self):
        self.copy(1, self.p.f_y, self.p.to_y).wait_recv()
        self.copy(2, self.p.f_y, self.p.to_core).start()

    def end(self):
        self.copy(0, self.p.f_core, self.p.to_core).wait_recv()
        self.copy(2, self.p.f_yc, self.p.to_core).wait_recv()

    def wait_sends(self):
        self.copy(1, self.p.f, self.p.to_y).wait_send()
        self.copy(0, self.p.f, self.p.to_core).wait_send()
        self.copy(2, self.p.f_y, self.p.to_core).wait_send()


class FsReduce:
    def __init__(self, pos, blocks, from_core, from_y, ss, rs):
        self.p, self.b, self.fc, self.fy, self.ss, self.rs = pos, blocks, from_core, from_y, ss, rs

    def c1(self):
        return rcopy(
            self.b(self.p.f_yc), self.fc.at[1], self.ss.at[1], self.rs.at[1], self.p.to_core
        )

    def c0(self):
        return rcopy(
            self.b(self.p.f_core), self.fc.at[0], self.ss.at[0], self.rs.at[0], self.p.to_core
        )

    def cy(self):
        return rcopy(self.fc.at[1], self.fy, self.ss.at[2], self.rs.at[2], self.p.to_y)

    def start(self):
        self.c1().start()
        self.c0().start()

    def mid(self, rows, tile=64):
        self.c1().wait_recv()
        mine = self.b(self.p.f_y)

        def add(t, _):
            r = pl.ds(al(t * tile, tile), tile)
            self.fc[1, r, :] = (self.fc[1, r, :].astype(F32) + mine[r, :].astype(F32)).astype(BF16)
            return 0

        lax.fori_loop(0, rows // tile, add, 0)
        self.cy().start()

    def end(self):
        self.c0().wait_recv()
        self.cy().wait_recv()

    def value(self, r):
        return (
            self.b(self.p.f)[r, :].astype(F32)
            + self.fc[0, r, :].astype(F32)
            + self.fy[r, :].astype(F32)
        )

    def wait_sends(self):
        self.c1().wait_send()
        self.c0().wait_send()
        self.cy().wait_send()


def softmax_parts(scores):
    top = jnp.max(scores, axis=-1, keepdims=True)
    lifted = jnp.exp(scores - top)
    return lifted / jnp.sum(lifted, axis=-1, keepdims=True)


def causal_bias(rows):
    r = lax.broadcasted_iota(jnp.int32, (rows, rows), 0)
    c = lax.broadcasted_iota(jnp.int32, (rows, rows), 1)
    return jnp.where(c <= r, 0.0, MASK_FILL).astype(F32)


def group_rows(ref, m, half, cols, own):
    t = own // 2
    first = ref[pl.ds((2 * half) * own + m * t, t), cols]
    second = ref[pl.ds((2 * half + 1) * own + m * t, t), cols]
    return jnp.concatenate([first, second], axis=0)


def put_rows(ref, m, half, cols, own, value):
    t = own // 2
    ref[pl.ds((2 * half) * own + m * t, t), cols] = value[:t]
    ref[pl.ds((2 * half + 1) * own + m * t, t), cols] = value[t:]


def forward_kernel(
    cfg,
    tok,
    dout,
    cos,
    sin,
    bias,
    seq_sh,
    gain_sh,
    qb_sh,
    out_sh,
    gate_sh,
    up_sh,
    down_sh,
    qb_all,
    out_all,
    gate_all,
    up_all,
    down_all,
    seq_all,
    gain_sum,
    lkv_o,
    q_o,
    mixed_o,
    latent_o,
    normed_o,
    middle_o,
    n2_o,
    d_o,
    seq_v,
    gain_v,
    qb_v,
    out_v,
    lkv_v,
    q_v,
    mixed_v,
    part_v,
    fcore_v,
    fy_v,
    n2_v,
    d_v,
    lat_v,
    zs,
    zr,
    xs,
    xr,
    fss,
    frs,
    sys_,
    syr,
    ls,
):
    ndp, own, dim, rank, hd, heads = cfg
    rows = NF * own
    p = Place(ndp)
    kvw = rank + 2 * hd
    sr = seq_sh.shape[0]
    items = []

    def add_item(src, dst):
        items.append((src, dst))
        return len(items) - 1

    i_seq = add_item(seq_sh, lambda j: seq_v.at[pl.ds(al((j * NF + p.f) * sr, sr), sr)])
    i_gain = add_item(gain_sh, lambda j: gain_v.at[j * NF + p.f])

    def weight_items(src, dst, pieces):
        n = src.shape[0]
        step = n // pieces
        return [
            add_item(
                src.at[pl.ds(c * step, step)],
                lambda j, c=c: dst.at[pl.ds(al(j * n + c * step, step), step)],
            )
            for c in range(pieces)
        ]

    i_qb = weight_items(qb_sh, qb_v, 1)
    i_out = weight_items(out_sh, out_v, 2)
    i_ffn = []
    for s, d in ((gate_sh, gate_all), (up_sh, up_all), (down_sh, down_all)):
        i_ffn += weight_items(s, d, 2)
    order = [i_seq, i_gain] + i_qb + i_out + i_ffn
    g = DpGather(p, items, zs, zr, xs, xr)
    fs_d = FsGather(p, lambda b: d_v.at[pl.ds(al(b * own, own), own)], fss.at[0], frs.at[0])
    fs_l = FsGather(p, lambda b: lkv_v.at[pl.ds(al(b * own, own), own)], fss.at[1], frs.at[1])
    fs_n = FsGather(p, lambda b: n2_v.at[pl.ds(al(b * own, own), own)], fss.at[2], frs.at[2])
    red = FsReduce(
        p, lambda b: part_v.at[pl.ds(al(b * own, own), own)], fcore_v, fy_v, fss.at[3], frs.at[3]
    )

    local = []

    def local_copy(src, dst):
        c = pltpu.make_async_copy(src, dst, ls.at[len(local)])
        c.start()
        local.append(c)
        return c

    own_copies = {}
    for i in order:
        src, dst = items[i]
        own_copies[i] = local_copy(src, dst(p.me))
    d_copies = [
        local_copy(dout.at[m], d_v.at[pl.ds(al(p.f * own + m * (own // 2), 128), own // 2)])
        for m in range(2)
    ]

    p.barrier()
    g.start_x(i_seq)
    g.start_x(i_gain)
    g.start_x(i_qb[0])
    for i in order:
        g.start_z(i)
    npiece = ndp

    def seq_piece(j, fb):
        return seq_v.at[pl.ds(al((j * NF + fb) * sr, sr), sr)]

    def seq_copy(t, j, fb, dev, which):
        b = seq_piece(j, fb) if which == 0 else gain_v.at[j * NF + fb]
        return rcopy(b, b, sys_.at[which, t, j], syr.at[which, t, j], dev)

    def spread(j):
        for which in (0, 1):
            seq_copy(1, j, p.f, p.to_y, which).start()
            seq_copy(0, j, p.f, p.to_core, which).start()

    for m in range(2):
        x = tok[m].astype(F32)
        inv = lax.rsqrt(jnp.mean(x * x, axis=-1, keepdims=True) + EPSILON)
        middle_o[pl.ds(m * (own // 2), own // 2), :] = x * inv
    own_copies[i_seq].wait()
    own_copies[i_gain].wait()
    spread(p.me)
    queue = order[2:]
    lead = [1]

    def more_x():
        if lead[0] < len(queue):
            g.start_x(queue[lead[0]])
            lead[0] += 1

    for k in range(1, p.nz):
        for i in (i_seq, i_gain):
            g.forward(i, k)
        spread(p.zidx(-k) * 2 + p.x)
    more_x()
    for k in range(p.nz):
        for i in (i_seq, i_gain):
            g.xarrive(i, k).wait_recv()
        spread(p.zidx(-k) * 2 + 1 - p.x)
    for c in d_copies:
        c.wait()

    def spread_forward(j, _):
        for which in (0, 1):
            seq_copy(1, j, p.f_y, p.to_y, which).wait_recv()
            seq_copy(2, j, p.f_y, p.to_core, which).start()
        return 0

    events = [(i, k) for i in queue for k in range(1, p.nz)]
    done = [0]

    def tick(n):
        for _ in range(n):
            if done[0] >= len(events):
                return
            i, k = events[done[0]]
            if k == 1:
                more_x()
            g.forward(i, k)
            done[0] += 1

    tick(p.nz - 1)
    lax.fori_loop(0, npiece, spread_forward, 0)
    fs_d.start()
    tick(p.nz - 1)

    def spread_end(j, _):
        for which in (0, 1):
            seq_copy(0, j, p.f_core, p.to_core, which).wait_recv()
            seq_copy(2, j, p.f_yc, p.to_core, which).wait_recv()
        return 0

    lax.fori_loop(0, npiece, spread_end, 0)

    def gain_add(j, acc):
        return acc + gain_v[j]

    gains = lax.fori_loop(0, ndp * NF, gain_add, jnp.zeros(gain_v.shape[1:], F32))
    gain_sum[...] = gains
    wide = dim // rank
    gain_one = jnp.concatenate([gains[r : r + 1] for r in range(wide)], axis=1)
    gain_two = jnp.concatenate([gains[wide + r : wide + r + 1] for r in range(wide)], axis=1)
    gain_lat = gains[2 * wide : 2 * wide + 1]
    normed_o[...] = (middle_o[...] * gain_one).astype(BF16)
    seq_out = local_copy(seq_v, seq_all)

    def project(j, _):
        cols = pl.ds(al(j * 256, 256), 256)
        lat_v[:, cols] = mm(normed_o[...], seq_v[:, cols])
        return 0

    lax.fori_loop(0, kvw // 256, project, 0)
    own_rows = pl.ds(al(p.f * own, own), own)
    lat = lat_v[:, :rank]
    latent_o[...] = lat
    inv_lat = lax.rsqrt(jnp.mean(lat * lat, axis=-1, keepdims=True) + EPSILON)
    lkv_v[own_rows, :rank] = (lat * inv_lat * gain_lat).astype(BF16)
    half = hd // 2
    co, si = cos[own_rows, :], sin[own_rows, :]
    ka, kb = lat_v[:, rank : rank + half], lat_v[:, rank + half : rank + hd]
    lkv_v[own_rows, rank : rank + half] = (ka * co - kb * si).astype(BF16)
    lkv_v[own_rows, rank + half : rank + hd] = (kb * co + ka * si).astype(BF16)
    lkv_v[own_rows, rank + hd :] = lat_v[:, rank + hd :].astype(BF16)
    fs_l.start()
    tick(p.nz - 1)
    fs_d.mid()
    fs_l.mid()
    tick(p.nz - 1)
    for i in i_qb:
        own_copies[i].wait()
        g.wait_x(i)
    fs_l.end()
    qb_out = local_copy(qb_v, qb_all)
    lkv_out = local_copy(lkv_v, lkv_o)

    def query(j, _):
        cols = pl.ds(al(j * hd, hd), hd)
        c0 = pl.ds(al(j * hd, half), half)
        c1 = pl.ds(al(j * hd + half, half), half)
        for r in range(rows // 512):
            rr = pl.ds(r * 512, 512)
            acc = mm(lkv_v[rr, :rank], qb_v[:, cols])
            a, b = acc[:, :half], acc[:, half:]
            c, s = cos[rr, :], sin[rr, :]
            q_v[rr, c0] = (a * c - b * s).astype(BF16)
            q_v[rr, c1] = (b * c + a * s).astype(BF16)
        return 0

    lax.fori_loop(0, heads, query, 0)
    q_out = local_copy(q_v, q_o)
    tick(1)
    scale = hd ** (-0.5)
    kcols, vcols = slice(rank, rank + hd), slice(rank + hd, rank + 2 * hd)
    causal = causal_bias(PROMPT)
    for m in range(2):
        k0, k1 = (group_rows(lkv_v, m, h2, kcols, own) for h2 in (0, 1))
        v0, v1 = (group_rows(lkv_v, m, h2, vcols, own) for h2 in (0, 1))
        low = bias[m]

        def attend(h, _):
            cols = pl.ds(al(h * hd, hd), hd)
            q0 = group_rows(q_v, m, 0, cols, own)
            pr = softmax_parts(mm_nt(q0, k0) * scale + causal).astype(BF16)
            put_rows(mixed_v, m, 0, cols, own, mm(pr, v0).astype(BF16))
            q1 = group_rows(q_v, m, 1, cols, own)
            s0 = mm_nt(q1, k0) * scale
            s1 = mm_nt(q1, k1) * scale + low
            top = jnp.maximum(
                jnp.max(s0, axis=-1, keepdims=True), jnp.max(s1, axis=-1, keepdims=True)
            )
            e0, e1 = jnp.exp(s0 - top), jnp.exp(s1 - top)
            total = jnp.sum(e0, axis=-1, keepdims=True) + jnp.sum(e1, axis=-1, keepdims=True)
            mix = mm((e0 / total).astype(BF16), v0) + mm((e1 / total).astype(BF16), v1)
            put_rows(mixed_v, m, 1, cols, own, mix.astype(BF16))
            return 0

        lax.fori_loop(0, heads, attend, 0)
        tick(2)
    fs_d.end()
    d_out = local_copy(d_v, d_o)
    mixed_out = local_copy(mixed_v, mixed_o)
    tick(1)
    for i in i_out:
        own_copies[i].wait()
        g.wait_x(i)
    out_out = local_copy(out_v, out_all)

    def project_out(fb):
        rr = pl.ds(al(fb * own, own), own)

        def one(j, _):
            wr = pl.ds(al(j * 256, 256), 256)
            part_v[rr, wr] = mm_nt(mixed_v[rr, :], out_v[wr, :]).astype(BF16)
            return 0

        lax.fori_loop(0, dim // 256, one, 0)

    project_out(p.f_yc)
    project_out(p.f_core)
    red.start()
    tick(1)
    project_out(p.f_y)
    red.mid(own)
    project_out(p.f)
    tick(2)
    red.end()
    for m in range(2):
        rr = pl.ds(m * (own // 2), own // 2)
        mid = tok[m].astype(F32) + red.value(rr)
        middle_o[rr, :] = mid
        inv = lax.rsqrt(jnp.mean(mid * mid, axis=-1, keepdims=True) + EPSILON)
        n2_v[pl.ds(al(p.f * own + m * (own // 2), 128), own // 2), :] = (
            mid * inv * gain_two
        ).astype(BF16)
    fs_n.start()
    tick(4)
    fs_n.mid()
    tick(1)
    fs_n.end()
    n2_out = local_copy(n2_v, n2_o)
    tick(len(events))
    for i in i_ffn:
        own_copies[i].wait()
        g.wait_x(i)
    for i in order:
        g.wait_sends(i)

    def spread_sends(j, _):
        for which in (0, 1):
            seq_copy(0, j, p.f, p.to_core, which).wait_send()
            seq_copy(1, j, p.f, p.to_y, which).wait_send()
            seq_copy(2, j, p.f_y, p.to_core, which).wait_send()
        return 0

    lax.fori_loop(0, npiece, spread_sends, 0)
    for t in (fs_d, fs_l, fs_n, red):
        t.wait_sends()
    for c in (seq_out, qb_out, lkv_out, q_out, d_out, mixed_out, out_out, n2_out):
        c.wait()


def forward_call(ndp, tok, dout, cos, sin, bias, seq_sh, gain_sh, qb, out, gate, up, down):
    own = tok.shape[0] * tok.shape[1]
    dim = tok.shape[2]
    rank = qb.shape[0] * ndp
    hd = (seq_sh.shape[1] - rank) // 2
    heads = qb.shape[1] // hd
    rows = NF * own
    kvw = seq_sh.shape[1]
    nz = ndp // 2
    n_items = 2 + 1 + 2 + 6

    def sds(shape, dtype=BF16):
        return jax.ShapeDtypeStruct(shape, dtype)

    full = lambda w: sds((w.shape[0] * ndp, w.shape[1]))
    out_shape = (
        full(qb),
        full(out),
        full(gate),
        full(up),
        full(down),
        sds((seq_sh.shape[0] * ndp * NF, kvw)),
        sds(gain_sh.shape, F32),
        sds((rows, kvw)),
        sds((rows, heads * hd)),
        sds((rows, heads * hd)),
        sds((own, rank), F32),
        sds((own, dim)),
        sds((own, dim), F32),
        sds((rows, dim)),
        sds((rows, dim)),
    )
    out_specs = (ANY,) * 6 + (VMEM,) + (ANY,) * 3 + (VMEM,) * 3 + (ANY,) * 2
    dma = pltpu.SemaphoreType.DMA
    scratch = [
        pltpu.VMEM((seq_sh.shape[0] * ndp * NF, kvw), BF16),
        pltpu.VMEM((ndp * NF,) + gain_sh.shape, F32),
        pltpu.VMEM((qb.shape[0] * ndp, qb.shape[1]), BF16),
        pltpu.VMEM((out.shape[0] * ndp, out.shape[1]), BF16),
        pltpu.VMEM((rows, kvw), BF16),
        pltpu.VMEM((rows, heads * hd), BF16),
        pltpu.VMEM((rows, heads * hd), BF16),
        pltpu.VMEM((rows, dim), BF16),
        pltpu.VMEM((2, own, dim), BF16),
        pltpu.VMEM((own, dim), BF16),
        pltpu.VMEM((rows, dim), BF16),
        pltpu.VMEM((rows, dim), BF16),
        pltpu.VMEM((own, kvw), F32),
        dma((n_items, nz - 1)),
        dma((n_items, nz - 1)),
        dma((n_items, nz)),
        dma((n_items, nz)),
        dma((4, 3)),
        dma((4, 3)),
        dma((2, 3, ndp)),
        dma((2, 3, ndp)),
        dma((n_items + 10,)),
    ]
    return pl.pallas_call(
        functools.partial(forward_kernel, (ndp, own, dim, rank, hd, heads)),
        out_shape=out_shape,
        in_specs=(VMEM,) * 5 + (ANY,) * 7,
        out_specs=out_specs,
        scratch_shapes=scratch,
        compiler_params=pltpu.CompilerParams(
            collective_id=0, has_side_effects=True, vmem_limit_bytes=60 * 2**20
        ),
        name="gather_forward",
    )(tok, dout, cos, sin, bias, seq_sh, gain_sh, qb, out, gate, up, down)


class DpScatter:
    def __init__(self, pos, xs, xr, zs, zr, ls):
        self.p = pos
        self.xs, self.xr, self.zs, self.zr, self.ls = xs, xr, zs, zr, ls
        self.items = []

    def add(self, src, own, xbuf, zbuf, out, r0, r):
        self.items.append((src, own, xbuf, zbuf, out, pl.ds(r0, r), r0, r))
        return len(self.items) - 1

    def xcopy(self, i):
        src, own, xbuf, zbuf, out, rr, r0, r = self.items[i]
        return rcopy(
            src.at[:, 1 - self.p.x, rr], xbuf.at[:, rr], self.xs.at[i], self.xr.at[i], self.p.to_pair
        )

    def owncopy(self, i):
        src, own, xbuf, zbuf, out, rr, r0, r = self.items[i]
        return pltpu.make_async_copy(src.at[:, self.p.x, rr], own.at[:, rr], self.ls.at[i])

    def start(self, i):
        self.xcopy(i).start()
        if self.items[i][1] is not None:
            self.owncopy(i).start()

    def zcopy(self, i, k):
        src, own, xbuf, zbuf, out, rr, r0, r = self.items[i]
        return rcopy(
            xbuf.at[self.p.zidx(k), rr],
            zbuf.at[k - 1, rr],
            self.zs.at[i, k - 1],
            self.zr.at[i, k - 1],
            self.p.to_z(k),
        )

    def combine(self, i):
        src, own, xbuf, zbuf, out, rr, r0, r = self.items[i]
        p = self.p
        self.xcopy(i).wait_recv()
        if own is not None:
            self.owncopy(i).wait()
        tile = 16

        def mine(j, t):
            if own is None:
                return src[j, p.x, t, :].astype(F32)
            return own[j, t, :].astype(F32)

        for k in range(1, p.nz):
            j = p.zidx(k)

            def add(t, _):
                t = pl.ds(al(r0 + t * tile, tile), tile)
                xbuf[j, t, :] = (xbuf[j, t, :].astype(F32) + mine(j, t)).astype(BF16)
                return 0

            lax.fori_loop(0, r // tile, add, 0)
            self.zcopy(i, k).start()

        def keep(t, _):
            t = pl.ds(al(r0 + t * tile, tile), tile)
            out[t, :] = xbuf[p.z, t, :].astype(F32) + mine(p.z, t)
            return 0

        lax.fori_loop(0, r // tile, keep, 0)

    def finish(self, i):
        src, own, xbuf, zbuf, out, rr, r0, r = self.items[i]
        for k in range(1, self.p.nz):
            self.zcopy(i, k).wait_recv()
        tile = 16

        def add(t, _):
            t = pl.ds(al(r0 + t * tile, tile), tile)
            total = out[t, :]
            for k in range(self.p.nz - 1):
                total = total + zbuf[k, t, :].astype(F32)
            out[t, :] = total
            return 0

        lax.fori_loop(0, r // tile, add, 0)

    def wait_sends(self, i):
        self.xcopy(i).wait_send()
        for k in range(1, self.p.nz):
            self.zcopy(i, k).wait_send()


def scatter_kernel(ndp, pieces, n, *refs):
    refs = list(refs)

    def take(c):
        out = refs[:c]
        del refs[:c]
        return out

    heads = take(n)
    seq, gain = take(2)
    outs = take(n)
    seq_o, gain_o = take(2)
    owns, xbufs, zbufs = take(n), take(n), take(n)
    seq_own, seq_core, seq_y, seq_x, seq_z, gain_rx, gain_acc = take(7)
    xs, xr, zs, zr, ls, gs, gr, qs, qr, qls = take(10)
    p = Place(ndp)
    sc = DpScatter(p, xs, xr, zs, zr, ls)
    head_items = []
    for w in range(n):
        rows = outs[w].shape[0]
        step = rows // pieces[w]
        for c in range(pieces[w]):
            head_items.append(
                sc.add(heads[w], owns[w], xbufs[w], zbufs[w], outs[w], c * step, step)
            )
    sr = seq_o.shape[0]
    seq_item = sc.add(seq_core.at[0], None, seq_x, seq_z, seq_o, 0, sr)
    own_f = pltpu.make_async_copy(seq.at[:, :, p.f], seq_own.at[0], qls.at[0])
    own_y = pltpu.make_async_copy(seq.at[:, :, p.f_y], seq_own.at[1], qls.at[1])
    own_y.start()
    own_f.start()
    p.barrier()
    c1 = rcopy(seq.at[:, :, p.f_yc], seq_core.at[1], qs.at[1], qr.at[1], p.to_core)
    c0 = rcopy(seq.at[:, :, p.f_core], seq_core.at[0], qs.at[0], qr.at[0], p.to_core)
    cy = rcopy(seq_core.at[1], seq_y, qs.at[2], qr.at[2], p.to_y)
    c1.start()
    c0.start()
    gains = [
        rcopy(gain, gain_rx.at[0], gs.at[0], gr.at[0], p.to_core),
        rcopy(gain_acc.at[0], gain_rx.at[1], gs.at[1], gr.at[1], p.to_y),
        rcopy(gain_acc.at[1], gain_rx.at[2], gs.at[2], gr.at[2], p.to_pair),
    ] + [
        rcopy(gain_acc.at[2], gain_rx.at[2 + k], gs.at[2 + k], gr.at[2 + k], p.to_z(k))
        for k in range(1, p.nz)
    ]
    gains[0].start()
    for i in head_items:
        sc.start(i)
    gains[0].wait_recv()
    gain_acc[0] = gain[...] + gain_rx[0]
    gains[1].start()
    gains[1].wait_recv()
    gain_acc[1] = gain_acc[0] + gain_rx[1]
    gains[2].start()
    own_y.wait()
    own_f.wait()
    c1.wait_recv()
    nz = p.nz

    def add_y(j, _):
        for x in range(2):
            seq_core[1, j, x] = (
                seq_core[1, j, x].astype(F32) + seq_own[1, j, x].astype(F32)
            ).astype(BF16)
        return 0

    lax.fori_loop(0, nz, add_y, 0)
    cy.start()
    gains[2].wait_recv()
    gain_acc[2] = gain_acc[1] + gain_rx[2]
    for k in range(1, nz):
        gains[2 + k].start()
    sc.combine(head_items[0])
    c0.wait_recv()
    cy.wait_recv()

    def add_f(j, _):
        for x in range(2):
            seq_core[0, j, x] = (
                seq_core[0, j, x].astype(F32)
                + seq_own[0, j, x].astype(F32)
                + seq_y[j, x].astype(F32)
            ).astype(BF16)
        return 0

    lax.fori_loop(0, nz, add_f, 0)
    sc.start(seq_item)
    todo = head_items[1:] + [seq_item]
    for i in todo:
        sc.combine(i)
    total = gain_acc[2]
    for k in range(1, nz):
        gains[2 + k].wait_recv()
        total = total + gain_rx[2 + k]
    gain_o[...] = total
    for i in head_items + [seq_item]:
        sc.finish(i)
    for i in head_items + [seq_item]:
        sc.wait_sends(i)
    for t in [c1, c0, cy] + gains:
        t.wait_send()


def scatter_call(ndp, heads, seq, gain):
    nz = ndp // 2
    n = len(heads)
    shards = [(w.shape[0] // ndp, w.shape[1]) for w in heads]
    pieces = [2 if s[0] % 32 == 0 else 1 for s in shards]
    n_items = sum(pieces) + 1
    sr, kvw = seq.shape[0] // (ndp * NF), seq.shape[1]
    dma = pltpu.SemaphoreType.DMA
    scratch = (
        [pltpu.VMEM((nz,) + s, BF16) for s in shards]
        + [pltpu.VMEM((nz,) + s, BF16) for s in shards]
        + [pltpu.VMEM((nz - 1,) + s, BF16) for s in shards]
        + [
            pltpu.VMEM((2, nz, 2, sr, kvw), BF16),
            pltpu.VMEM((2, nz, 2, sr, kvw), BF16),
            pltpu.VMEM((nz, 2, sr, kvw), BF16),
            pltpu.VMEM((nz, sr, kvw), BF16),
            pltpu.VMEM((nz - 1, sr, kvw), BF16),
            pltpu.VMEM((2 + nz,) + gain.shape, F32),
            pltpu.VMEM((3,) + gain.shape, F32),
            dma((n_items,)),
            dma((n_items,)),
            dma((n_items, nz - 1)),
            dma((n_items, nz - 1)),
            dma((n_items,)),
            dma((2 + nz,)),
            dma((2 + nz,)),
            dma((3,)),
            dma((3,)),
            dma((2,)),
        ]
    )
    return pl.pallas_call(
        functools.partial(scatter_kernel, ndp, pieces, n),
        out_shape=tuple(jax.ShapeDtypeStruct(s, F32) for s in shards)
        + (jax.ShapeDtypeStruct((sr, kvw), F32), jax.ShapeDtypeStruct(gain.shape, F32)),
        in_specs=(ANY,) * (n + 1) + (VMEM,),
        out_specs=(VMEM,) * (n + 2),
        scratch_shapes=scratch,
        compiler_params=pltpu.CompilerParams(
            collective_id=1, has_side_effects=True, vmem_limit_bytes=60 * 2**20
        ),
        name="scatter_grads",
    )(*[w.reshape((nz, 2) + s) for w, s in zip(heads, shards)], seq.reshape(nz, 2, NF, sr, kvw), gain)


def unrotate(vector, cos_tab, sin_tab):
    half_width = vector.shape[-1] // 2
    lower_half = vector[..., :half_width]
    upper_half = vector[..., half_width:]
    return jnp.concatenate(
        [lower_half * cos_tab + upper_half * sin_tab, upper_half * cos_tab - lower_half * sin_tab],
        axis=-1,
    )


def norm_back(grad_in, values, inverse, gain):
    scaled = grad_in * gain
    gain_term = jnp.sum(grad_in * values * inverse, axis=0)
    inner_sum = jnp.mean(scaled * values, axis=-1, keepdims=True)
    return (inverse * scaled - values * inverse * inverse * inverse * inner_sum, gain_term)


def inverse_rms(v):
    return lax.rsqrt(jnp.mean(v * v, axis=-1, keepdims=True) + EPSILON)


def per_device(
    ndp,
    tokens,
    membership,
    d_output,
    gain_attn,
    w_qa,
    gain_latent,
    w_qb,
    w_key,
    w_value,
    w_out,
    gain_ffn,
    w_gate,
    w_up,
    w_down,
):
    micro, tlen, dim = tokens.shape
    own = micro * tlen
    rank = w_qa.shape[1]
    hd = w_key.shape[1]
    heads = w_qb.shape[1] // hd
    rows = NF * own
    wide = dim // rank
    labels, positions = jax.vmap(lambda r: layout(r, BLK))(membership[0])
    pos_rows = positions.reshape(micro, NF, tlen).transpose(1, 0, 2).reshape(rows)
    cos, sin = rope_tables(pos_rows, hd)
    tail = labels[:, PROMPT:]
    idx = jnp.arange(tail.shape[1], dtype=jnp.int32)
    seen = (idx[None, None, :] <= idx[None, :, None]) & (tail[:, None, :] == tail[:, :, None])
    bias = jnp.where(seen, 0.0, MASK_FILL).astype(F32)
    block = lax.axis_index("dp") * NF + lax.axis_index("fsdp")

    def spot(gain):
        width = gain.shape[0]
        count = ndp * NF
        at = lax.broadcasted_iota(jnp.int32, (count, width), 0) == block
        placed = jnp.where(at, gain.astype(F32)[None, :], 0.0)
        return placed.reshape(count * width // rank, rank)

    gain_sh = jnp.concatenate([spot(gain_attn), spot(gain_ffn), spot(gain_latent)], axis=0)
    gain_sh = jnp.pad(gain_sh, ((0, 8 - gain_sh.shape[0]), (0, 0)))
    seq_sh = jnp.concatenate([w_qa, w_key, w_value], axis=1)
    (
        qb_all,
        out_all,
        gate_all,
        up_all,
        down_all,
        seq_all,
        gains,
        lkv,
        q_all,
        mixed,
        latent,
        normed,
        middle,
        n2,
        d_all,
    ) = forward_call(
        ndp, tokens, d_output, cos, sin, bias, seq_sh, gain_sh, w_qb, w_out, w_gate, w_up, w_down
    )
    gain_one = gains[:wide].reshape(1, dim)
    gain_two = gains[wide : 2 * wide].reshape(1, dim)
    gain_lat = gains[2 * wide].reshape(1, rank)

    gate = jnp.dot(n2, gate_all, preferred_element_type=F32)
    up = jnp.dot(n2, up_all, preferred_element_type=F32)
    sig = jax.nn.sigmoid(gate)
    hidden = (gate * sig * up).astype(BF16)
    grad_hidden = jnp.dot(d_all, down_all, preferred_element_type=F32)
    grad_gate = (grad_hidden * up * sig * (1.0 + gate * (1.0 - sig))).astype(BF16)
    grad_up = (grad_hidden * gate * sig).astype(BF16)
    ffn_part = mm_nt(hidden, down_all).astype(BF16)
    gnt_part = (mm_nt(grad_gate, gate_all) + mm_nt(grad_up, up_all)).astype(BF16)
    gw_down = mm_tn(d_all, hidden).astype(BF16)
    gw_gate = mm_tn(n2, grad_gate).astype(BF16)
    gw_up = mm_tn(n2, grad_up).astype(BF16)

    ffn_own = lax.psum_scatter(ffn_part, "fsdp", scatter_dimension=0, tiled=True).astype(F32)
    output = (middle + ffn_own).astype(BF16).reshape(tokens.shape)
    grad_n2 = lax.psum_scatter(gnt_part, "fsdp", scatter_dimension=0, tiled=True).astype(F32)
    grad_mid_norm, g_gain_two = norm_back(grad_n2, middle, inverse_rms(middle), gain_two)
    grad_middle = d_output.reshape(own, dim).astype(F32) + grad_mid_norm
    proj_all = lax.all_gather(grad_middle.astype(BF16), "fsdp", axis=0, tiled=True)
    gw_out = mm_tn(proj_all, mixed).astype(BF16)
    grad_mixed = mm(proj_all, out_all).astype(BF16)

    def by_group(v, *tail_shape):
        return (
            v.reshape((NF, micro, tlen) + tail_shape)
            .swapaxes(0, 1)
            .reshape((micro, NF * tlen) + tail_shape)
        )

    def by_block(v):
        tail_shape = v.shape[2:]
        return (
            v.reshape((micro, NF, tlen) + tail_shape)
            .swapaxes(0, 1)
            .reshape((rows,) + tail_shape)
        )

    scale = hd ** (-0.5)
    ki = jnp.arange(NF * tlen, dtype=jnp.int32)
    allowed = (ki[None, None, :] <= ki[None, :, None]) & (
        (labels[:, None, :] == 0) | (labels[:, None, :] == labels[:, :, None])
    )
    qg = by_group(q_all, heads, hd) if False else by_group(q_all.reshape(rows, heads, hd), heads, hd)
    gm = by_group(grad_mixed.reshape(rows, heads, hd), heads, hd)
    keys = by_group(lkv[:, rank : rank + hd], hd)
    values = by_group(lkv[:, rank + hd :], hd)
    scores = jnp.einsum("mqhd,mkd->mhqk", qg, keys, preferred_element_type=F32) * scale
    scores = jnp.where(allowed[:, None], scores, MASK_FILL)
    probs = jax.nn.softmax(scores, axis=-1)
    gp = jnp.einsum("mqhd,mkd->mhqk", gm, values, preferred_element_type=F32)
    gv = jnp.einsum("mhqk,mqhd->mkd", probs.astype(BF16), gm, preferred_element_type=F32)
    gs = (probs * (gp - jnp.sum(probs * gp, axis=-1, keepdims=True))).astype(BF16)
    gq = jnp.einsum("mhqk,mkd->mqhd", gs, keys, preferred_element_type=F32) * scale
    gk = jnp.einsum("mhqk,mqhd->mkd", gs, qg, preferred_element_type=F32) * scale
    gq = unrotate(by_block(gq), cos[:, None, :], sin[:, None, :]).astype(BF16)
    gq = gq.reshape(rows, heads * hd)
    gw_qb = mm_tn(lkv[:, :rank], gq).astype(BF16)
    glat_part = mm_nt(gq, qb_all).astype(BF16)
    packed = jnp.concatenate(
        [glat_part, by_block(gk).astype(BF16), by_block(gv).astype(BF16)], axis=1
    )
    back_own = lax.psum_scatter(packed, "fsdp", scatter_dimension=0, tiled=True).astype(F32)
    cos_own = lax.dynamic_slice_in_dim(cos, lax.axis_index("fsdp") * own, own, 0)
    sin_own = lax.dynamic_slice_in_dim(sin, lax.axis_index("fsdp") * own, own, 0)
    g_lat, g_gain_lat = norm_back(back_own[:, :rank], latent, inverse_rms(latent), gain_lat)
    g_key = unrotate(back_own[:, rank : rank + hd], cos_own, sin_own)
    g_all = jnp.concatenate([g_lat, g_key, back_own[:, rank + hd :]], axis=1).astype(BF16)
    gw_seq = mm_tn(normed, g_all).astype(BF16)
    grad_normed = mm_nt(g_all, seq_all)
    inputs = tokens.reshape(own, dim).astype(F32)
    grad_in, g_gain_one = norm_back(grad_normed, inputs, inverse_rms(inputs), gain_one)
    input_grad = (grad_middle + grad_in).astype(BF16).reshape(tokens.shape)
    gain_part = jnp.concatenate(
        [
            g_gain_one.reshape(wide, rank),
            g_gain_two.reshape(wide, rank),
            g_gain_lat.reshape(1, rank),
        ],
        axis=0,
    )
    gain_part = jnp.pad(gain_part, ((0, 8 - gain_part.shape[0]), (0, 0)))
    o_gate, o_up, o_down, o_out, o_qb, o_seq, o_gain = scatter_call(
        ndp, (gw_gate, gw_up, gw_down, gw_out, gw_qb), gw_seq, gain_part
    )

    def own_gain(flat, width):
        return lax.dynamic_slice_in_dim(flat.reshape(-1), block * width, width, 0)

    return (
        output,
        input_grad,
        own_gain(o_gain[:wide], gain_attn.shape[0]),
        o_seq[:, :rank],
        own_gain(o_gain[2 * wide], gain_latent.shape[0]),
        o_qb,
        o_seq[:, rank : rank + hd],
        o_seq[:, rank + hd :],
        o_out,
        own_gain(o_gain[wide : 2 * wide], gain_ffn.shape[0]),
        o_gate,
        o_up,
        o_down,
    )


def solution(mesh):
    both = ("dp", "fsdp")
    rowwise, vector = P(both, None), P(both)
    tok = P(None, both, None)
    head = P("dp", "fsdp")
    return jax.shard_map(
        functools.partial(per_device, mesh.shape["dp"]),
        mesh=mesh,
        in_specs=(
            tok,
            P("dp", None, None),
            tok,
            vector,
            rowwise,
            vector,
            head,
            rowwise,
            rowwise,
            head,
            vector,
            head,
            head,
            head,
        ),
        out_specs=(
            tok,
            tok,
            vector,
            rowwise,
            vector,
            head,
            rowwise,
            rowwise,
            head,
            vector,
            head,
            head,
            head,
        ),
        check_vma=False,
    )
```

time: 2190 us -> 1200 us (0.55)
  waiting for transfers between devices: 1690 us -> 62.2 us
  Pallas kernels: 0 us -> 876 us
  blocking collectives: 108 us -> 0 us
  matrix products: 244 us -> 152 us
  other arithmetic: 57.1 us -> 34.9 us
    reduce_scatter x20 -> x3, waiting for transfers between devices: 1100 us -> 49.5 us  [the longest x1 49.5 us: per_device(): lax.psum_scatter(gnt_part, 'fsdp', scatter_dimension=0, tiled=True)]
    pallas_call x0 -> x2, Pallas kernels: none -> 876 us  [the longest x1 534 us: scatter_call(): pl.pallas_call(functools.partial(scatter_kernel, ndp, pieces, n), out_sha...]
    all_gather x16 -> x1, waiting for transfers between devices: 584 us -> 12.7 us  [per_device(): lax.all_gather(grad_middle.astype(BF16), 'fsdp', axis=0, tiled=True)]
    dot_general x76 -> x19, matrix products: 244 us -> 144 us  [the longest x6 49.3 us: mm_tn(): lax.dot_general(a, b, (((0,), (0,)), ((), ())), preferred_element_type=F32)]
    unnamed x2 -> x0, blocking collectives: 83.1 us -> none
    all_gather x4 -> x0, blocking collectives: 25.3 us -> none  [the longest x2 13.4 us: micro_forward(): lax.all_gather(key_own, 'fsdp', axis=0, tiled=True)]
  transfers between devices with their start and end apart: 36 -> 4, of which waited for: 30 -> 2; matrix products, arithmetic and copies ran while one was open for 13% -> 9% of each run, Pallas kernels for 0% -> 45%
where the time goes in v1:
time: 1200 us; the launch traced here: 1190 us
  Pallas kernels  876 us (73%)
  matrix products  152 us (13%)
  waiting for transfers between devices  62.2 us (5%)
  local copies, waits for them, and re-layouts  52.2 us (4%)
  other arithmetic  34.9 us (3%)
  between operations  14.5 us (1%)
    pallas_call x1, Pallas kernels, scatter_call(): pl.pallas_call(functools.partial(scatter_kernel, ndp, pieces, n), out_sha...  534 us
    pallas_call x1, Pallas kernels, forward_call(): pl.pallas_call(functools.partial(forward_kernel, (ndp, own, dim, rank, hd...  342 us
    reduce_scatter x1, waiting for transfers between devices, per_device(): lax.psum_scatter(gnt_part, 'fsdp', scatter_dimension=0, tiled=True)  49.5 us
    dot_general x6, matrix products, mm_tn(): lax.dot_general(a, b, (((0,), (0,)), ((), ())), preferred_element_type=F32)  49.3 us
    dot_general x5, matrix products, mm_nt(): lax.dot_general(a, b, (((1,), (1,)), ((), ())), preferred_element_type=F32)  39.2 us
  transfers between devices with their start and end apart: 4, of which 2 were waited for; matrix products, arithmetic and copies ran while one was open for 9% of the time, Pallas kernels for 45%

profile of v1, /device:TPU:0, one launch (start us, length us, event | category | flops | bytes accessed | tf_op | source)
XLA Modules:
  0.0 1192.3 jit_solution(9706690320127863703)
XLA Ops:
  8.0 0.8 fusion.46
  8.8 0.9 convert_reduce_fusion
  13.5 3.0 multiply_sine_fusion
  16.5 1.0 and_select_fusion.bias
  17.4 1.6 pad_maximum_fusion.3.seq_sh
  19.7 341.9 %gather_forward.1 = (bf16[1024,1024]{1,0:T(8,128)(2,1)}, bf16[2048,1024]{1,0:T(8,128)(2,1)}, bf16[2048,1408]{1,0:T(8,128)(2,1)}, bf16[2048,1408]{1,0:T(8,128)(2,...) custom-call(bf16[2,128,2048]{2,1,0:T(8,128)(2,1)} %tok.1, ...), custom_call_target="tpu_custom_call" | custom-call | tf_op jit(solution)/shard_map/gather_forward/pallas_call | solution.py:647
  361.7 11.8 fusion.56
  373.5 8.5 fusion.57
  382.0 14.9 %multiply_convert_fusion = (bf16[1024,1408]{1,0:T(8,128)(2,1)}, bf16[1024,1408]{1,0:T(8,128)(2,1)S(1)}, bf16[1024,1408]{1,0:T(8,128)(2,1)}) fusion(f32[1024,1408]{1,0:T(8,128)} %fusion.56, f32[1024,1408]{1,0:T(8,128)} %fusion.57, bf16[1024,2048]{1,0:T(8,128)(2,1)} %get-tuple-element.40, bf16[2048,1408]{1,0:T(8,128)(2,1)S(1)} %bitcast.218), kind=kOutput, calls=%fused_computation.14 | convolution fusion | flops 5928648704 | bytes 30146560 | tf_op jit(solution)/shard_map/dot_general | solution.py:988
  397.0 6.7 fusion.58
  403.7 10.1 add_convert_fusion
  414.6 0.8 copy-done
  415.6 49.5 %reduce-scatter.6.cloned.1.call-done = bf16[256,2048]{1,0:T(8,128)(2,1)} async-done(((bf16[1024,2048]{1,0:T(8,128)(2,1)}), bf16[256,2048]{1,0:T(8,128)(2,1)}) %reduce-scatter.6.cloned.1.call-update) | async-done | bytes 1048592 | tf_op jit(solution)/shard_map/reduce_scatter | solution.py:999
  465.1 1.9 fusion.16
  467.1 1.8 fusion.52
  469.0 2.1 fusion.53
  471.0 0.8 copy.59
  471.9 4.7 reshape_reshape.6
  476.6 3.7 copy.60
  480.3 0.8 copy.61
  481.2 1.3 or_and_fusion
  482.6 8.3 fusion.55
  490.9 12.7 %all-gather.2.cloned.1.call-done = bf16[1024,2048]{1,0:T(8,128)(2,1)} async-done(((bf16[256,2048]{1,0:T(8,128)(2,1)}), bf16[1024,2048]{1,0:T(8,128)(2,1)}) %all-gather.2.cloned.1.call-update) | async-done | bytes 4194320 | tf_op jit(solution)/shard_map/all_gather | solution.py:1002
  503.6 9.3 convolution_convert_fusion.7
  512.9 4.5 reshape_reshape.7
  517.4 2.1 copy.62
  519.5 4.8 fusion.37
  524.4 1.6 fusion.1
  526.0 2.4 fusion.3
  528.4 1.2 fusion.36
  529.7 3.3 multiply_bitcast_fusion
  533.0 0.8 copy.69
  533.8 0.8 copy.68
  534.6 5.3 reshape.357
  539.9 5.3 copy.65
  545.2 3.0 add_convert_fusion.1
  548.2 1.6 pad_maximum_fusion.1
  549.8 4.0 copy.66
  553.8 4.7 convolution_convert_fusion.6
  558.5 1.8 pad_maximum_fusion
  560.3 11.4 convolution_convert_fusion.4
  571.8 1.5 fusion.17
  573.3 11.0 convolution_convert_fusion.3
  584.3 1.4 multiply_reduce_fusion.3
  585.7 11.2 convolution_convert_fusion.2
  596.9 8.8 convolution_convert_fusion.1
  605.8 6.3 fusion.29
  612.0 6.2 convolution_convert_fusion.5
  618.3 1.0 slice.86
  619.3 1.5 convert_element_type.173
  621.2 1.0 add_convert_fusion.3
  622.6 6.3 fusion.26
  629.5 5.9 convolution_convert_fusion
  635.3 534.1 %scatter_grads.1 = (f32[256,1408]{1,0:T(8,128)}, f32[256,1408]{1,0:T(8,128)}, f32[256,1408]{1,0:T(8,128)}, f32[256,1024]{1,0:T(8,128)}, f32[128,1024]{1,0:T(8,12...) custom-call(bf16[4,2,256,1408]{3,2,1,0:T(8,128)(2,1)} %bitcast.184, bf16[4,2,256,1408]{3,2,1,0:T(8,128)(2,1)} %bitcast.185, ...), custom_call_target="tpu_custom_call" | custom-call | tf_op jit(solution)/shard_map/scatter_grads/pallas_call | solution.py:883
  1169.5 1.7 slice.75
  1171.1 0.8 slice.76
  1171.9 0.8 slice_bitcast_fusion
  1174.5 1.5 fusion.54
  1176.0 4.4 fusion.23
  1180.5 0.8 copy.94
  1181.3 1.0 copy.95
  1182.2 1.1 copy.96
  1183.3 1.1 copy.97
  1184.4 1.1 copy.98
  (125 shorter events, 9.6 us)
Async XLA Ops:
  7.2 457.9 %reduce-scatter.6.cloned.1.call-start = ((), (), s32[]{:S(2)}) async-start(), calls=%async_computation.4 | async-start | bytes 5242880 | tf_op jit(solution)/shard_map/reduce_scatter | solution.py:999
  361.6 11.9 copy-start.18
  361.6 11.9 copy-start.20
  361.7 20.4 %slice-start.2 = ((s8[5767168]{0:T(1024)(128)(4,1)}), s8[4194304]{0:T(1024)(128)(4,1)S(1)}, s32[]{:S(2)}) async-start(s8[5767168]{0:T(1024)(128)(4,1)} %bitcast.217), calls=%async_computation.9 | async-start | bytes 8388608
  373.5 8.5 slice-start.3
  373.5 23.4 %slice-start.4 = ((s8[5767168]{0:T(1024)(128)(4,1)}), s8[4194304]{0:T(1024)(128)(4,1)S(1)}, s32[]{:S(2)}) async-start(s8[5767168]{0:T(1024)(128)(4,1)} %bitcast.219), calls=%async_computation.11 | async-start | bytes 8388608
  382.0 14.9 %slice-start.5 = ((s8[5767168]{0:T(1024)(128)(4,1)}), s8[1572864]{0:T(1024)(128)(4,1)S(1)}, s32[]{:S(2)}) async-start(s8[5767168]{0:T(1024)(128)(4,1)} %bitcast.219), calls=%async_computation.12 | async-start | bytes 3145728
  396.9 6.7 copy-start.23
  413.8 0.8 copy-start.17
  413.8 1.6 copy-start
  413.8 53.3 %copy-start.1 = (bf16[2,128,2048]{2,1,0:T(8,128)(2,1)S(1)}, bf16[2,128,2048]{2,1,0:T(8,128)(2,1)}, u32[]{:S(2)}) copy-start(bf16[2,128,2048]{2,1,0:T(8,128)(2,1)} %dout.1) | copy-start | bytes 3145732
  413.8 89.7 %all-gather.2.cloned.1.call-start = ((), (), s32[]{:S(2)}) async-start(), calls=%async_computation.5 | async-start | bytes 5242880 | tf_op jit(solution)/shard_map/all_gather | solution.py:1002
  465.1 2.0 copy-start.2
  468.9 149.3 %reduce-scatter.8.cloned.1.call-start = ((), (), s32[]{:S(2)}) async-start(), calls=%async_computation.6 | async-start | bytes 3932160 | tf_op jit(solution)/shard_map/reduce_scatter | solution.py:1045
  476.6 3.7 copy-start.10
  517.4 7.0 slice-start
  519.5 4.9 slice-start.1
  519.5 4.9 copy-start.16
  526.0 2.4 copy-start.8
  528.4 1.3 copy-start.5
  553.8 4.7 copy-start.6
  553.8 4.7 copy-start.7
  560.3 615.7 %reduce-scatter.4.cloned.1.call-start = ((), (), s32[]{:S(2)}) async-start(), calls=%async_computation.3 | async-start | bytes 5242880 | tf_op jit(solution)/shard_map/reduce_scatter | solution.py:997
  585.7 11.2 copy-start.19
  585.7 11.2 copy-start.24
  605.7 6.3 copy-start.21
  605.8 6.3 copy-start.22
  618.3 2.5 copy-start.3
  620.8 1.8 copy-start.4
  622.5 6.3 copy-start.9
  1176.0 4.4 copy-start.15
  1176.0 5.2 copy-start.14
  1180.5 1.8 copy-start.13
  1180.5 2.9 copy-start.12
  1182.2 2.2 copy-start.11
Sparse Core Ops, SparseCore 0:
  413.9 51.1 reduce-scatter.5
  469.0 34.4 all-gather.1
  560.4 37.9 reduce-scatter.7
  600.8 45.2 reduce-scatter.3

commit v2 on v1

--- a/solution.py
+++ b/solution.py
@@ -364,8 +364,16 @@
     g.start_x(i_seq)
     g.start_x(i_gain)
     g.start_x(i_qb[0])
-    for i in order:
+    zahead = 4
+    for i in order[:zahead]:
         g.start_z(i)
+    zlead = [zahead]
+
+    def more_z():
+        if zlead[0] < len(order):
+            g.start_z(order[zlead[0]])
+            zlead[0] += 1
+
     npiece = ndp
 
     def seq_piece(j, fb):
@@ -424,6 +432,8 @@
             if k == 1:
                 more_x()
             g.forward(i, k)
+            if k == p.nz - 1:
+                more_z()
             done[0] += 1
 
     tick(p.nz - 1)
@@ -658,261 +668,608 @@
 
 
 class DpScatter:
-    def __init__(self, pos, xs, xr, zs, zr, ls):
-        self.p = pos
+    SLOTS = 4
+    AHEAD = 2
+
+    def __init__(self, pos, count, xbuf, zbuf, own, acc, xs, xr, zs, zr, ls, xcredit, zcredit):
+        self.p, self.count = pos, count
+        self.xbuf, self.zbuf, self.own, self.acc = xbuf, zbuf, own, acc
         self.xs, self.xr, self.zs, self.zr, self.ls = xs, xr, zs, zr, ls
+        self.xcredit, self.zcredit = xcredit, zcredit
         self.items = []
-
-    def add(self, src, own, xbuf, zbuf, out, r0, r):
-        self.items.append((src, own, xbuf, zbuf, out, pl.ds(r0, r), r0, r))
-        return len(self.items) - 1
-
-    def xcopy(self, i):
-        src, own, xbuf, zbuf, out, rr, r0, r = self.items[i]
+        self.started = self.stepped = 0
+
+    def add(self, src, base, in_vmem, out, pieces):
+        rows, cols = out.shape
+        r = rows // pieces
+        for c in range(pieces):
+            self.items.append((src, base, in_vmem, out, rows, cols, c * r, r))
+        self.pump()
+
+    def block(self, n, j, x):
+        src, base, in_vmem, out, rows, cols, r0, r = self.items[n]
+        return src.at[pl.ds(al(base + (j * 2 + x) * rows + r0, r), r)]
+
+    def slot(self, buf, n):
+        src, base, in_vmem, out, rows, cols, r0, r = self.items[n]
+        return buf.at[n % self.SLOTS, :, pl.ds(0, r), pl.ds(0, cols)]
+
+    def xcopy(self, n, j):
         return rcopy(
-            src.at[:, 1 - self.p.x, rr], xbuf.at[:, rr], self.xs.at[i], self.xr.at[i], self.p.to_pair
+            self.block(n, j, 1 - self.p.x),
+            self.slot(self.xbuf, n).at[j],
+            self.xs.at[n % self.SLOTS, j],
+            self.xr.at[n % self.SLOTS, j],
+            self.p.to_pair,
         )
 
-    def owncopy(self, i):
-        src, own, xbuf, zbuf, out, rr, r0, r = self.items[i]
-        return pltpu.make_async_copy(src.at[:, self.p.x, rr], own.at[:, rr], self.ls.at[i])
-
-    def start(self, i):
-        self.xcopy(i).start()
-        if self.items[i][1] is not None:
-            self.owncopy(i).start()
-
-    def zcopy(self, i, k):
-        src, own, xbuf, zbuf, out, rr, r0, r = self.items[i]
+    def owncopy(self, n, j):
+        return pltpu.make_async_copy(
+            self.block(n, j, self.p.x), self.slot(self.own, n).at[j], self.ls.at[n % self.SLOTS, j]
+        )
+
+    def zcopy(self, n, k):
         return rcopy(
-            xbuf.at[self.p.zidx(k), rr],
-            zbuf.at[k - 1, rr],
-            self.zs.at[i, k - 1],
-            self.zr.at[i, k - 1],
+            self.slot(self.xbuf, n).at[self.p.zidx(k)],
+            self.slot(self.zbuf, n).at[k - 1],
+            self.zs.at[n % self.SLOTS, k - 1],
+            self.zr.at[n % self.SLOTS, k - 1],
             self.p.to_z(k),
         )
 
-    def combine(self, i):
-        src, own, xbuf, zbuf, out, rr, r0, r = self.items[i]
-        p = self.p
-        self.xcopy(i).wait_recv()
-        if own is not None:
-            self.owncopy(i).wait()
+    def outcopy(self, n):
+        src, base, in_vmem, out, rows, cols, r0, r = self.items[n]
+        return pltpu.make_async_copy(
+            self.acc.at[n % self.SLOTS, pl.ds(0, r), pl.ds(0, cols)],
+            out.at[pl.ds(r0, r)],
+            self.ls.at[n % self.SLOTS, self.p.nz],
+        )
+
+    def pump(self):
+        while self.started < min(len(self.items), self.stepped + self.AHEAD):
+            n = self.started
+            if n >= self.SLOTS:
+                pl.semaphore_wait(self.xcredit, 1)
+                for j in range(self.p.nz):
+                    self.xcopy(n - self.SLOTS, j).wait_send()
+            for j in range(self.p.nz):
+                self.xcopy(n, j).start()
+            for j in range(self.p.nz):
+                self.owncopy(n, j).start()
+            self.started += 1
+
+    def tick(self, steps=1):
+        for _ in range(steps):
+            n = self.stepped
+            if n >= self.started:
+                return
+            self.combine(n)
+            if n >= 1:
+                for k in range(1, self.p.nz):
+                    self.zcopy(n - 1, k).wait_send()
+                if n - 1 + self.SLOTS < self.count:
+                    pl.semaphore_signal(
+                        self.xcredit, inc=1, device_id=self.p.to_pair, device_id_type=MESH
+                    )
+            self.stepped += 1
+            self.pump()
+            if n >= 2:
+                self.finish(n - 2)
+
+    def combine(self, n):
+        src, base, in_vmem, out, rows, cols, r0, r = self.items[n]
+        p, s = self.p, n % self.SLOTS
         tile = 16
-
-        def mine(j, t):
-            if own is None:
-                return src[j, p.x, t, :].astype(F32)
-            return own[j, t, :].astype(F32)
-
+        for j in range(p.nz):
+            self.xcopy(n, j).wait_recv()
+        for j in range(p.nz):
+            self.owncopy(n, j).wait()
         for k in range(1, p.nz):
             j = p.zidx(k)
 
             def add(t, _):
-                t = pl.ds(al(r0 + t * tile, tile), tile)
-                xbuf[j, t, :] = (xbuf[j, t, :].astype(F32) + mine(j, t)).astype(BF16)
+                t = pl.ds(al(t * tile, tile), tile)
+                self.xbuf[s, j, t, :cols] = self.xbuf[s, j, t, :cols] + self.own[s, j, t, :cols]
                 return 0
 
             lax.fori_loop(0, r // tile, add, 0)
-            self.zcopy(i, k).start()
+            if n >= self.SLOTS:
+                pl.semaphore_wait(self.zcredit.at[k - 1], 1)
+            self.zcopy(n, k).start()
+        if n >= self.SLOTS:
+            self.outcopy(n - self.SLOTS).wait()
 
         def keep(t, _):
-            t = pl.ds(al(r0 + t * tile, tile), tile)
-            out[t, :] = xbuf[p.z, t, :].astype(F32) + mine(p.z, t)
+            t = pl.ds(al(t * tile, tile), tile)
+            self.acc[s, t, :cols] = self.xbuf[s, p.z, t, :cols].astype(F32) + self.own[
+                s, p.z, t, :cols
+            ].astype(F32)
             return 0
 
         lax.fori_loop(0, r // tile, keep, 0)
 
-    def finish(self, i):
-        src, own, xbuf, zbuf, out, rr, r0, r = self.items[i]
+    def finish(self, n):
+        src, base, in_vmem, out, rows, cols, r0, r = self.items[n]
+        p, s = self.p, n % self.SLOTS
+        for k in range(1, p.nz):
+            self.zcopy(n, k).wait_recv()
+        tile = 16
+
+        def add(t, _):
+            t = pl.ds(al(t * tile, tile), tile)
+            total = self.acc[s, t, :cols]
+            for k in range(p.nz - 1):
+                total = total + self.zbuf[s, k, t, :cols].astype(F32)
+            self.acc[s, t, :cols] = total
+            return 0
+
+        lax.fori_loop(0, r // tile, add, 0)
+        self.outcopy(n).start()
+        if n + self.SLOTS < self.count:
+            for k in range(1, p.nz):
+                pl.semaphore_signal(
+                    self.zcredit.at[k - 1], inc=1, device_id=p.to_z(-k), device_id_type=MESH
+                )
+
+    def drain(self):
+        self.tick(self.count)
+        last = self.count - 1
         for k in range(1, self.p.nz):
-            self.zcopy(i, k).wait_recv()
-        tile = 16
-
-        def add(t, _):
-            t = pl.ds(al(r0 + t * tile, tile), tile)
-            total = out[t, :]
-            for k in range(self.p.nz - 1):
-                total = total + zbuf[k, t, :].astype(F32)
-            out[t, :] = total
+            self.zcopy(last, k).wait_send()
+        self.finish(last - 1)
+        self.finish(last)
+        for n in range(max(0, self.count - self.SLOTS), self.count):
+            self.outcopy(n).wait()
+        for n in range(max(0, self.count - self.SLOTS), self.count):
+            for j in range(self.p.nz):
+                self.xcopy(n, j).wait_send()
+
+
+def piece_rows(rows, nz):
+    return min(rows, max(16, 256 // nz))
+
+
+def backward_kernel(
+    cfg,
+    tok,
+    dout,
+    middle,
+    latent,
+    normed,
+    gains,
+    cos,
+    sin,
+    bias,
+    gw_gate,
+    gw_up,
+    gw_down,
+    gnt,
+    lkv_h,
+    q_h,
+    mixed_h,
+    qb_h,
+    out_h,
+    seq_h,
+    o_gate,
+    o_up,
+    o_down,
+    o_out,
+    o_qb,
+    o_seq,
+    o_gain,
+    o_in,
+    gnt_v,
+    fcore_v,
+    fy_v,
+    proj_v,
+    gmid_v,
+    gnorm_v,
+    lkv_v,
+    q_v,
+    mixed_v,
+    gm_v,
+    kv_acc,
+    qb_v,
+    out_v,
+    seq_v,
+    seqy_v,
+    gall_v,
+    gain_rx,
+    gain_acc,
+    xbuf,
+    zbuf,
+    own_b,
+    acc_b,
+    xs,
+    xr,
+    zs,
+    zr,
+    dls,
+    xcredit,
+    zcredit,
+    fss,
+    frs,
+    gs,
+    gr,
+    ls,
+):
+    ndp, own, dim, rank, hd, heads, pieces = cfg
+    rows = NF * own
+    t2 = own // 2
+    kvw = rank + 2 * hd
+    wide = dim // rank
+    p = Place(ndp)
+    nz = p.nz
+    sr = o_seq.shape[0]
+    local = []
+
+    def local_copy(src, dst):
+        c = pltpu.make_async_copy(src, dst, ls.at[len(local)])
+        c.start()
+        local.append(c)
+        return c
+
+    gnt_own = local_copy(gnt.at[pl.ds(al(p.f * own, own), own)], gnt_v.at[0])
+    gnt_y = local_copy(gnt.at[pl.ds(al(p.f_y * own, own), own)], gnt_v.at[1])
+    out_in = local_copy(out_h, out_v)
+    mixed_in = local_copy(mixed_h, mixed_v)
+    q_in = local_copy(q_h, q_v)
+    lkv_in = local_copy(lkv_h, lkv_v)
+    qb_in = local_copy(qb_h, qb_v)
+    seq_in = local_copy(seq_h, seq_v)
+    sc = DpScatter(
+        p, sum(pieces), xbuf, zbuf, own_b, acc_b, xs, xr, zs, zr, dls, xcredit, zcredit
+    )
+    p.barrier()
+
+    def gnt_block(b):
+        return gnt.at[pl.ds(al(b * own, own), own)]
+
+    red1 = FsReduce(p, gnt_block, fcore_v, fy_v, fss.at[0], frs.at[0])
+    red1.start()
+    sc.add(gw_gate, 0, False, o_gate, pieces[0])
+    sc.add(gw_up, 0, False, o_up, pieces[1])
+    sc.add(gw_down, 0, False, o_down, pieces[2])
+    gnt_y.wait()
+    gnt_own.wait()
+    red1.c1().wait_recv()
+
+    def add_y(t, _):
+        r = pl.ds(al(t * 64, 64), 64)
+        fcore_v[1, r, :] = fcore_v[1, r, :] + gnt_v[1, r, :]
+        return 0
+
+    lax.fori_loop(0, own // 64, add_y, 0)
+    red1.cy().start()
+    sc.tick(1)
+    red1.end()
+    red1.wait_sends()
+    gain_two = jnp.concatenate([gains[wide + r : wide + r + 1] for r in range(wide)], axis=1)
+    gain_one = jnp.concatenate([gains[r : r + 1] for r in range(wide)], axis=1)
+    gain_lat = gains[2 * wide : 2 * wide + 1]
+    part_two = jnp.zeros((1, dim), F32)
+    for m in range(2):
+        rr = pl.ds(m * t2, t2)
+        e = gnt_v[0, rr, :].astype(F32) + fcore_v[0, rr, :].astype(F32) + fy_v[rr, :].astype(F32)
+        v = middle[rr, :]
+        inv = lax.rsqrt(jnp.mean(v * v, axis=-1, keepdims=True) + EPSILON)
+        part_two += jnp.sum(e * v * inv, axis=0, keepdims=True)
+        scaled = e * gain_two
+        inner = jnp.mean(scaled * v, axis=-1, keepdims=True)
+        g = dout[m].astype(F32) + inv * scaled - v * (inv * inv * inv * inner)
+        gmid_v[rr, :] = g
+        proj_v[pl.ds(al(p.f * own + m * t2, t2), t2), :] = g.astype(BF16)
+    gain_acc[0] = jnp.zeros(gain_acc.shape[1:], F32)
+    for r in range(wide):
+        gain_acc[0, pl.ds(wide + r, 1), :] = part_two[:, r * rank : (r + 1) * rank]
+    ag = FsGather(p, lambda b: proj_v.at[pl.ds(al(b * own, own), own)], fss.at[1], frs.at[1])
+    ag.start()
+    sc.tick(1)
+    ag.mid()
+    sc.tick(1)
+    out_in.wait()
+    ag.end()
+    ag.wait_sends()
+
+    def back_out(j, _):
+        cols = pl.ds(al(j * 256, 256), 256)
+        for r in range(rows // 512):
+            rr = pl.ds(r * 512, 512)
+            gm_v[rr, cols] = mm(proj_v[rr, :], out_v[:, cols]).astype(BF16)
+        return 0
+
+    lax.fori_loop(0, heads * hd // 256, back_out, 0)
+    sc.tick(1)
+    mixed_in.wait()
+
+    def grad_out(j, _):
+        cols = pl.ds(al(j * 256, 256), 256)
+        out_v[cols, :] = mm_tn(proj_v[:, cols], mixed_v[...]).astype(BF16)
+        return 0
+
+    lax.fori_loop(0, dim // 256, grad_out, 0)
+    sc.tick(1)
+    sc.add(out_v, 0, True, o_out, pieces[3])
+    q_in.wait()
+    lkv_in.wait()
+    scale = hd ** (-0.5)
+    half = hd // 2
+    kcols, vcols = slice(rank, rank + hd), slice(rank + hd, rank + 2 * hd)
+    causal = causal_bias(PROMPT)
+    everything = slice(None)
+
+    for m in range(2):
+        k0, k1 = (group_rows(lkv_v, m, h2, kcols, own) for h2 in (0, 1))
+        v0, v1 = (group_rows(lkv_v, m, h2, vcols, own) for h2 in (0, 1))
+        low = bias[m]
+        kv_acc[...] = jnp.zeros(kv_acc.shape, F32)
+
+        def put_query(h, which, g):
+            co = group_rows(cos, m, which, everything, own)
+            si = group_rows(sin, m, which, everything, own)
+            a, b = g[:, :half] * scale, g[:, half:] * scale
+            c0 = pl.ds(al(h * hd, half), half)
+            c1 = pl.ds(al(h * hd + half, half), half)
+            put_rows(gm_v, m, which, c0, own, (a * co + b * si).astype(BF16))
+            put_rows(gm_v, m, which, c1, own, (b * co - a * si).astype(BF16))
+
+        def attend_back(h, _):
+            cols = pl.ds(al(h * hd, hd), hd)
+            q0 = group_rows(q_v, m, 0, cols, own)
+            g0 = group_rows(gm_v, m, 0, cols, own)
+            pr = softmax_parts(mm_nt(q0, k0) * scale + causal)
+            gp = mm_nt(g0, v0)
+            gsc = (pr * (gp - jnp.sum(pr * gp, axis=-1, keepdims=True))).astype(BF16)
+            kv_acc[2] += mm_tn(pr.astype(BF16), g0)
+            kv_acc[0] += mm_tn(gsc, q0)
+            put_query(h, 0, mm(gsc, k0))
+            q1 = group_rows(q_v, m, 1, cols, own)
+            g1 = group_rows(gm_v, m, 1, cols, own)
+            s0 = mm_nt(q1, k0) * scale
+            s1 = mm_nt(q1, k1) * scale + low
+            top = jnp.maximum(
+                jnp.max(s0, axis=-1, keepdims=True), jnp.max(s1, axis=-1, keepdims=True)
+            )
+            e0, e1 = jnp.exp(s0 - top), jnp.exp(s1 - top)
+            total = jnp.sum(e0, axis=-1, keepdims=True) + jnp.sum(e1, axis=-1, keepdims=True)
+            p0, p1 = e0 / total, e1 / total
+            gp0, gp1 = mm_nt(g1, v0), mm_nt(g1, v1)
+            inner = jnp.sum(p0 * gp0, axis=-1, keepdims=True) + jnp.sum(
+                p1 * gp1, axis=-1, keepdims=True
+            )
+            gs0 = (p0 * (gp0 - inner)).astype(BF16)
+            gs1 = (p1 * (gp1 - inner)).astype(BF16)
+            kv_acc[2] += mm_tn(p0.astype(BF16), g1)
+            kv_acc[3] += mm_tn(p1.astype(BF16), g1)
+            kv_acc[0] += mm_tn(gs0, q1)
+            kv_acc[1] += mm_tn(gs1, q1)
+            put_query(h, 1, mm(gs0, k0) + mm(gs1, k1))
             return 0
 
-        lax.fori_loop(0, r // tile, add, 0)
-
-    def wait_sends(self, i):
-        self.xcopy(i).wait_send()
-        for k in range(1, self.p.nz):
-            self.zcopy(i, k).wait_send()
-
-
-def scatter_kernel(ndp, pieces, n, *refs):
-    refs = list(refs)
-
-    def take(c):
-        out = refs[:c]
-        del refs[:c]
-        return out
-
-    heads = take(n)
-    seq, gain = take(2)
-    outs = take(n)
-    seq_o, gain_o = take(2)
-    owns, xbufs, zbufs = take(n), take(n), take(n)
-    seq_own, seq_core, seq_y, seq_x, seq_z, gain_rx, gain_acc = take(7)
-    xs, xr, zs, zr, ls, gs, gr, qs, qr, qls = take(10)
-    p = Place(ndp)
-    sc = DpScatter(p, xs, xr, zs, zr, ls)
-    head_items = []
-    for w in range(n):
-        rows = outs[w].shape[0]
-        step = rows // pieces[w]
-        for c in range(pieces[w]):
-            head_items.append(
-                sc.add(heads[w], owns[w], xbufs[w], zbufs[w], outs[w], c * step, step)
-            )
-    sr = seq_o.shape[0]
-    seq_item = sc.add(seq_core.at[0], None, seq_x, seq_z, seq_o, 0, sr)
-    own_f = pltpu.make_async_copy(seq.at[:, :, p.f], seq_own.at[0], qls.at[0])
-    own_y = pltpu.make_async_copy(seq.at[:, :, p.f_y], seq_own.at[1], qls.at[1])
-    own_y.start()
-    own_f.start()
-    p.barrier()
-    c1 = rcopy(seq.at[:, :, p.f_yc], seq_core.at[1], qs.at[1], qr.at[1], p.to_core)
-    c0 = rcopy(seq.at[:, :, p.f_core], seq_core.at[0], qs.at[0], qr.at[0], p.to_core)
-    cy = rcopy(seq_core.at[1], seq_y, qs.at[2], qr.at[2], p.to_y)
+        lax.fori_loop(0, heads, attend_back, 0)
+        for h2 in (0, 1):
+            put_rows(proj_v, m, h2, kcols, own, (kv_acc[h2] * scale).astype(BF16))
+            put_rows(proj_v, m, h2, vcols, own, kv_acc[2 + h2].astype(BF16))
+        sc.tick(1)
+    qb_in.wait()
+
+    def back_latent(j, _):
+        wr = pl.ds(al(j * 256, 256), 256)
+        for r in range(rows // 512):
+            rr = pl.ds(r * 512, 512)
+            proj_v[rr, wr] = mm_nt(gm_v[rr, :], qb_v[wr, :]).astype(BF16)
+        return 0
+
+    lax.fori_loop(0, rank // 256, back_latent, 0)
+
+    def grad_qb(j, _):
+        cols = pl.ds(al(j * 256, 256), 256)
+        qb_v[cols, :] = mm_tn(lkv_v[:, cols], gm_v[...]).astype(BF16)
+        return 0
+
+    lax.fori_loop(0, rank // 256, grad_qb, 0)
+    narrow = pl.ds(0, kvw)
+    red2 = FsReduce(
+        p,
+        lambda b: proj_v.at[pl.ds(al(b * own, own), own), narrow],
+        fcore_v.at[:, :, narrow],
+        fy_v.at[:, narrow],
+        fss.at[2],
+        frs.at[2],
+    )
+    red2.start()
+    sc.tick(1)
+    sc.add(qb_v, 0, True, o_qb, pieces[4])
+    red2.mid(own)
+    sc.tick(1)
+    red2.end()
+    own_rows = pl.ds(al(p.f * own, own), own)
+    part_lat = jnp.zeros((1, rank), F32)
+    for m in range(2):
+        rr = pl.ds(m * t2, t2)
+        gr_rows = pl.ds(al(p.f * own + m * t2, t2), t2)
+        e = red2.value(rr)
+        v = latent[rr, :]
+        inv = lax.rsqrt(jnp.mean(v * v, axis=-1, keepdims=True) + EPSILON)
+        el = e[:, :rank]
+        part_lat += jnp.sum(el * v * inv, axis=0, keepdims=True)
+        scaled = el * gain_lat
+        inner = jnp.mean(scaled * v, axis=-1, keepdims=True)
+        gall_v[rr, :rank] = (inv * scaled - v * (inv * inv * inv * inner)).astype(BF16)
+        co, si = cos[gr_rows, :], sin[gr_rows, :]
+        a, b = e[:, rank : rank + half], e[:, rank + half : rank + hd]
+        gall_v[rr, rank : rank + half] = (a * co + b * si).astype(BF16)
+        gall_v[rr, rank + half : rank + hd] = (b * co - a * si).astype(BF16)
+        gall_v[rr, rank + hd :] = e[:, rank + hd :].astype(BF16)
+    gain_acc[0, pl.ds(2 * wide, 1), :] = part_lat
+    seq_in.wait()
+
+    def back_seq(j, _):
+        wr = pl.ds(al(j * 256, 256), 256)
+        gnorm_v[:, wr] = mm_nt(gall_v[...], seq_v[wr, :])
+        return 0
+
+    lax.fori_loop(0, dim // 256, back_seq, 0)
+    sc.tick(1)
+    span = NF * sr
+
+    def grad_seq(j, _):
+        cols = pl.ds(al(j * 256, 256), 256)
+        g = mm_tn(normed[:, cols], gall_v[...]).astype(BF16)
+        for i in range(256 // span):
+            for fb in range(NF):
+                seq_v[pl.ds(al(fb * ndp * sr + (j * (256 // span) + i) * sr, sr), sr), :] = g[
+                    i * span + fb * sr : i * span + (fb + 1) * sr
+                ]
+        return 0
+
+    lax.fori_loop(0, dim // 256, grad_seq, 0)
+    srows = ndp * sr
+    core3 = [lkv_v.at[pl.ds(0, srows)], lkv_v.at[pl.ds(srows, srows)]]
+
+    def sblock(b):
+        return seq_v.at[pl.ds(al(b * srows, srows), srows)]
+
+    c1 = rcopy(sblock(p.f_yc), core3[1], fss.at[3, 1], frs.at[3, 1], p.to_core)
+    c0 = rcopy(sblock(p.f_core), core3[0], fss.at[3, 0], frs.at[3, 0], p.to_core)
+    cy = rcopy(core3[1], seqy_v, fss.at[3, 2], frs.at[3, 2], p.to_y)
     c1.start()
     c0.start()
-    gains = [
-        rcopy(gain, gain_rx.at[0], gs.at[0], gr.at[0], p.to_core),
-        rcopy(gain_acc.at[0], gain_rx.at[1], gs.at[1], gr.at[1], p.to_y),
-        rcopy(gain_acc.at[1], gain_rx.at[2], gs.at[2], gr.at[2], p.to_pair),
+    part_one = jnp.zeros((1, dim), F32)
+    for m in range(2):
+        rr = pl.ds(m * t2, t2)
+        e = gnorm_v[rr, :]
+        v = tok[m].astype(F32)
+        inv = lax.rsqrt(jnp.mean(v * v, axis=-1, keepdims=True) + EPSILON)
+        part_one += jnp.sum(e * v * inv, axis=0, keepdims=True)
+        scaled = e * gain_one
+        inner = jnp.mean(scaled * v, axis=-1, keepdims=True)
+        o_in[m] = (gmid_v[rr, :] + inv * scaled - v * (inv * inv * inv * inner)).astype(BF16)
+    for r in range(wide):
+        gain_acc[0, pl.ds(r, 1), :] = part_one[:, r * rank : (r + 1) * rank]
+    gain_steps = [
+        rcopy(gain_acc.at[0], gain_rx.at[0], gs.at[0], gr.at[0], p.to_core),
+        rcopy(gain_acc.at[1], gain_rx.at[1], gs.at[1], gr.at[1], p.to_y),
+        rcopy(gain_acc.at[2], gain_rx.at[2], gs.at[2], gr.at[2], p.to_pair),
     ] + [
-        rcopy(gain_acc.at[2], gain_rx.at[2 + k], gs.at[2 + k], gr.at[2 + k], p.to_z(k))
-        for k in range(1, p.nz)
+        rcopy(gain_acc.at[3], gain_rx.at[2 + k], gs.at[2 + k], gr.at[2 + k], p.to_z(k))
+        for k in range(1, nz)
     ]
-    gains[0].start()
-    for i in head_items:
-        sc.start(i)
-    gains[0].wait_recv()
-    gain_acc[0] = gain[...] + gain_rx[0]
-    gains[1].start()
-    gains[1].wait_recv()
-    gain_acc[1] = gain_acc[0] + gain_rx[1]
-    gains[2].start()
-    own_y.wait()
-    own_f.wait()
+    gain_steps[0].start()
     c1.wait_recv()
-    nz = p.nz
-
-    def add_y(j, _):
-        for x in range(2):
-            seq_core[1, j, x] = (
-                seq_core[1, j, x].astype(F32) + seq_own[1, j, x].astype(F32)
-            ).astype(BF16)
+
+    def seq_y(t, _):
+        t = al(t * 64, 64)
+        a = pl.ds(srows + t, 64)
+        b = pl.ds(al(p.f_y * srows + t, 64), 64)
+        lkv_v[a, :] = lkv_v[a, :] + seq_v[b, :]
         return 0
 
-    lax.fori_loop(0, nz, add_y, 0)
+    lax.fori_loop(0, srows // 64, seq_y, 0)
     cy.start()
-    gains[2].wait_recv()
-    gain_acc[2] = gain_acc[1] + gain_rx[2]
-    for k in range(1, nz):
-        gains[2 + k].start()
-    sc.combine(head_items[0])
+    for n in range(3):
+        gain_steps[n].wait_recv()
+        gain_acc[n + 1] = gain_acc[n] + gain_rx[n]
+        if n < 2:
+            gain_steps[n + 1].start()
+        else:
+            for k in range(1, nz):
+                gain_steps[2 + k].start()
+        sc.tick(1)
     c0.wait_recv()
     cy.wait_recv()
 
-    def add_f(j, _):
-        for x in range(2):
-            seq_core[0, j, x] = (
-                seq_core[0, j, x].astype(F32)
-                + seq_own[0, j, x].astype(F32)
-                + seq_y[j, x].astype(F32)
-            ).astype(BF16)
+    def seq_f(t, _):
+        t = al(t * 64, 64)
+        a = pl.ds(t, 64)
+        b = pl.ds(al(p.f * srows + t, 64), 64)
+        seq_v[b, :] = (
+            lkv_v[a, :].astype(F32) + seq_v[b, :].astype(F32) + seqy_v[a, :].astype(F32)
+        ).astype(BF16)
         return 0
 
-    lax.fori_loop(0, nz, add_f, 0)
-    sc.start(seq_item)
-    todo = head_items[1:] + [seq_item]
-    for i in todo:
-        sc.combine(i)
-    total = gain_acc[2]
+    lax.fori_loop(0, srows // 64, seq_f, 0)
+    sc.add(seq_v, p.f * srows, True, o_seq, pieces[5])
+    total = gain_acc[3]
     for k in range(1, nz):
-        gains[2 + k].wait_recv()
+        gain_steps[2 + k].wait_recv()
         total = total + gain_rx[2 + k]
-    gain_o[...] = total
-    for i in head_items + [seq_item]:
-        sc.finish(i)
-    for i in head_items + [seq_item]:
-        sc.wait_sends(i)
-    for t in [c1, c0, cy] + gains:
+    o_gain[...] = total
+    sc.drain()
+    red2.wait_sends()
+    for t in [c1, c0, cy] + gain_steps:
         t.wait_send()
 
 
-def scatter_call(ndp, heads, seq, gain):
+def backward_call(ndp, tok, dout, middle, latent, normed, gains, cos, sin, bias, grads, gnt, saved):
+    lkv, q, mixed, qb, out, seq = saved
     nz = ndp // 2
-    n = len(heads)
-    shards = [(w.shape[0] // ndp, w.shape[1]) for w in heads]
-    pieces = [2 if s[0] % 32 == 0 else 1 for s in shards]
-    n_items = sum(pieces) + 1
-    sr, kvw = seq.shape[0] // (ndp * NF), seq.shape[1]
+    own, dim = middle.shape
+    rank = latent.shape[1]
+    kvw = lkv.shape[1]
+    hd = (kvw - rank) // 2
+    heads = q.shape[1] // hd
+    rows = NF * own
+    sr = seq.shape[0] // (ndp * NF)
+    shards = [(w.shape[0] // ndp, w.shape[1]) for w in grads] + [
+        (out.shape[0] // ndp, out.shape[1]),
+        (qb.shape[0] // ndp, qb.shape[1]),
+        (sr, kvw),
+    ]
+    pieces = tuple(s[0] // piece_rows(s[0], nz) for s in shards)
+    n = sum(pieces)
+    slots = DpScatter.SLOTS
+    pr = max(piece_rows(s[0], nz) for s in shards)
+    width = max(s[1] for s in shards)
     dma = pltpu.SemaphoreType.DMA
-    scratch = (
-        [pltpu.VMEM((nz,) + s, BF16) for s in shards]
-        + [pltpu.VMEM((nz,) + s, BF16) for s in shards]
-        + [pltpu.VMEM((nz - 1,) + s, BF16) for s in shards]
-        + [
-            pltpu.VMEM((2, nz, 2, sr, kvw), BF16),
-            pltpu.VMEM((2, nz, 2, sr, kvw), BF16),
-            pltpu.VMEM((nz, 2, sr, kvw), BF16),
-            pltpu.VMEM((nz, sr, kvw), BF16),
-            pltpu.VMEM((nz - 1, sr, kvw), BF16),
-            pltpu.VMEM((2 + nz,) + gain.shape, F32),
-            pltpu.VMEM((3,) + gain.shape, F32),
-            dma((n_items,)),
-            dma((n_items,)),
-            dma((n_items, nz - 1)),
-            dma((n_items, nz - 1)),
-            dma((n_items,)),
-            dma((2 + nz,)),
-            dma((2 + nz,)),
-            dma((3,)),
-            dma((3,)),
-            dma((2,)),
-        ]
-    )
+    scratch = [
+        pltpu.VMEM((2, own, dim), BF16),
+        pltpu.VMEM((2, own, dim), BF16),
+        pltpu.VMEM((own, dim), BF16),
+        pltpu.VMEM((rows, dim), BF16),
+        pltpu.VMEM((own, dim), F32),
+        pltpu.VMEM((own, dim), F32),
+        pltpu.VMEM(lkv.shape, BF16),
+        pltpu.VMEM(q.shape, BF16),
+        pltpu.VMEM(mixed.shape, BF16),
+        pltpu.VMEM(q.shape, BF16),
+        pltpu.VMEM((4, rows // 4, hd), F32),
+        pltpu.VMEM(qb.shape, BF16),
+        pltpu.VMEM(out.shape, BF16),
+        pltpu.VMEM(seq.shape, BF16),
+        pltpu.VMEM((ndp * sr, kvw), BF16),
+        pltpu.VMEM((own, kvw), BF16),
+        pltpu.VMEM((2 + nz,) + gains.shape, F32),
+        pltpu.VMEM((4,) + gains.shape, F32),
+        pltpu.VMEM((slots, nz, pr, width), BF16),
+        pltpu.VMEM((slots, nz - 1, pr, width), BF16),
+        pltpu.VMEM((slots, nz, pr, width), BF16),
+        pltpu.VMEM((slots, pr, width), F32),
+        dma((slots, nz)),
+        dma((slots, nz)),
+        dma((slots, nz - 1)),
+        dma((slots, nz - 1)),
+        dma((slots, nz + 1)),
+        pltpu.SemaphoreType.REGULAR,
+        pltpu.SemaphoreType.REGULAR((nz - 1,)),
+        dma((4, 3)),
+        dma((4, 3)),
+        dma((2 + nz,)),
+        dma((2 + nz,)),
+        dma((8,)),
+    ]
     return pl.pallas_call(
-        functools.partial(scatter_kernel, ndp, pieces, n),
+        functools.partial(backward_kernel, (ndp, own, dim, rank, hd, heads, pieces)),
         out_shape=tuple(jax.ShapeDtypeStruct(s, F32) for s in shards)
-        + (jax.ShapeDtypeStruct((sr, kvw), F32), jax.ShapeDtypeStruct(gain.shape, F32)),
-        in_specs=(ANY,) * (n + 1) + (VMEM,),
-        out_specs=(VMEM,) * (n + 2),
+        + (jax.ShapeDtypeStruct(gains.shape, F32), jax.ShapeDtypeStruct(tok.shape, BF16)),
+        in_specs=(VMEM,) * 9 + (ANY,) * 10,
+        out_specs=(ANY,) * 6 + (VMEM,) * 2,
         scratch_shapes=scratch,
         compiler_params=pltpu.CompilerParams(
-            collective_id=1, has_side_effects=True, vmem_limit_bytes=60 * 2**20
+            collective_id=1, has_side_effects=True, vmem_limit_bytes=62 * 2**20
         ),
-        name="scatter_grads",
-    )(*[w.reshape((nz, 2) + s) for w, s in zip(heads, shards)], seq.reshape(nz, 2, NF, sr, kvw), gain)
-
-
-def unrotate(vector, cos_tab, sin_tab):
-    half_width = vector.shape[-1] // 2
-    lower_half = vector[..., :half_width]
-    upper_half = vector[..., half_width:]
-    return jnp.concatenate(
-        [lower_half * cos_tab + upper_half * sin_tab, upper_half * cos_tab - lower_half * sin_tab],
-        axis=-1,
-    )
-
-
-def norm_back(grad_in, values, inverse, gain):
-    scaled = grad_in * gain
-    gain_term = jnp.sum(grad_in * values * inverse, axis=0)
-    inner_sum = jnp.mean(scaled * values, axis=-1, keepdims=True)
-    return (inverse * scaled - values * inverse * inverse * inverse * inner_sum, gain_term)
-
-
-def inverse_rms(v):
-    return lax.rsqrt(jnp.mean(v * v, axis=-1, keepdims=True) + EPSILON)
+        name="backward_scatter",
+    )(tok, dout, middle, latent, normed, gains, cos, sin, bias, *grads, gnt, lkv, q, mixed, qb, out, seq)
 
 
 def per_device(
@@ -977,10 +1334,6 @@
     ) = forward_call(
         ndp, tokens, d_output, cos, sin, bias, seq_sh, gain_sh, w_qb, w_out, w_gate, w_up, w_down
     )
-    gain_one = gains[:wide].reshape(1, dim)
-    gain_two = gains[wide : 2 * wide].reshape(1, dim)
-    gain_lat = gains[2 * wide].reshape(1, rank)
-
     gate = jnp.dot(n2, gate_all, preferred_element_type=F32)
     up = jnp.dot(n2, up_all, preferred_element_type=F32)
     sig = jax.nn.sigmoid(gate)
@@ -996,74 +1349,20 @@
 
     ffn_own = lax.psum_scatter(ffn_part, "fsdp", scatter_dimension=0, tiled=True).astype(F32)
     output = (middle + ffn_own).astype(BF16).reshape(tokens.shape)
-    grad_n2 = lax.psum_scatter(gnt_part, "fsdp", scatter_dimension=0, tiled=True).astype(F32)
-    grad_mid_norm, g_gain_two = norm_back(grad_n2, middle, inverse_rms(middle), gain_two)
-    grad_middle = d_output.reshape(own, dim).astype(F32) + grad_mid_norm
-    proj_all = lax.all_gather(grad_middle.astype(BF16), "fsdp", axis=0, tiled=True)
-    gw_out = mm_tn(proj_all, mixed).astype(BF16)
-    grad_mixed = mm(proj_all, out_all).astype(BF16)
-
-    def by_group(v, *tail_shape):
-        return (
-            v.reshape((NF, micro, tlen) + tail_shape)
-            .swapaxes(0, 1)
-            .reshape((micro, NF * tlen) + tail_shape)
-        )
-
-    def by_block(v):
-        tail_shape = v.shape[2:]
-        return (
-            v.reshape((micro, NF, tlen) + tail_shape)
-            .swapaxes(0, 1)
-            .reshape((rows,) + tail_shape)
-        )
-
-    scale = hd ** (-0.5)
-    ki = jnp.arange(NF * tlen, dtype=jnp.int32)
-    allowed = (ki[None, None, :] <= ki[None, :, None]) & (
-        (labels[:, None, :] == 0) | (labels[:, None, :] == labels[:, :, None])
-    )
-    qg = by_group(q_all, heads, hd) if False else by_group(q_all.reshape(rows, heads, hd), heads, hd)
-    gm = by_group(grad_mixed.reshape(rows, heads, hd), heads, hd)
-    keys = by_group(lkv[:, rank : rank + hd], hd)
-    values = by_group(lkv[:, rank + hd :], hd)
-    scores = jnp.einsum("mqhd,mkd->mhqk", qg, keys, preferred_element_type=F32) * scale
-    scores = jnp.where(allowed[:, None], scores, MASK_FILL)
-    probs = jax.nn.softmax(scores, axis=-1)
-    gp = jnp.einsum("mqhd,mkd->mhqk", gm, values, preferred_element_type=F32)
-    gv = jnp.einsum("mhqk,mqhd->mkd", probs.astype(BF16), gm, preferred_element_type=F32)
-    gs = (probs * (gp - jnp.sum(probs * gp, axis=-1, keepdims=True))).astype(BF16)
-    gq = jnp.einsum("mhqk,mkd->mqhd", gs, keys, preferred_element_type=F32) * scale
-    gk = jnp.einsum("mhqk,mqhd->mkd", gs, qg, preferred_element_type=F32) * scale
-    gq = unrotate(by_block(gq), cos[:, None, :], sin[:, None, :]).astype(BF16)
-    gq = gq.reshape(rows, heads * hd)
-    gw_qb = mm_tn(lkv[:, :rank], gq).astype(BF16)
-    glat_part = mm_nt(gq, qb_all).astype(BF16)
-    packed = jnp.concatenate(
-        [glat_part, by_block(gk).astype(BF16), by_block(gv).astype(BF16)], axis=1
-    )
-    back_own = lax.psum_scatter(packed, "fsdp", scatter_dimension=0, tiled=True).astype(F32)
-    cos_own = lax.dynamic_slice_in_dim(cos, lax.axis_index("fsdp") * own, own, 0)
-    sin_own = lax.dynamic_slice_in_dim(sin, lax.axis_index("fsdp") * own, own, 0)
-    g_lat, g_gain_lat = norm_back(back_own[:, :rank], latent, inverse_rms(latent), gain_lat)
-    g_key = unrotate(back_own[:, rank : rank + hd], cos_own, sin_own)
-    g_all = jnp.concatenate([g_lat, g_key, back_own[:, rank + hd :]], axis=1).astype(BF16)
-    gw_seq = mm_tn(normed, g_all).astype(BF16)
-    grad_normed = mm_nt(g_all, seq_all)
-    inputs = tokens.reshape(own, dim).astype(F32)
-    grad_in, g_gain_one = norm_back(grad_normed, inputs, inverse_rms(inputs), gain_one)
-    input_grad = (grad_middle + grad_in).astype(BF16).reshape(tokens.shape)
-    gain_part = jnp.concatenate(
-        [
-            g_gain_one.reshape(wide, rank),
-            g_gain_two.reshape(wide, rank),
-            g_gain_lat.reshape(1, rank),
-        ],
-        axis=0,
-    )
-    gain_part = jnp.pad(gain_part, ((0, 8 - gain_part.shape[0]), (0, 0)))
-    o_gate, o_up, o_down, o_out, o_qb, o_seq, o_gain = scatter_call(
-        ndp, (gw_gate, gw_up, gw_down, gw_out, gw_qb), gw_seq, gain_part
+    o_gate, o_up, o_down, o_out, o_qb, o_seq, o_gain, input_grad = backward_call(
+        ndp,
+        tokens,
+        d_output,
+        middle,
+        latent,
+        normed,
+        gains,
+        cos,
+        sin,
+        bias,
+        (gw_gate, gw_up, gw_down),
+        gnt_part,
+        (lkv, q_all, mixed, qb_all, out_all, seq_all),
     )
 
     def own_gain(flat, width):

time: 1200 us -> 774 us (0.65)
  Pallas kernels: 876 us -> 639 us
  matrix products: 152 us -> 83.5 us
  waiting for transfers between devices: 62.2 us -> 0.02 us
  local copies, waits for them, and re-layouts: 52.2 us -> 17.3 us
  other arithmetic: 34.9 us -> 12.8 us
    pallas_call x1, Pallas kernels: 534 us -> 342 us  [backward_call(): pl.pallas_call(functools.partial(backward_kernel, (ndp, own, dim, rank, h...]
    reduce_scatter x2 -> x0, waiting for transfers between devices: 49.5 us -> none  [the longest x1 49.5 us: per_device(): lax.psum_scatter(gnt_part, 'fsdp', scatter_dimension=0, tiled=True)]
    pallas_call x1, Pallas kernels: 342 us -> 298 us  [forward_call(): pl.pallas_call(functools.partial(forward_kernel, (ndp, own, dim, rank, hd...]
    dot_general x6 -> x3, matrix products: 49.3 us -> 29 us  [mm_tn(): lax.dot_general(a, b, (((0,), (0,)), ((), ())), preferred_element_type=F32)]
    dot_general x5 -> x0, matrix products: 20.3 us -> none  [the longest x1 9.33 us: mm(): lax.dot_general(a, b, (((1,), (0,)), ((), ())), preferred_element_type=F32)]
    dot_general x5 -> x3, matrix products: 39.2 us -> 23.5 us  [mm_nt(): lax.dot_general(a, b, (((1,), (1,)), ((), ())), preferred_element_type=F32)]
    all_gather x1 -> x0, waiting for transfers between devices: 12.7 us -> none  [per_device(): lax.all_gather(grad_middle.astype(BF16), 'fsdp', axis=0, tiled=True)]
  transfers between devices with their start and end apart: 4 -> 1, of which waited for: 2 -> 0; matrix products, arithmetic and copies ran while one was open for 9% -> 7% of each run, Pallas kernels for 45% -> 45%
where the time goes in v2:
time: 774 us; the launch traced here: 768 us
  Pallas kernels  639 us (83%)
  matrix products  83.5 us (11%)
  local copies, waits for them, and re-layouts  17.3 us (2%)
  between operations  14.5 us (2%)
  other arithmetic  12.8 us (2%)
    pallas_call x1, Pallas kernels, backward_call(): pl.pallas_call(functools.partial(backward_kernel, (ndp, own, dim, rank, h...  342 us
    pallas_call x1, Pallas kernels, forward_call(): pl.pallas_call(functools.partial(forward_kernel, (ndp, own, dim, rank, hd...  298 us
    dot_general x3, matrix products, mm_tn(): lax.dot_general(a, b, (((0,), (0,)), ((), ())), preferred_element_type=F32)  29 us
    dot_general x3, matrix products, mm_nt(): lax.dot_general(a, b, (((1,), (1,)), ((), ())), preferred_element_type=F32)  23.5 us
  transfers between devices with their start and end apart: 1, of which 0 were waited for; matrix products, arithmetic and copies ran while one was open for 7% of the time, Pallas kernels for 45%

profile of v2, /device:TPU:0, one launch (start us, length us, event | category | flops | bytes accessed | tf_op | source)
XLA Modules:
  0.0 767.6 jit_solution(4715652122607389938)
XLA Ops:
  7.2 0.0 reduce-scatter.2.cloned.1.call-start
  7.3 0.7 broadcast_compare_fusion
  8.0 0.8 fusion.3
  8.8 0.1 iota.88
  8.9 0.1 iota.89
  9.0 0.7 broadcast_in_dim.73
  9.6 0.1 broadcast_in_dim.74
  9.7 0.7 broadcast_in_dim.77
  10.4 0.1 broadcast_in_dim.78
  10.4 0.7 convert_element_type.68
  11.1 0.1 broadcast_select_fusion
  11.2 0.1 select_n.50
  11.3 0.9 convert_reduce_fusion
  12.2 0.1 broadcast_in_dim.69
  12.3 0.1 mul.88
  12.4 0.1 broadcast_in_dim.68
  12.4 0.1 gt.15
  12.5 0.1 convert_bitcast_fusion
  12.6 0.8 broadcast_in_dim.70
  13.4 0.1 reshape.149
  13.5 3.0 multiply_sine_fusion
  16.5 1.0 and_select_fusion.bias
  17.5 0.6 select_maximum_fusion.gain_sh
  18.1 1.6 pad_maximum_fusion.seq_sh
  19.7 297.5 %gather_forward.1 = (bf16[1024,1024]{1,0:T(8,128)(2,1)}, bf16[2048,1024]{1,0:T(8,128)(2,1)}, bf16[2048,1408]{1,0:T(8,128)(2,1)}, bf16[2048,1408]{1,0:T(8,128)(2,...) custom-call(bf16[2,128,2048]{2,1,0:T(8,128)(2,1)} %tok.3, ...), custom_call_target="tpu_custom_call" | custom-call | tf_op jit(solution)/shard_map/gather_forward/pallas_call | solution.py:657
  317.3 0.0 copy-start.6
  317.3 0.0 copy-start.7
  317.3 0.0 slice-start.4
  317.3 10.6 %fusion.6 = f32[1024,1408]{1,0:T(8,128)S(1)} fusion(bf16[1024,2048]{1,0:T(8,128)(2,1)} %get-tuple-element.37, bf16[2048,1408]{1,0:T(8,128)(2,1)} %get-tuple-element.39), kind=kOutput, calls=%fused_computation.44 | convolution fusion | flops 5905580032 | bytes 15728640 | tf_op jit(solution)/shard_map/dot_general | solution.py:1338
  327.9 0.0 slice-start.5
  327.9 8.7 %fusion.5 = f32[1024,1408]{1,0:T(8,128)} fusion(bf16[1024,2048]{1,0:T(8,128)(2,1)S(1)} %copy-done.7, bf16[2048,1408]{1,0:T(8,128)(2,1)S(1)} %copy-done.6), kind=kOutput, calls=%fused_computation.43 | convolution fusion | flops 5905580032 | bytes 15728640 | tf_op jit(solution)/shard_map/dot_general | solution.py:1337
  336.6 0.0 slice-done.4
  336.6 11.8 %multiply_convert_fusion = (bf16[1024,1408]{1,0:T(8,128)(2,1)}, bf16[1024,1408]{1,0:T(8,128)(2,1)}, bf16[1024,1408]{1,0:T(8,128)(2,1)S(1)}) fusion(f32[1024,1408]{1,0:T(8,128)} %fusion.5, f32[1024,1408]{1,0:T(8,128)S(1)} %fusion.6, bf16[1024,2048]{1,0:T(8,128)(2,1)S(1)} %copy-done.9, bf16[2048,1408]{1,0:T(8,128)(2,1)S(1)} %bitcast.44), kind=kOutput, calls=%fused_computation.4 | convolution fusion | flops 5928648704 | bytes 30146560 | tf_op jit(solution)/shard_map/dot_general | solution.py:1341
  348.4 1.6 copy-done.12
  350.0 8.3 %convolution_convert_fusion.3 = bf16[1024,2048]{1,0:T(8,128)(2,1)} fusion(bf16[1024,1408]{1,0:T(8,128)(2,1)S(1)} %get-tuple-element.61, bf16[2048,1408]{1,0:T(8,128)(2,1)S(1)} %bitcast.44), kind=kOutput, calls=%fused_computation.8 | convolution fusion | flops 5907677184 | bytes 12845056 | tf_op jit(solution)/shard_map/dot_general | solution.py:57
  358.3 0.0 reduce-scatter.2.cloned.1.call-update
  358.3 0.0 slice-start.3
  358.3 11.6 %convolution_convert_fusion.gw_down = bf16[2048,1408]{1,0:T(8,128)(2,1)} fusion(bf16[1024,2048]{1,0:T(8,128)(2,1)} %get-tuple-element.44, bf16[1024,1408]{1,0:T(8,128)(2,1)} %copy-done.12), kind=kOutput, calls=%fused_computation.1 | convolution fusion | flops 5908463616 | bytes 12845056 | tf_op jit(solution)/shard_map/dot_general | solution.py:61
  370.0 6.7 fusion.7
  376.7 0.0 slice-start
  376.7 8.7 %convolution_convert_fusion.2.gw_gate = bf16[2048,1408]{1,0:T(8,128)(2,1)} fusion(bf16[1024,2048]{1,0:T(8,128)(2,1)S(1)} %copy-done.8, bf16[1024,1408]{1,0:T(8,128)(2,1)S(1)} %copy-done.10), kind=kOutput, calls=%fused_computation.3 | convolution fusion | flops 5908463616 | bytes 12845056 | tf_op jit(solution)/shard_map/dot_general | solution.py:61
  385.4 0.0 copy-done.11
  385.4 8.7 %convolution_convert_fusion.1.gw_up = bf16[2048,1408]{1,0:T(8,128)(2,1)} fusion(bf16[1024,2048]{1,0:T(8,128)(2,1)S(1)} %copy-done.8, bf16[1024,1408]{1,0:T(8,128)(2,1)S(1)} %copy-done.11), kind=kOutput, calls=%fused_computation.2 | convolution fusion | flops 5908463616 | bytes 12845056 | tf_op jit(solution)/shard_map/dot_general | solution.py:61
  394.1 0.0 slice-done
  394.1 8.5 %add_convert_fusion.gnt = bf16[1024,2048]{1,0:T(8,128)(2,1)} fusion(f32[1024,2048]{1,0:T(8,128)S(1)} %fusion.7, bf16[1024,1408]{1,0:T(8,128)(2,1)S(1)} %copy-done.11, bf16[2048,1408]{1,0:T(8,128)(2,1)S(1)} %bitcast.40), kind=kOutput, calls=%fused_computation | convolution fusion | flops 5909774336 | bytes 21233664 | tf_op jit(solution)/shard_map/dot_general | solution.py:57
  402.7 341.8 %backward_scatter.1 = (f32[256,1408]{1,0:T(8,128)}, f32[256,1408]{1,0:T(8,128)}, f32[256,1408]{1,0:T(8,128)}, f32[256,1024]{1,0:T(8,128)}, f32[128,1024]{1,0:T(8...) custom-call(bf16[2,128,2048]{2,1,0:T(8,128)(2,1)} %tok.3, ...), custom_call_target="tpu_custom_call" | custom-call | tf_op jit(solution)/shard_map/backward_scatter/pallas_call | solution.py:1261
  744.4 0.0 copy-start.4
  744.5 0.0 copy-start.3
  744.5 0.9 slice.24
  745.4 0.8 slice_bitcast_fusion
  746.2 0.6 dynamic_slice.14
  746.8 0.6 dynamic_slice.11
  747.4 1.7 slice.23
  749.1 0.6 dynamic-slice_bitcast_fusion
  749.6 1.5 fusion.4
  751.2 3.3 add_convert_fusion.1
  754.4 1.0 copy.39
  755.4 0.8 copy.40
  756.2 0.0 copy-done.3
  756.2 1.0 copy.41
  757.2 0.0 copy-done.2
  757.2 1.1 copy.42
  758.3 1.1 copy.43
  759.4 1.1 copy.44
  (40 shorter events, 0.2 us)
Async XLA Ops:
  7.2 744.0 %reduce-scatter.2.cloned.1.call-start = ((), (), s32[]{:S(2)}) async-start(), calls=%async_computation.1 | async-start | bytes 5242880 | tf_op jit(solution)/shard_map/reduce_scatter | solution.py:1350
  317.3 10.6 %copy-start.6 = (bf16[2048,1408]{1,0:T(8,128)(2,1)S(1)}, bf16[2048,1408]{1,0:T(8,128)(2,1)}, u32[]{:S(2)}) copy-start(bf16[2048,1408]{1,0:T(8,128)(2,1)} %get-tuple-element.38) | copy-start | bytes 17301508
  317.3 10.6 %copy-start.7 = (bf16[1024,2048]{1,0:T(8,128)(2,1)S(1)}, bf16[1024,2048]{1,0:T(8,128)(2,1)}, u32[]{:S(2)}) copy-start(bf16[1024,2048]{1,0:T(8,128)(2,1)} %get-tuple-element.37) | copy-start | bytes 12582916
  317.3 19.3 %slice-start.4 = ((s8[5767168]{0:T(1024)(128)(4,1)}), s8[4194304]{0:T(1024)(128)(4,1)S(1)}, s32[]{:S(2)}) async-start(s8[5767168]{0:T(1024)(128)(4,1)} %bitcast.43), calls=%async_computation.6 | async-start | bytes 8388608
  327.9 8.7 %slice-start.5 = ((s8[5767168]{0:T(1024)(128)(4,1)}), s8[1572864]{0:T(1024)(128)(4,1)S(1)}, s32[]{:S(2)}) async-start(s8[5767168]{0:T(1024)(128)(4,1)} %bitcast.43), calls=%async_computation.7 | async-start | bytes 3145728
  327.9 8.7 %copy-start.9 = (bf16[1024,2048]{1,0:T(8,128)(2,1)S(1)}, bf16[1024,2048]{1,0:T(8,128)(2,1)}, u32[]{:S(2)}) copy-start(bf16[1024,2048]{1,0:T(8,128)(2,1)} %get-tuple-element.44) | copy-start | bytes 12582916
  348.4 1.6 copy-start.12
  358.3 11.6 %slice-start.2 = ((s8[5767168]{0:T(1024)(128)(4,1)}), s8[1572864]{0:T(1024)(128)(4,1)S(1)}, s32[]{:S(2)}) async-start(s8[5767168]{0:T(1024)(128)(4,1)} %bitcast.41), calls=%async_computation.4 | async-start | bytes 3145728
  358.3 11.6 %slice-start.3 = ((s8[5767168]{0:T(1024)(128)(4,1)}), s8[4194304]{0:T(1024)(128)(4,1)S(1)}, s32[]{:S(2)}) async-start(s8[5767168]{0:T(1024)(128)(4,1)} %bitcast.41), calls=%async_computation.5 | async-start | bytes 8388608
  358.3 11.6 %copy-start.10 = (bf16[1024,1408]{1,0:T(8,128)(2,1)S(1)}, bf16[1024,1408]{1,0:T(8,128)(2,1)}, u32[]{:S(2)}) copy-start(bf16[1024,1408]{1,0:T(8,128)(2,1)} %get-tuple-element.60) | copy-start | bytes 8650756
  370.0 6.7 copy-start.8
  376.7 8.7 %copy-start.11 = (bf16[1024,1408]{1,0:T(8,128)(2,1)S(1)}, bf16[1024,1408]{1,0:T(8,128)(2,1)}, u32[]{:S(2)}) copy-start(bf16[1024,1408]{1,0:T(8,128)(2,1)} %get-tuple-element.59) | copy-start | bytes 8650756
  376.7 17.4 %slice-start = ((s8[5767168]{0:T(1024)(128)(4,1)}), s8[4194304]{0:T(1024)(128)(4,1)S(1)}, s32[]{:S(2)}) async-start(s8[5767168]{0:T(1024)(128)(4,1)} %bitcast.39), calls=%async_computation.2 | async-start | bytes 8388608
  385.4 8.7 %slice-start.1 = ((s8[5767168]{0:T(1024)(128)(4,1)}), s8[1572864]{0:T(1024)(128)(4,1)S(1)}, s32[]{:S(2)}) async-start(s8[5767168]{0:T(1024)(128)(4,1)} %bitcast.39), calls=%async_computation.3 | async-start | bytes 3145728
  744.4 10.0 %copy-start.4 = (bf16[2,128,2048]{2,1,0:T(8,128)(2,1)S(1)}, bf16[2,128,2048]{2,1,0:T(8,128)(2,1)}, u32[]{:S(2)}) copy-start(bf16[2,128,2048]{2,1,0:T(8,128)(2,1)} %get-tuple-element.86) | copy-start | bytes 3145732
  744.5 11.8 %copy-start.3 = (f32[256,1024]{1,0:T(8,128)S(1)}, f32[256,1024]{1,0:T(8,128)}, u32[]{:S(2)}) copy-start(f32[256,1024]{1,0:T(8,128)} %get-tuple-element.93) | copy-start | bytes 3145732
  751.2 6.0 copy-start.2
  751.2 4.2 copy-start.5
  754.4 3.9 copy-start.1
  756.2 3.2 copy-start
Sparse Core Ops, SparseCore 0:
  358.4 65.6 reduce-scatter.1

commit v3 on v2

--- a/solution.py
+++ b/solution.py
@@ -18,6 +18,14 @@
 ANY = pl.BlockSpec(memory_space=pl.ANY)
 VMEM = pl.BlockSpec(memory_space=pltpu.VMEM)
 NF = 4
+GATHER_ROWS = 64
+GATHER_AHEAD = 4
+FFN_ROWS = 128
+FFN_COLS = 512
+
+
+def ffn_chunks(cols):
+    return [(c, min(FFN_COLS, cols - c)) for c in range(0, cols, FFN_COLS)]
 
 
 def layout(member_row, block_len):
@@ -64,36 +72,38 @@
 class Place:
     def __init__(self, ndp):
         self.ndp = ndp
-        self.nz = ndp // 2
+        self.bits = [1 << b for b in range(ndp.bit_length() - 1)]
         self.me = lax.axis_index("dp")
         self.f = lax.axis_index("fsdp")
-        self.z = self.me // 2
-        self.x = self.me % 2
-        self.pair = self.z * 2 + 1 - self.x
         y, c = self.f // 2, self.f % 2
         self.f_core = y * 2 + 1 - c
         self.f_y = (1 - y) * 2 + c
         self.f_yc = (1 - y) * 2 + 1 - c
-        self.to_pair = (self.pair, self.f)
         self.to_core = (self.me, self.f_core)
         self.to_y = (self.me, self.f_y)
 
-    def zidx(self, k):
-        return lax.rem(self.z + k + self.nz, self.nz)
-
-    def to_z(self, k):
-        return (self.zidx(k) * 2 + self.x, self.f)
-
-    def barrier(self, fsdp=True):
+    def at(self, mask):
+        j = self.me
+        for b in self.bits:
+            if mask & b:
+                j = j + b - 2 * b * ((self.me // b) % 2)
+        return j
+
+    def to_dp(self, mask):
+        return (self.at(mask), self.f)
+
+    def orders(self, swapped):
+        o = list(self.bits)
+        if swapped and len(o) > 1:
+            o[0], o[1] = o[1], o[0]
+        return o
+
+    def barrier(self):
         bar = pltpu.get_barrier_semaphore()
-        count = self.nz
-        devs = [self.to_pair] + [self.to_z(k) for k in range(1, self.nz)]
-        if fsdp:
-            devs += [self.to_core, self.to_y]
-            count += 2
+        devs = [self.to_dp(b) for b in self.bits] + [self.to_core, self.to_y]
         for d in devs:
             pl.semaphore_signal(bar, inc=1, device_id=d, device_id_type=MESH)
-        pl.semaphore_wait(bar, count)
+        pl.semaphore_wait(bar, len(devs))
 
 
 def rcopy(src, dst, ss, rs, dev):
@@ -103,53 +113,79 @@
 
 
 class DpGather:
-    def __init__(self, pos, items, zs, zr, xs, xr):
-        self.p, self.items = pos, items
-        self.zs, self.zr, self.xs, self.xr = zs, zr, xs, xr
-
-    def zcopy(self, i, k):
-        src, dst = self.items[i]
+    def __init__(self, pos, ss, rs):
+        self.p, self.ss, self.rs = pos, ss, rs
+        self.items, self.events = [], []
+        self.launched = self.seen = 0
+
+    def add(self, src, dst, swapped=False):
+        self.items.append((src, dst, self.p.orders(swapped)[::-1]))
+        return len(self.items) - 1
+
+    def copy(self, n, mask, stage):
+        src, dst, order = self.items[n]
+        j = self.p.at(mask)
+        k = self.index(n, mask | order[stage])
         return rcopy(
-            src, dst(self.p.me), self.zs.at[i, k - 1], self.zr.at[i, k - 1], self.p.to_z(k)
+            src if mask == 0 else dst(j),
+            dst(j),
+            self.ss.at[n, k],
+            self.rs.at[n, k],
+            self.p.to_dp(order[stage]),
         )
 
-    def zarrive(self, i, k):
-        src, dst = self.items[i]
-        j = self.p.zidx(-k) * 2 + self.p.x
-        return rcopy(src, dst(j), self.zs.at[i, k - 1], self.zr.at[i, k - 1], self.p.to_z(-k))
-
-    def xcopy(self, i, k):
-        src, dst = self.items[i]
-        j = self.p.zidx(-k) * 2 + self.p.x
-        return rcopy(
-            src if k == 0 else dst(j), dst(j), self.xs.at[i, k], self.xr.at[i, k], self.p.to_pair
-        )
-
-    def xarrive(self, i, k):
-        src, dst = self.items[i]
-        j = self.p.zidx(-k) * 2 + 1 - self.p.x
-        return rcopy(src, dst(j), self.xs.at[i, k], self.xr.at[i, k], self.p.to_pair)
-
-    def start_z(self, i):
-        for k in range(1, self.p.nz):
-            self.zcopy(i, k).start()
-
-    def start_x(self, i):
-        self.xcopy(i, 0).start()
-
-    def forward(self, i, k):
-        self.zarrive(i, k).wait_recv()
-        self.xcopy(i, k).start()
-
-    def wait_x(self, i):
-        for k in range(self.p.nz):
-            self.xarrive(i, k).wait_recv()
-
-    def wait_sends(self, i):
-        for k in range(self.p.nz):
-            self.xcopy(i, k).wait_send()
-        for k in range(1, self.p.nz):
-            self.zcopy(i, k).wait_send()
+    def index(self, n, mask):
+        return mask - 1
+
+    def stage_of(self, n, mask):
+        return max(i for i, b in enumerate(self.items[n][2]) if mask & b)
+
+    def arrived(self, n, mask):
+        src, dst, order = self.items[n]
+        stage = self.stage_of(n, mask)
+        j = self.p.at(mask)
+        k = self.index(n, mask)
+        rcopy(src, dst(j), self.ss.at[n, k], self.rs.at[n, k], self.p.to_dp(order[stage])).wait_recv()
+
+    def launch(self):
+        if self.launched < len(self.items):
+            n = self.launched
+            for stage in range(len(self.p.bits)):
+                self.copy(n, 0, stage).start()
+            self.launched += 1
+
+    def masks(self, n):
+        order = self.items[n][2]
+        last = order[-1]
+        out = [m for m in range(1, self.p.ndp) if not m & last]
+        return sorted(out, key=lambda m: (self.stage_of(n, m), m))
+
+    def forward(self, n):
+        for m in self.masks(n):
+            self.arrived(n, m)
+            for stage in range(self.stage_of(n, m) + 1, len(self.p.bits)):
+                self.copy(n, m, stage).start()
+
+    def steps(self, count, ahead):
+        for _ in range(count):
+            if self.seen >= len(self.items):
+                return
+            while self.launched < min(len(self.items), self.seen + ahead):
+                self.launch()
+            self.forward(self.seen)
+            self.seen += 1
+
+    def wait_last(self, n):
+        last = self.items[n][2][-1]
+        for m in range(self.p.ndp):
+            if m & last:
+                self.arrived(n, m)
+
+    def wait_sends(self, n):
+        for m in range(self.p.ndp):
+            first = 0 if m == 0 else self.stage_of(n, m) + 1
+            for stage in range(first, len(self.p.bits)):
+                self.copy(n, m, stage).wait_send()
 
 
 class FsGather:
@@ -279,8 +315,12 @@
     latent_o,
     normed_o,
     middle_o,
-    n2_o,
-    d_o,
+    hid_o,
+    gg_o,
+    gu_o,
+    gw_gate,
+    gw_up,
+    gw_down,
     seq_v,
     gain_v,
     qb_v,
@@ -293,49 +333,53 @@
     fy_v,
     n2_v,
     d_v,
+    n2_t,
+    d_t,
     lat_v,
-    zs,
-    zr,
-    xs,
-    xr,
+    gss,
+    grs,
     fss,
     frs,
     sys_,
     syr,
     ls,
+    ffn_ls,
 ):
     ndp, own, dim, rank, hd, heads = cfg
     rows = NF * own
     p = Place(ndp)
     kvw = rank + 2 * hd
     sr = seq_sh.shape[0]
-    items = []
-
-    def add_item(src, dst):
-        items.append((src, dst))
-        return len(items) - 1
-
-    i_seq = add_item(seq_sh, lambda j: seq_v.at[pl.ds(al((j * NF + p.f) * sr, sr), sr)])
-    i_gain = add_item(gain_sh, lambda j: gain_v.at[j * NF + p.f])
-
-    def weight_items(src, dst, pieces):
+    g = DpGather(p, gss, grs)
+    i_seq = g.add(seq_sh, lambda j: seq_v.at[pl.ds(al((j * NF + p.f) * sr, sr), sr)])
+    i_gain = g.add(gain_sh, lambda j: gain_v.at[j * NF + p.f])
+    turn = [0]
+
+    def weight_items(src, dst, cols=slice(None), most=GATHER_ROWS):
         n = src.shape[0]
-        step = n // pieces
-        return [
-            add_item(
-                src.at[pl.ds(c * step, step)],
-                lambda j, c=c: dst.at[pl.ds(al(j * n + c * step, step), step)],
+        step = min(n, most)
+        out = []
+        for c in range(n // step):
+            turn[0] += 1
+            out.append(
+                g.add(
+                    src.at[pl.ds(c * step, step), cols],
+                    lambda j, c=c: dst.at[pl.ds(al(j * n + c * step, step), step), cols],
+                    turn[0] % 4 == 0,
+                )
             )
-            for c in range(pieces)
-        ]
-
-    i_qb = weight_items(qb_sh, qb_v, 1)
-    i_out = weight_items(out_sh, out_v, 2)
+        return out
+
+    i_qb = weight_items(qb_sh, qb_v)
+    i_out = weight_items(out_sh, out_v)
     i_ffn = []
-    for s, d in ((gate_sh, gate_all), (up_sh, up_all), (down_sh, down_all)):
-        i_ffn += weight_items(s, d, 2)
-    order = [i_seq, i_gain] + i_qb + i_out + i_ffn
-    g = DpGather(p, items, zs, zr, xs, xr)
+    for c0, cw in ffn_chunks(gate_sh.shape[1]):
+        cols = pl.ds(c0, cw)
+        some = []
+        for s, d in ((gate_sh, gate_all), (up_sh, up_all), (down_sh, down_all)):
+            some += weight_items(s, d, cols, FFN_ROWS)
+        i_ffn.append(some)
+    order = range(len(g.items))
     fs_d = FsGather(p, lambda b: d_v.at[pl.ds(al(b * own, own), own)], fss.at[0], frs.at[0])
     fs_l = FsGather(p, lambda b: lkv_v.at[pl.ds(al(b * own, own), own)], fss.at[1], frs.at[1])
     fs_n = FsGather(p, lambda b: n2_v.at[pl.ds(al(b * own, own), own)], fss.at[2], frs.at[2])
@@ -353,7 +397,7 @@
 
     own_copies = {}
     for i in order:
-        src, dst = items[i]
+        src, dst, _ = g.items[i]
         own_copies[i] = local_copy(src, dst(p.me))
     d_copies = [
         local_copy(dout.at[m], d_v.at[pl.ds(al(p.f * own + m * (own // 2), 128), own // 2)])
@@ -361,19 +405,8 @@
     ]
 
     p.barrier()
-    g.start_x(i_seq)
-    g.start_x(i_gain)
-    g.start_x(i_qb[0])
-    zahead = 4
-    for i in order[:zahead]:
-        g.start_z(i)
-    zlead = [zahead]
-
-    def more_z():
-        if zlead[0] < len(order):
-            g.start_z(order[zlead[0]])
-            zlead[0] += 1
-
+    for _ in range(GATHER_AHEAD):
+        g.launch()
     npiece = ndp
 
     def seq_piece(j, fb):
@@ -395,23 +428,13 @@
     own_copies[i_seq].wait()
     own_copies[i_gain].wait()
     spread(p.me)
-    queue = order[2:]
-    lead = [1]
-
-    def more_x():
-        if lead[0] < len(queue):
-            g.start_x(queue[lead[0]])
-            lead[0] += 1
-
-    for k in range(1, p.nz):
+    for m in sorted(range(1, ndp), key=lambda m: g.stage_of(i_seq, m)):
         for i in (i_seq, i_gain):
-            g.forward(i, k)
-        spread(p.zidx(-k) * 2 + p.x)
-    more_x()
-    for k in range(p.nz):
-        for i in (i_seq, i_gain):
-            g.xarrive(i, k).wait_recv()
-        spread(p.zidx(-k) * 2 + 1 - p.x)
+            g.arrived(i, m)
+            for stage in range(g.stage_of(i, m) + 1, len(p.bits)):
+                g.copy(i, m, stage).start()
+        spread(p.at(m))
+    g.seen = 2
     for c in d_copies:
         c.wait()
 
@@ -421,25 +444,13 @@
             seq_copy(2, j, p.f_y, p.to_core, which).start()
         return 0
 
-    events = [(i, k) for i in queue for k in range(1, p.nz)]
-    done = [0]
-
     def tick(n):
-        for _ in range(n):
-            if done[0] >= len(events):
-                return
-            i, k = events[done[0]]
-            if k == 1:
-                more_x()
-            g.forward(i, k)
-            if k == p.nz - 1:
-                more_z()
-            done[0] += 1
-
-    tick(p.nz - 1)
+        g.steps(n, GATHER_AHEAD)
+
+    tick(1)
     lax.fori_loop(0, npiece, spread_forward, 0)
     fs_d.start()
-    tick(p.nz - 1)
+    tick(1)
 
     def spread_end(j, _):
         for which in (0, 1):
@@ -479,13 +490,13 @@
     lkv_v[own_rows, rank + half : rank + hd] = (kb * co + ka * si).astype(BF16)
     lkv_v[own_rows, rank + hd :] = lat_v[:, rank + hd :].astype(BF16)
     fs_l.start()
-    tick(p.nz - 1)
+    tick(1)
     fs_d.mid()
     fs_l.mid()
-    tick(p.nz - 1)
+    tick(1)
     for i in i_qb:
         own_copies[i].wait()
-        g.wait_x(i)
+        g.wait_last(i)
     fs_l.end()
     qb_out = local_copy(qb_v, qb_all)
     lkv_out = local_copy(lkv_v, lkv_o)
@@ -534,12 +545,11 @@
         lax.fori_loop(0, heads, attend, 0)
         tick(2)
     fs_d.end()
-    d_out = local_copy(d_v, d_o)
     mixed_out = local_copy(mixed_v, mixed_o)
     tick(1)
     for i in i_out:
         own_copies[i].wait()
-        g.wait_x(i)
+        g.wait_last(i)
     out_out = local_copy(out_v, out_all)
 
     def project_out(fb):
@@ -570,16 +580,29 @@
             mid * inv * gain_two
         ).astype(BF16)
     fs_n.start()
-    tick(4)
+    tick(1)
+
+    def turn_d(j, _):
+        cols = pl.ds(al(j * 256, 256), 256)
+        d_t[cols, :] = d_v[:, cols].T
+        return 0
+
+    lax.fori_loop(0, dim // 256, turn_d, 0)
+    tick(1)
     fs_n.mid()
     tick(1)
     fs_n.end()
-    n2_out = local_copy(n2_v, n2_o)
-    tick(len(events))
-    for i in i_ffn:
-        own_copies[i].wait()
-        g.wait_x(i)
-    for i in order:
+
+    def turn_n2(j, _):
+        cols = pl.ds(al(j * 256, 256), 256)
+        n2_t[cols, :] = n2_v[:, cols].T
+        return 0
+
+    lax.fori_loop(0, dim // 256, turn_n2, 0)
+    for c in (q_out, mixed_out, out_out, seq_out):
+        c.wait()
+    early = [i_seq, i_gain] + i_qb + i_out
+    for i in early:
         g.wait_sends(i)
 
     def spread_sends(j, _):
@@ -590,9 +613,91 @@
         return 0
 
     lax.fori_loop(0, npiece, spread_sends, 0)
-    for t in (fs_d, fs_l, fs_n, red):
+    red.wait_sends()
+    pending = []
+    width = FFN_COLS
+    for (c0, cw), some in zip(ffn_chunks(gate_sh.shape[1]), i_ffn):
+        tick(some[-1] + 1 - g.seen)
+        for i in some:
+            own_copies[i].wait()
+            g.wait_last(i)
+        cols = pl.ds(c0, cw)
+        loads = [
+            pltpu.make_async_copy(w.at[:, cols], seq_v.at[:, pl.ds(n * width, cw)], ffn_ls.at[n])
+            for n, w in enumerate((gate_all, up_all, down_all))
+        ]
+        for c in loads:
+            c.start()
+        for c in pending:
+            c.wait()
+        for c in loads:
+            c.wait()
+        gate_c, up_c, down_c = (slice(n * width, n * width + cw) for n in range(3))
+
+        def both(t, _):
+            rr = pl.ds(al(t * 256, 256), 256)
+            gate = mm(n2_v[rr, :], seq_v[:, gate_c])
+            up = mm(n2_v[rr, :], seq_v[:, up_c])
+            grad_hidden = mm(d_v[rr, :], seq_v[:, down_c])
+            sig = 1.0 / (1.0 + jnp.exp(-gate))
+            act = gate * sig
+            mixed_v[rr, :cw] = (act * up).astype(BF16)
+            q_v[rr, gate_c] = (grad_hidden * up * (sig * (1.0 + gate * (1.0 - sig)))).astype(BF16)
+            q_v[rr, up_c] = (grad_hidden * act).astype(BF16)
+            return 0
+
+        lax.fori_loop(0, rows // 256, both, 0)
+        pending = [
+            pltpu.make_async_copy(src, dst.at[:, cols], ffn_ls.at[3 + n])
+            for n, (src, dst) in enumerate(
+                (
+                    (mixed_v.at[:, pl.ds(0, cw)], hid_o),
+                    (q_v.at[:, pl.ds(0, cw)], gg_o),
+                    (q_v.at[:, pl.ds(width, cw)], gu_o),
+                )
+            )
+        ]
+        for c in pending:
+            c.start()
+
+        half_rows = part_v.shape[0] // 256
+        for lo in range(0, dim // 256, half_rows):
+
+            def weight_grads(j, _):
+                rr = pl.ds(al(j * 256, 256), 256)
+                pr = pl.ds(al((j - lo) * 256, 256), 256)
+                pc = slice((lo // half_rows) * width, (lo // half_rows) * width + cw)
+                out_v[rr, gate_c] = mm(n2_t[rr, :], q_v[:, gate_c]).astype(BF16)
+                out_v[rr, up_c] = mm(n2_t[rr, :], q_v[:, up_c]).astype(BF16)
+                part_v[pr, pc] = mm(d_t[rr, :], mixed_v[:, :cw]).astype(BF16)
+                return 0
+
+            lax.fori_loop(lo, min(dim // 256, lo + half_rows), weight_grads, 0)
+        saves = [
+            pltpu.make_async_copy(out_v.at[:, pl.ds(0, cw)], gw_gate.at[:, cols], ffn_ls.at[6]),
+            pltpu.make_async_copy(out_v.at[:, pl.ds(width, cw)], gw_up.at[:, cols], ffn_ls.at[7]),
+        ]
+        prow = part_v.shape[0]
+        for n in range(dim // prow):
+            saves.append(
+                pltpu.make_async_copy(
+                    part_v.at[:, pl.ds(n * width, cw)],
+                    gw_down.at[pl.ds(n * prow, prow), cols],
+                    ffn_ls.at[8 + n],
+                )
+            )
+        for c in saves:
+            c.start()
+        pending = pending + saves
+    for c in pending:
+        c.wait()
+    tick(len(g.items))
+    for i in order:
+        if i not in early:
+            g.wait_sends(i)
+    for t in (fs_d, fs_l, fs_n):
         t.wait_sends()
-    for c in (seq_out, qb_out, lkv_out, q_out, d_out, mixed_out, out_out, n2_out):
+    for c in (qb_out, lkv_out):
         c.wait()
 
 
@@ -604,8 +709,10 @@
     heads = qb.shape[1] // hd
     rows = NF * own
     kvw = seq_sh.shape[1]
-    nz = ndp // 2
-    n_items = 2 + 1 + 2 + 6
+    n_items = 2 + sum(w.shape[0] // min(w.shape[0], GATHER_ROWS) for w in (qb, out))
+    n_items += sum(w.shape[0] // min(w.shape[0], FFN_ROWS) for w in (gate, up, down)) * len(
+        ffn_chunks(gate.shape[1])
+    )
 
     def sds(shape, dtype=BF16):
         return jax.ShapeDtypeStruct(shape, dtype)
@@ -625,10 +732,14 @@
         sds((own, rank), F32),
         sds((own, dim)),
         sds((own, dim), F32),
-        sds((rows, dim)),
-        sds((rows, dim)),
+        sds((rows, gate.shape[1])),
+        sds((rows, gate.shape[1])),
+        sds((rows, gate.shape[1])),
+        full(gate),
+        full(up),
+        full(down),
     )
-    out_specs = (ANY,) * 6 + (VMEM,) + (ANY,) * 3 + (VMEM,) * 3 + (ANY,) * 2
+    out_specs = (ANY,) * 6 + (VMEM,) + (ANY,) * 3 + (VMEM,) * 3 + (ANY,) * 6
     dma = pltpu.SemaphoreType.DMA
     scratch = [
         pltpu.VMEM((seq_sh.shape[0] * ndp * NF, kvw), BF16),
@@ -643,16 +754,17 @@
         pltpu.VMEM((own, dim), BF16),
         pltpu.VMEM((rows, dim), BF16),
         pltpu.VMEM((rows, dim), BF16),
+        pltpu.VMEM((dim, rows), BF16),
+        pltpu.VMEM((dim, rows), BF16),
         pltpu.VMEM((own, kvw), F32),
-        dma((n_items, nz - 1)),
-        dma((n_items, nz - 1)),
-        dma((n_items, nz)),
-        dma((n_items, nz)),
+        dma((n_items, ndp - 1)),
+        dma((n_items, ndp - 1)),
         dma((4, 3)),
         dma((4, 3)),
         dma((2, 3, ndp)),
         dma((2, 3, ndp)),
         dma((n_items + 10,)),
+        dma((10,)),
     ]
     return pl.pallas_call(
         functools.partial(forward_kernel, (ndp, own, dim, rank, hd, heads)),
@@ -668,74 +780,112 @@
 
 
 class DpScatter:
-    SLOTS = 4
+    SLOTS = 5
     AHEAD = 2
-
-    def __init__(self, pos, count, xbuf, zbuf, own, acc, xs, xr, zs, zr, ls, xcredit, zcredit):
+    OWN = 3
+
+    def __init__(self, pos, count, first, later, own, acc, ss, rs, ls, credit):
         self.p, self.count = pos, count
-        self.xbuf, self.zbuf, self.own, self.acc = xbuf, zbuf, own, acc
-        self.xs, self.xr, self.zs, self.zr, self.ls = xs, xr, zs, zr, ls
-        self.xcredit, self.zcredit = xcredit, zcredit
+        self.n = len(pos.bits)
+        self.first, self.later, self.own, self.acc = first, later, own, acc
+        self.ss, self.rs, self.ls, self.credit = ss, rs, ls, credit
         self.items = []
         self.started = self.stepped = 0
 
-    def add(self, src, base, in_vmem, out, pieces):
+    def order(self, n):
+        return self.p.orders(n % 4 == 3)
+
+    def width(self, stage):
+        return 1 << (self.n - 1 - stage)
+
+    def add(self, src, base, out, pieces):
         rows, cols = out.shape
         r = rows // pieces
         for c in range(pieces):
-            self.items.append((src, base, in_vmem, out, rows, cols, c * r, r))
+            self.items.append((src, base, out, rows, cols, c * r, r))
         self.pump()
 
-    def block(self, n, j, x):
-        src, base, in_vmem, out, rows, cols, r0, r = self.items[n]
-        return src.at[pl.ds(al(base + (j * 2 + x) * rows + r0, r), r)]
-
-    def slot(self, buf, n):
-        src, base, in_vmem, out, rows, cols, r0, r = self.items[n]
-        return buf.at[n % self.SLOTS, :, pl.ds(0, r), pl.ds(0, cols)]
-
-    def xcopy(self, n, j):
-        return rcopy(
-            self.block(n, j, 1 - self.p.x),
-            self.slot(self.xbuf, n).at[j],
-            self.xs.at[n % self.SLOTS, j],
-            self.xr.at[n % self.SLOTS, j],
-            self.p.to_pair,
+    def mask(self, n, i):
+        order = self.order(n)
+        return sum(order[1 + t] for t in range(self.n - 1) if i >> (self.n - 2 - t) & 1)
+
+    def block(self, n, mask):
+        src, base, out, rows, cols, r0, r = self.items[n]
+        return src.at[pl.ds(al(base + self.p.at(mask) * rows + r0, r), r)]
+
+    def place(self, buf, n, lo, size):
+        src, base, out, rows, cols, r0, r = self.items[n]
+        return buf.at[n % self.SLOTS, pl.ds(lo, size), pl.ds(0, r), pl.ds(0, cols)]
+
+    def copies(self, n, stage):
+        bit = self.order(n)[stage]
+        dev = self.p.to_dp(bit)
+        s = n % self.SLOTS
+        if stage == 0:
+            return [
+                rcopy(
+                    self.block(n, bit | self.mask(n, i)),
+                    self.place(self.first, n, i, 1).at[0],
+                    self.ss.at[s, i],
+                    self.rs.at[s, i],
+                    dev,
+                )
+                for i in range(self.width(0))
+            ]
+        w = self.width(stage)
+        k = self.width(0) + stage - 1
+        return [
+            rcopy(
+                self.place(self.first, n, w, w),
+                self.place(self.later, n, w - 1, w),
+                self.ss.at[s, k],
+                self.rs.at[s, k],
+                dev,
+            )
+        ]
+
+    def owncopy(self, n, i):
+        src, base, out, rows, cols, r0, r = self.items[n]
+        s = n % self.OWN
+        return pltpu.make_async_copy(
+            self.block(n, self.mask(n, i)),
+            self.own.at[s, i, pl.ds(0, r), pl.ds(0, cols)],
+            self.ls.at[s, i],
         )
 
-    def owncopy(self, n, j):
+    def outcopy(self, n):
+        src, base, out, rows, cols, r0, r = self.items[n]
+        s = n % self.SLOTS
         return pltpu.make_async_copy(
-            self.block(n, j, self.p.x), self.slot(self.own, n).at[j], self.ls.at[n % self.SLOTS, j]
+            self.acc.at[s, pl.ds(0, r), pl.ds(0, cols)],
+            out.at[pl.ds(r0, r)],
+            self.ls.at[s, self.width(0)],
         )
 
-    def zcopy(self, n, k):
-        return rcopy(
-            self.slot(self.xbuf, n).at[self.p.zidx(k)],
-            self.slot(self.zbuf, n).at[k - 1],
-            self.zs.at[n % self.SLOTS, k - 1],
-            self.zr.at[n % self.SLOTS, k - 1],
-            self.p.to_z(k),
-        )
-
-    def outcopy(self, n):
-        src, base, in_vmem, out, rows, cols, r0, r = self.items[n]
-        return pltpu.make_async_copy(
-            self.acc.at[n % self.SLOTS, pl.ds(0, r), pl.ds(0, cols)],
-            out.at[pl.ds(r0, r)],
-            self.ls.at[n % self.SLOTS, self.p.nz],
-        )
+    def free(self, n, stage):
+        m = n + self.SLOTS
+        if m < self.count:
+            bit = self.order(m)[stage]
+            pl.semaphore_signal(
+                self.credit.at[stage, self.p.bits.index(bit)],
+                inc=1,
+                device_id=self.p.to_dp(bit),
+                device_id_type=MESH,
+            )
+
+    def send(self, n, stage):
+        bit = self.order(n)[stage]
+        if n >= self.SLOTS:
+            pl.semaphore_wait(self.credit.at[stage, self.p.bits.index(bit)], 1)
+        for c in self.copies(n, stage):
+            c.start()
 
     def pump(self):
         while self.started < min(len(self.items), self.stepped + self.AHEAD):
             n = self.started
-            if n >= self.SLOTS:
-                pl.semaphore_wait(self.xcredit, 1)
-                for j in range(self.p.nz):
-                    self.xcopy(n - self.SLOTS, j).wait_send()
-            for j in range(self.p.nz):
-                self.xcopy(n, j).start()
-            for j in range(self.p.nz):
-                self.owncopy(n, j).start()
+            self.send(n, 0)
+            for i in range(self.width(0)):
+                self.owncopy(n, i).start()
             self.started += 1
 
     def tick(self, steps=1):
@@ -743,86 +893,64 @@
             n = self.stepped
             if n >= self.started:
                 return
-            self.combine(n)
-            if n >= 1:
-                for k in range(1, self.p.nz):
-                    self.zcopy(n - 1, k).wait_send()
-                if n - 1 + self.SLOTS < self.count:
-                    pl.semaphore_signal(
-                        self.xcredit, inc=1, device_id=self.p.to_pair, device_id_type=MESH
-                    )
+            self.combine(n, 0)
             self.stepped += 1
             self.pump()
-            if n >= 2:
-                self.finish(n - 2)
-
-    def combine(self, n):
-        src, base, in_vmem, out, rows, cols, r0, r = self.items[n]
-        p, s = self.p, n % self.SLOTS
-        tile = 16
-        for j in range(p.nz):
-            self.xcopy(n, j).wait_recv()
-        for j in range(p.nz):
-            self.owncopy(n, j).wait()
-        for k in range(1, p.nz):
-            j = p.zidx(k)
-
-            def add(t, _):
+            for stage in range(1, self.n):
+                if n >= stage:
+                    self.combine(n - stage, stage)
+
+    def combine(self, n, stage):
+        src, base, out, rows, cols, r0, r = self.items[n]
+        s, tile = n % self.SLOTS, 16
+        w = self.width(stage)
+        for c in self.copies(n, stage):
+            c.wait_recv()
+        if stage == 0:
+            for i in range(w):
+                self.owncopy(n, i).wait()
+        else:
+            for c in self.copies(n, stage):
+                c.wait_send()
+        last = stage == self.n - 1
+
+        def add(lo, size):
+            def one(t, _):
                 t = pl.ds(al(t * tile, tile), tile)
-                self.xbuf[s, j, t, :cols] = self.xbuf[s, j, t, :cols] + self.own[s, j, t, :cols]
+                for i in range(lo, lo + size):
+                    a = self.first[s, i, t, :cols]
+                    b = self.own[n % self.OWN, i, t, :cols] if stage == 0 else self.later[s, w - 1 + i, t, :cols]
+                    if last:
+                        self.acc[s, t, :cols] = a.astype(F32) + b.astype(F32)
+                    else:
+                        self.first[s, i, t, :cols] = a + b
                 return 0
 
-            lax.fori_loop(0, r // tile, add, 0)
+            lax.fori_loop(0, r // tile, one, 0)
+
+        if last:
             if n >= self.SLOTS:
-                pl.semaphore_wait(self.zcredit.at[k - 1], 1)
-            self.zcopy(n, k).start()
-        if n >= self.SLOTS:
-            self.outcopy(n - self.SLOTS).wait()
-
-        def keep(t, _):
-            t = pl.ds(al(t * tile, tile), tile)
-            self.acc[s, t, :cols] = self.xbuf[s, p.z, t, :cols].astype(F32) + self.own[
-                s, p.z, t, :cols
-            ].astype(F32)
-            return 0
-
-        lax.fori_loop(0, r // tile, keep, 0)
-
-    def finish(self, n):
-        src, base, in_vmem, out, rows, cols, r0, r = self.items[n]
-        p, s = self.p, n % self.SLOTS
-        for k in range(1, p.nz):
-            self.zcopy(n, k).wait_recv()
-        tile = 16
-
-        def add(t, _):
-            t = pl.ds(al(t * tile, tile), tile)
-            total = self.acc[s, t, :cols]
-            for k in range(p.nz - 1):
-                total = total + self.zbuf[s, k, t, :cols].astype(F32)
-            self.acc[s, t, :cols] = total
-            return 0
-
-        lax.fori_loop(0, r // tile, add, 0)
-        self.outcopy(n).start()
-        if n + self.SLOTS < self.count:
-            for k in range(1, p.nz):
-                pl.semaphore_signal(
-                    self.zcredit.at[k - 1], inc=1, device_id=p.to_z(-k), device_id_type=MESH
-                )
+                self.outcopy(n - self.SLOTS).wait()
+            for c in self.copies(n, 0):
+                c.wait_send()
+            add(0, 1)
+            self.outcopy(n).start()
+            for t in range(self.n):
+                self.free(n, t)
+        else:
+            half = w // 2
+            add(half, half)
+            self.send(n, stage + 1)
+            add(0, half)
 
     def drain(self):
         self.tick(self.count)
-        last = self.count - 1
-        for k in range(1, self.p.nz):
-            self.zcopy(last, k).wait_send()
-        self.finish(last - 1)
-        self.finish(last)
+        for n in range(self.count, self.count + self.n - 1):
+            for stage in range(1, self.n):
+                if 0 <= n - stage < self.count:
+                    self.combine(n - stage, stage)
         for n in range(max(0, self.count - self.SLOTS), self.count):
             self.outcopy(n).wait()
-        for n in range(max(0, self.count - self.SLOTS), self.count):
-            for j in range(self.p.nz):
-                self.xcopy(n, j).wait_send()
 
 
 def piece_rows(rows, nz):
@@ -843,7 +971,12 @@
     gw_gate,
     gw_up,
     gw_down,
-    gnt,
+    hid_h,
+    gg_h,
+    gu_h,
+    gate_h,
+    up_h,
+    down_h,
     lkv_h,
     q_h,
     mixed_h,
@@ -858,7 +991,7 @@
     o_seq,
     o_gain,
     o_in,
-    gnt_v,
+    o_y,
     fcore_v,
     fy_v,
     proj_v,
@@ -872,26 +1005,23 @@
     qb_v,
     out_v,
     seq_v,
-    seqy_v,
     gall_v,
     gain_rx,
     gain_acc,
-    xbuf,
-    zbuf,
+    first_b,
+    later_b,
     own_b,
     acc_b,
-    xs,
-    xr,
-    zs,
-    zr,
+    dss,
+    drs,
     dls,
-    xcredit,
-    zcredit,
+    credit,
     fss,
     frs,
     gs,
     gr,
     ls,
+    tls,
 ):
     ndp, own, dim, rank, hd, heads, pieces = cfg
     rows = NF * own
@@ -899,7 +1029,6 @@
     kvw = rank + 2 * hd
     wide = dim // rank
     p = Place(ndp)
-    nz = p.nz
     sr = o_seq.shape[0]
     local = []
 
@@ -909,48 +1038,88 @@
         local.append(c)
         return c
 
-    gnt_own = local_copy(gnt.at[pl.ds(al(p.f * own, own), own)], gnt_v.at[0])
-    gnt_y = local_copy(gnt.at[pl.ds(al(p.f_y * own, own), own)], gnt_v.at[1])
-    out_in = local_copy(out_h, out_v)
+    ff = gg_h.shape[1]
+    ffc = pl.ds(0, ff)
+    gg_in = local_copy(gg_h, lkv_v.at[:, ffc])
+    gu_in = local_copy(gu_h, seq_v.at[pl.ds(0, rows), ffc])
     mixed_in = local_copy(mixed_h, mixed_v)
     q_in = local_copy(q_h, q_v)
+    qb_in = local_copy(qb_h, qb_v)
+    hh = out_v.shape[1]
+
+    def tile_load(t, which):
+        src = gate_h if which == 0 else up_h
+        s = lax.rem(t, 2) * 2 + which
+        return pltpu.make_async_copy(
+            src.at[pl.ds(al(t * 256, 256), 256)],
+            seq_v.at[pl.ds(al(rows + s * 256, 256), 256), ffc],
+            tls.at[s],
+        )
+
+    for which in (0, 1):
+        tile_load(0, which).start()
+    sc = DpScatter(p, sum(pieces), first_b, later_b, own_b, acc_b, dss, drs, dls, credit)
+    p.barrier()
+    sc.add(gw_gate, 0, o_gate, pieces[0])
+    sc.add(gw_up, 0, o_up, pieces[1])
+    sc.add(gw_down, 0, o_down, pieces[2])
+    gg_in.wait()
+    gu_in.wait()
+    n_tiles = dim // 256
+    per_half = hh // 256
+
+    def norm_grad(t, _):
+        for which in (0, 1):
+            tile_load(t, which).wait()
+
+        @pl.when(t + 1 < n_tiles)
+        def _():
+            for which in (0, 1):
+                tile_load(t + 1, which).start()
+
+        s = lax.rem(t, 2) * 2
+        wg = seq_v[pl.ds(al(rows + s * 256, 256), 256), ffc]
+        wu = seq_v[pl.ds(al(rows + s * 256 + 256, 256), 256), ffc]
+        cols = pl.ds(al(lax.rem(t, per_half) * 256, 256), 256)
+        for r in range(rows // 256):
+            rr = pl.ds(r * 256, 256)
+            to = pl.ds(al((t // per_half) * rows + r * 256, 256), 256)
+            out_v[to, cols] = (
+                mm_nt(lkv_v[rr, ffc], wg) + mm_nt(seq_v[rr, ffc], wu)
+            ).astype(BF16)
+        return 0
+
+    halves = []
+    for h in range(dim // hh):
+        wide_cols = pl.ds(h * hh, hh)
+        lax.fori_loop(h * per_half, (h + 1) * per_half, norm_grad, 0)
+        red = FsReduce(
+            p,
+            lambda b, h=h: out_v.at[pl.ds(al(h * rows + b * own, own), own)],
+            fcore_v.at[:, :, wide_cols],
+            fy_v.at[:, wide_cols],
+            fss.at[4 * h],
+            frs.at[4 * h],
+        )
+        red.start()
+        if h > 0:
+            halves[-1].mid(own)
+        sc.tick(1)
+        halves.append(red)
     lkv_in = local_copy(lkv_h, lkv_v)
-    qb_in = local_copy(qb_h, qb_v)
     seq_in = local_copy(seq_h, seq_v)
-    sc = DpScatter(
-        p, sum(pieces), xbuf, zbuf, own_b, acc_b, xs, xr, zs, zr, dls, xcredit, zcredit
-    )
-    p.barrier()
-
-    def gnt_block(b):
-        return gnt.at[pl.ds(al(b * own, own), own)]
-
-    red1 = FsReduce(p, gnt_block, fcore_v, fy_v, fss.at[0], frs.at[0])
-    red1.start()
-    sc.add(gw_gate, 0, False, o_gate, pieces[0])
-    sc.add(gw_up, 0, False, o_up, pieces[1])
-    sc.add(gw_down, 0, False, o_down, pieces[2])
-    gnt_y.wait()
-    gnt_own.wait()
-    red1.c1().wait_recv()
-
-    def add_y(t, _):
-        r = pl.ds(al(t * 64, 64), 64)
-        fcore_v[1, r, :] = fcore_v[1, r, :] + gnt_v[1, r, :]
-        return 0
-
-    lax.fori_loop(0, own // 64, add_y, 0)
-    red1.cy().start()
+    halves[-1].mid(own)
     sc.tick(1)
-    red1.end()
-    red1.wait_sends()
+    for red in halves:
+        red.end()
+        red.wait_sends()
     gain_two = jnp.concatenate([gains[wide + r : wide + r + 1] for r in range(wide)], axis=1)
     gain_one = jnp.concatenate([gains[r : r + 1] for r in range(wide)], axis=1)
     gain_lat = gains[2 * wide : 2 * wide + 1]
     part_two = jnp.zeros((1, dim), F32)
     for m in range(2):
         rr = pl.ds(m * t2, t2)
-        e = gnt_v[0, rr, :].astype(F32) + fcore_v[0, rr, :].astype(F32) + fy_v[rr, :].astype(F32)
+        e = jnp.concatenate([red.value(rr) for red in halves], axis=1)
         v = middle[rr, :]
         inv = lax.rsqrt(jnp.mean(v * v, axis=-1, keepdims=True) + EPSILON)
         part_two += jnp.sum(e * v * inv, axis=0, keepdims=True)
@@ -959,6 +1128,7 @@
         g = dout[m].astype(F32) + inv * scaled - v * (inv * inv * inv * inner)
         gmid_v[rr, :] = g
         proj_v[pl.ds(al(p.f * own + m * t2, t2), t2), :] = g.astype(BF16)
+    out_in = local_copy(out_h, out_v)
     gain_acc[0] = jnp.zeros(gain_acc.shape[1:], F32)
     for r in range(wide):
         gain_acc[0, pl.ds(wide + r, 1), :] = part_two[:, r * rank : (r + 1) * rank]
@@ -989,7 +1159,7 @@
 
     lax.fori_loop(0, dim // 256, grad_out, 0)
     sc.tick(1)
-    sc.add(out_v, 0, True, o_out, pieces[3])
+    sc.add(out_v, 0, o_out, pieces[3])
     q_in.wait()
     lkv_in.wait()
     scale = hd ** (-0.5)
@@ -1079,10 +1249,11 @@
     )
     red2.start()
     sc.tick(1)
-    sc.add(qb_v, 0, True, o_qb, pieces[4])
+    sc.add(qb_v, 0, o_qb, pieces[4])
     red2.mid(own)
     sc.tick(1)
     red2.end()
+    red2.wait_sends()
     own_rows = pl.ds(al(p.f * own, own), own)
     part_lat = jnp.zeros((1, rank), F32)
     for m in range(2):
@@ -1132,7 +1303,23 @@
 
     c1 = rcopy(sblock(p.f_yc), core3[1], fss.at[3, 1], frs.at[3, 1], p.to_core)
     c0 = rcopy(sblock(p.f_core), core3[0], fss.at[3, 0], frs.at[3, 0], p.to_core)
-    cy = rcopy(core3[1], seqy_v, fss.at[3, 2], frs.at[3, 2], p.to_y)
+    mw = mixed_v.shape[1]
+    cys = [
+        rcopy(
+            lkv_v.at[pl.ds(srows, srows), pl.ds(0, mw)],
+            mixed_v.at[pl.ds(0, srows)],
+            fss.at[3, 2],
+            frs.at[3, 2],
+            p.to_y,
+        ),
+        rcopy(
+            lkv_v.at[pl.ds(srows, srows), pl.ds(mw, kvw - mw)],
+            mixed_v.at[pl.ds(srows, srows), pl.ds(0, kvw - mw)],
+            fss.at[3, 3],
+            frs.at[3, 3],
+            p.to_y,
+        ),
+    ]
     c1.start()
     c0.start()
     part_one = jnp.zeros((1, dim), F32)
@@ -1150,10 +1337,9 @@
     gain_steps = [
         rcopy(gain_acc.at[0], gain_rx.at[0], gs.at[0], gr.at[0], p.to_core),
         rcopy(gain_acc.at[1], gain_rx.at[1], gs.at[1], gr.at[1], p.to_y),
-        rcopy(gain_acc.at[2], gain_rx.at[2], gs.at[2], gr.at[2], p.to_pair),
     ] + [
-        rcopy(gain_acc.at[3], gain_rx.at[2 + k], gs.at[2 + k], gr.at[2 + k], p.to_z(k))
-        for k in range(1, nz)
+        rcopy(gain_acc.at[2 + b], gain_rx.at[2 + b], gs.at[2 + b], gr.at[2 + b], p.to_dp(bit))
+        for b, bit in enumerate(p.bits)
     ]
     gain_steps[0].start()
     c1.wait_recv()
@@ -1166,42 +1352,91 @@
         return 0
 
     lax.fori_loop(0, srows // 64, seq_y, 0)
-    cy.start()
-    for n in range(3):
+    for c in cys:
+        c.start()
+    for n in range(len(gain_steps)):
         gain_steps[n].wait_recv()
         gain_acc[n + 1] = gain_acc[n] + gain_rx[n]
-        if n < 2:
+        if n + 1 < len(gain_steps):
             gain_steps[n + 1].start()
-        else:
-            for k in range(1, nz):
-                gain_steps[2 + k].start()
-        sc.tick(1)
+        if n % 2 == 0:
+            sc.tick(1)
     c0.wait_recv()
-    cy.wait_recv()
+    for c in cys:
+        c.wait_recv()
 
     def seq_f(t, _):
         t = al(t * 64, 64)
         a = pl.ds(t, 64)
         b = pl.ds(al(p.f * srows + t, 64), 64)
-        seq_v[b, :] = (
-            lkv_v[a, :].astype(F32) + seq_v[b, :].astype(F32) + seqy_v[a, :].astype(F32)
+        a2 = pl.ds(srows + t, 64)
+        seq_v[b, :mw] = (
+            lkv_v[a, :mw].astype(F32) + seq_v[b, :mw].astype(F32) + mixed_v[a, :].astype(F32)
+        ).astype(BF16)
+        seq_v[b, mw:] = (
+            lkv_v[a, mw:].astype(F32)
+            + seq_v[b, mw:].astype(F32)
+            + mixed_v[a2, : kvw - mw].astype(F32)
         ).astype(BF16)
         return 0
 
     lax.fori_loop(0, srows // 64, seq_f, 0)
-    sc.add(seq_v, p.f * srows, True, o_seq, pieces[5])
-    total = gain_acc[3]
-    for k in range(1, nz):
-        gain_steps[2 + k].wait_recv()
-        total = total + gain_rx[2 + k]
-    o_gain[...] = total
+    sc.add(seq_v, p.f * srows, o_seq, pieces[5])
+    o_gain[...] = gain_acc[len(gain_steps)]
+    for t in [c1, c0] + cys:
+        t.wait_send()
+    hid_in = local_copy(hid_h, lkv_v.at[:, ffc])
+
+    def down_load(t):
+        s = lax.rem(t, 2)
+        return pltpu.make_async_copy(
+            down_h.at[pl.ds(al(t * 256, 256), 256)],
+            seq_v.at[pl.ds(al(p.f_core * srows + s * 256, 256), 256), ffc],
+            tls.at[s],
+        )
+
+    down_load(0).start()
+    sc.tick(1)
+    hid_in.wait()
+
+    def ffn_out(t, _):
+        down_load(t).wait()
+
+        @pl.when(t + 1 < n_tiles)
+        def _():
+            down_load(t + 1).start()
+
+        w = seq_v[pl.ds(al(p.f_core * srows + lax.rem(t, 2) * 256, 256), 256), ffc]
+        cols = pl.ds(al(t * 256, 256), 256)
+        for r in range(rows // 256):
+            rr = pl.ds(r * 256, 256)
+            proj_v[rr, cols] = mm_nt(lkv_v[rr, ffc], w).astype(BF16)
+        return 0
+
+    lax.fori_loop(0, n_tiles, ffn_out, 0)
+    red3 = FsReduce(
+        p,
+        lambda b: proj_v.at[pl.ds(al(b * own, own), own)],
+        fcore_v,
+        fy_v,
+        fss.at[5],
+        frs.at[5],
+    )
+    red3.start()
+    sc.tick(1)
+    red3.mid(own)
+    sc.tick(2)
+    red3.end()
+    for m in range(2):
+        rr = pl.ds(m * t2, t2)
+        o_y[m] = (middle[rr, :] + red3.value(rr)).astype(BF16)
     sc.drain()
-    red2.wait_sends()
-    for t in [c1, c0, cy] + gain_steps:
+    red3.wait_sends()
+    for t in gain_steps:
         t.wait_send()
 
 
-def backward_call(ndp, tok, dout, middle, latent, normed, gains, cos, sin, bias, grads, gnt, saved):
+def backward_call(ndp, tok, dout, middle, latent, normed, gains, cos, sin, bias, grads, ffn, saved):
     lkv, q, mixed, qb, out, seq = saved
     nz = ndp // 2
     own, dim = middle.shape
@@ -1219,11 +1454,11 @@
     pieces = tuple(s[0] // piece_rows(s[0], nz) for s in shards)
     n = sum(pieces)
     slots = DpScatter.SLOTS
+    nb = ndp.bit_length() - 1
     pr = max(piece_rows(s[0], nz) for s in shards)
     width = max(s[1] for s in shards)
     dma = pltpu.SemaphoreType.DMA
     scratch = [
-        pltpu.VMEM((2, own, dim), BF16),
         pltpu.VMEM((2, own, dim), BF16),
         pltpu.VMEM((own, dim), BF16),
         pltpu.VMEM((rows, dim), BF16),
@@ -1237,39 +1472,40 @@
         pltpu.VMEM(qb.shape, BF16),
         pltpu.VMEM(out.shape, BF16),
         pltpu.VMEM(seq.shape, BF16),
-        pltpu.VMEM((ndp * sr, kvw), BF16),
         pltpu.VMEM((own, kvw), BF16),
-        pltpu.VMEM((2 + nz,) + gains.shape, F32),
-        pltpu.VMEM((4,) + gains.shape, F32),
+        pltpu.VMEM((2 + nb,) + gains.shape, F32),
+        pltpu.VMEM((3 + nb,) + gains.shape, F32),
         pltpu.VMEM((slots, nz, pr, width), BF16),
         pltpu.VMEM((slots, nz - 1, pr, width), BF16),
-        pltpu.VMEM((slots, nz, pr, width), BF16),
+        pltpu.VMEM((DpScatter.OWN, nz, pr, width), BF16),
         pltpu.VMEM((slots, pr, width), F32),
-        dma((slots, nz)),
-        dma((slots, nz)),
-        dma((slots, nz - 1)),
-        dma((slots, nz - 1)),
+        dma((slots, nz + nb - 1)),
+        dma((slots, nz + nb - 1)),
         dma((slots, nz + 1)),
-        pltpu.SemaphoreType.REGULAR,
-        pltpu.SemaphoreType.REGULAR((nz - 1,)),
-        dma((4, 3)),
-        dma((4, 3)),
-        dma((2 + nz,)),
-        dma((2 + nz,)),
-        dma((8,)),
+        pltpu.SemaphoreType.REGULAR((nb, nb)),
+        dma((6, 4)),
+        dma((6, 4)),
+        dma((2 + nb,)),
+        dma((2 + nb,)),
+        dma((9,)),
+        dma((4,)),
     ]
     return pl.pallas_call(
         functools.partial(backward_kernel, (ndp, own, dim, rank, hd, heads, pieces)),
         out_shape=tuple(jax.ShapeDtypeStruct(s, F32) for s in shards)
-        + (jax.ShapeDtypeStruct(gains.shape, F32), jax.ShapeDtypeStruct(tok.shape, BF16)),
-        in_specs=(VMEM,) * 9 + (ANY,) * 10,
-        out_specs=(ANY,) * 6 + (VMEM,) * 2,
+        + (
+            jax.ShapeDtypeStruct(gains.shape, F32),
+            jax.ShapeDtypeStruct(tok.shape, BF16),
+            jax.ShapeDtypeStruct(tok.shape, BF16),
+        ),
+        in_specs=(VMEM,) * 9 + (ANY,) * 15,
+        out_specs=(ANY,) * 6 + (VMEM,) * 3,
         scratch_shapes=scratch,
         compiler_params=pltpu.CompilerParams(
             collective_id=1, has_side_effects=True, vmem_limit_bytes=62 * 2**20
         ),
         name="backward_scatter",
-    )(tok, dout, middle, latent, normed, gains, cos, sin, bias, *grads, gnt, lkv, q, mixed, qb, out, seq)
+    )(tok, dout, middle, latent, normed, gains, cos, sin, bias, *grads, *ffn, lkv, q, mixed, qb, out, seq)
 
 
 def per_device(
@@ -1329,27 +1565,16 @@
         latent,
         normed,
         middle,
-        n2,
-        d_all,
+        hidden,
+        grad_gate,
+        grad_up,
+        gw_gate,
+        gw_up,
+        gw_down,
     ) = forward_call(
         ndp, tokens, d_output, cos, sin, bias, seq_sh, gain_sh, w_qb, w_out, w_gate, w_up, w_down
     )
-    gate = jnp.dot(n2, gate_all, preferred_element_type=F32)
-    up = jnp.dot(n2, up_all, preferred_element_type=F32)
-    sig = jax.nn.sigmoid(gate)
-    hidden = (gate * sig * up).astype(BF16)
-    grad_hidden = jnp.dot(d_all, down_all, preferred_element_type=F32)
-    grad_gate = (grad_hidden * up * sig * (1.0 + gate * (1.0 - sig))).astype(BF16)
-    grad_up = (grad_hidden * gate * sig).astype(BF16)
-    ffn_part = mm_nt(hidden, down_all).astype(BF16)
-    gnt_part = (mm_nt(grad_gate, gate_all) + mm_nt(grad_up, up_all)).astype(BF16)
-    gw_down = mm_tn(d_all, hidden).astype(BF16)
-    gw_gate = mm_tn(n2, grad_gate).astype(BF16)
-    gw_up = mm_tn(n2, grad_up).astype(BF16)
-
-    ffn_own = lax.psum_scatter(ffn_part, "fsdp", scatter_dimension=0, tiled=True).astype(F32)
-    output = (middle + ffn_own).astype(BF16).reshape(tokens.shape)
-    o_gate, o_up, o_down, o_out, o_qb, o_seq, o_gain, input_grad = backward_call(
+    o_gate, o_up, o_down, o_out, o_qb, o_seq, o_gain, input_grad, output = backward_call(
         ndp,
         tokens,
         d_output,
@@ -1361,7 +1586,7 @@
         sin,
         bias,
         (gw_gate, gw_up, gw_down),
-        gnt_part,
+        (hidden, grad_gate, grad_up, gate_all, up_all, down_all),
         (lkv, q_all, mixed, qb_all, out_all, seq_all),
     )
 

time: 774 us -> 747 us (0.965)
  matrix products: 83.5 us -> 0 us
  Pallas kernels: 639 us -> 715 us
  between operations: 14.5 us -> 0.73 us
    dot_general x9 -> x0, matrix products: 83.5 us -> none  [the longest x3 29 us: mm_tn(): lax.dot_general(a, b, (((0,), (0,)), ((), ())), preferred_element_type=F32)]
    pallas_call x1, Pallas kernels: 298 us -> 380 us  [forward_call(): pl.pallas_call(functools.partial(forward_kernel, (ndp, own, dim, rank, hd...]
  transfers between devices with their start and end apart: 1 -> 0, of which waited for: 0 -> 0; matrix products, arithmetic and copies ran while one was open for 7% -> 0% of each run, Pallas kernels for 45% -> 0%
where the time goes in v3:
time: 747 us; the launch traced here: 743 us
  Pallas kernels  715 us (96%)
  local copies, waits for them, and re-layouts  17.9 us (2%)
  other arithmetic  9.6 us (1%)
    pallas_call x1, Pallas kernels, forward_call(): pl.pallas_call(functools.partial(forward_kernel, (ndp, own, dim, rank, hd...  380 us
    pallas_call x1, Pallas kernels, backward_call(): pl.pallas_call(functools.partial(backward_kernel, (ndp, own, dim, rank, h...  334 us

profile of v3, /device:TPU:0, one launch (start us, length us, event | category | flops | bytes accessed | tf_op | source)
XLA Modules:
  0.0 742.8 jit_solution(13423949034350989448)
XLA Ops:
  0.7 0.1 iota.88
  0.7 0.1 iota.89
  0.8 0.7 broadcast_in_dim.73
  1.5 0.1 broadcast_in_dim.74
  1.6 0.7 broadcast_in_dim.77
  2.2 0.1 broadcast_in_dim.78
  2.3 0.7 convert_element_type.38
  3.0 0.1 broadcast_select_fusion
  3.1 0.1 select_n.50
  3.1 0.6 select_maximum_fusion.gain_sh
  3.8 0.9 convert_reduce_fusion
  4.7 0.1 broadcast_in_dim.69
  4.8 0.1 mul.64
  4.9 0.7 broadcast_compare_fusion
  5.6 0.1 broadcast_in_dim.68
  5.6 0.1 gt.15
  5.7 0.8 fusion.3
  6.5 0.1 convert_bitcast_fusion
  6.6 3.1 multiply_sine_fusion
  9.7 0.7 broadcast_in_dim.70
  10.4 0.1 reshape.146
  10.6 1.0 and_select_fusion.bias
  11.5 1.6 pad_maximum_fusion.seq_sh
  13.2 380.2 %gather_forward.1 = (bf16[1024,1024]{1,0:T(8,128)(2,1)}, bf16[2048,1024]{1,0:T(8,128)(2,1)}, bf16[2048,1408]{1,0:T(8,128)(2,1)}, bf16[2048,1408]{1,0:T(8,128)(2,...) custom-call(bf16[2,128,2048]{2,1,0:T(8,128)(2,1)} %tok.3, ...), custom_call_target="tpu_custom_call" | custom-call | tf_op jit(solution)/shard_map/gather_forward/pallas_call | solution.py:769
  393.4 334.4 %backward_scatter.1 = (f32[256,1408]{1,0:T(8,128)}, f32[256,1408]{1,0:T(8,128)}, f32[256,1408]{1,0:T(8,128)}, f32[256,1024]{1,0:T(8,128)}, f32[128,1024]{1,0:T(8...) custom-call(bf16[2,128,2048]{2,1,0:T(8,128)(2,1)} %tok.3, ...), custom_call_target="tpu_custom_call" | custom-call | tf_op jit(solution)/shard_map/backward_scatter/pallas_call | solution.py:1493
  727.7 0.0 copy-start.4
  727.8 0.0 copy-start.5
  727.8 0.9 slice_bitcast_fusion
  728.7 0.6 dynamic_slice.14
  729.3 0.6 dynamic_slice.11
  729.8 1.7 slice.23
  731.5 0.0 copy-start.3
  731.5 1.6 fusion.4
  733.1 0.8 slice.24
  733.9 0.6 dynamic-slice_bitcast_fusion
  734.5 2.3 copy.40
  736.8 0.0 copy-done.4
  736.8 0.0 copy-start.2
  736.8 1.0 copy.41
  737.7 0.0 copy-done.5
  737.8 0.0 copy-start.1
  737.8 0.8 copy.42
  738.5 0.0 copy-done.3
  738.5 1.0 copy.43
  739.5 0.0 copy-done.2
  739.5 0.0 copy-start
  739.5 1.1 copy.44
  740.6 0.0 copy-done.1
  740.6 1.1 copy.45
  741.7 0.0 copy-done
  741.7 1.1 copy.46
  (12 shorter events, 0.1 us)
Async XLA Ops:
  727.7 9.0 %copy-start.4 = (bf16[2,128,2048]{2,1,0:T(8,128)(2,1)S(1)}, bf16[2,128,2048]{2,1,0:T(8,128)(2,1)}, u32[]{:S(2)}) copy-start(bf16[2,128,2048]{2,1,0:T(8,128)(2,1)} %get-tuple-element.93) | copy-start | bytes 3145732
  727.8 10.0 %copy-start.5 = (f32[128,1024]{1,0:T(8,128)S(1)}, f32[128,1024]{1,0:T(8,128)}, u32[]{:S(2)}) copy-start(f32[128,1024]{1,0:T(8,128)} %get-tuple-element.97) | copy-start | bytes 1572868
  731.5 7.0 copy-start.3
  736.8 2.7 copy-start.2
  737.8 2.9 copy-start.1
  739.5 2.2 copy-start

commit v4 on v3

--- a/solution.py
+++ b/solution.py
@@ -116,7 +116,7 @@
     def __init__(self, pos, ss, rs):
         self.p, self.ss, self.rs = pos, ss, rs
         self.items, self.events = [], []
-        self.launched = self.seen = 0
+        self.launched = self.seen = self.first = 0
 
     def add(self, src, dst, swapped=False):
         self.items.append((src, dst, self.p.orders(swapped)[::-1]))
@@ -160,20 +160,28 @@
         out = [m for m in range(1, self.p.ndp) if not m & last]
         return sorted(out, key=lambda m: (self.stage_of(n, m), m))
 
-    def forward(self, n):
+    def forward(self, n, stage):
         for m in self.masks(n):
-            self.arrived(n, m)
-            for stage in range(self.stage_of(n, m) + 1, len(self.p.bits)):
-                self.copy(n, m, stage).start()
+            if self.stage_of(n, m) == stage:
+                self.arrived(n, m)
+                for later in range(stage + 1, len(self.p.bits)):
+                    self.copy(n, m, later).start()
 
     def steps(self, count, ahead):
+        lag = len(self.p.bits) - 1
         for _ in range(count):
-            if self.seen >= len(self.items):
+            if self.seen >= len(self.items) + lag - 1:
                 return
             while self.launched < min(len(self.items), self.seen + ahead):
                 self.launch()
-            self.forward(self.seen)
+            for stage in range(lag):
+                n = self.seen - stage
+                if self.first <= n < len(self.items):
+                    self.forward(n, stage)
             self.seen += 1
+
+    def need(self, n, ahead):
+        self.steps(n + len(self.p.bits) - 1 - self.seen, ahead)
 
     def wait_last(self, n):
         last = self.items[n][2][-1]
@@ -434,7 +442,7 @@
             for stage in range(g.stage_of(i, m) + 1, len(p.bits)):
                 g.copy(i, m, stage).start()
         spread(p.at(m))
-    g.seen = 2
+    g.seen = g.first = 2
     for c in d_copies:
         c.wait()
 
@@ -495,6 +503,7 @@
     fs_l.mid()
     tick(1)
     for i in i_qb:
+        g.need(i, GATHER_AHEAD)
         own_copies[i].wait()
         g.wait_last(i)
     fs_l.end()
@@ -548,6 +557,7 @@
     mixed_out = local_copy(mixed_v, mixed_o)
     tick(1)
     for i in i_out:
+        g.need(i, GATHER_AHEAD)
         own_copies[i].wait()
         g.wait_last(i)
     out_out = local_copy(out_v, out_all)
@@ -617,7 +627,7 @@
     pending = []
     width = FFN_COLS
     for (c0, cw), some in zip(ffn_chunks(gate_sh.shape[1]), i_ffn):
-        tick(some[-1] + 1 - g.seen)
+        g.need(some[-1], GATHER_AHEAD)
         for i in some:
             own_copies[i].wait()
             g.wait_last(i)
@@ -691,7 +701,7 @@
         pending = pending + saves
     for c in pending:
         c.wait()
-    tick(len(g.items))
+    tick(2 * len(g.items))
     for i in order:
         if i not in early:
             g.wait_sends(i)
@@ -780,20 +790,19 @@
 
 
 class DpScatter:
-    SLOTS = 5
-    AHEAD = 2
-    OWN = 3
+    PER_TICK = 2
 
     def __init__(self, pos, count, first, later, own, acc, ss, rs, ls, credit):
         self.p, self.count = pos, count
         self.n = len(pos.bits)
+        self.SLOTS, self.AHEAD, self.OWN = scatter_ring(pos.ndp // 2)
         self.first, self.later, self.own, self.acc = first, later, own, acc
         self.ss, self.rs, self.ls, self.credit = ss, rs, ls, credit
         self.items = []
         self.started = self.stepped = 0
 
     def order(self, n):
-        return self.p.orders(n % 4 == 3)
+        return self.p.orders(False)
 
     def width(self, stage):
         return 1 << (self.n - 1 - stage)
@@ -889,7 +898,7 @@
             self.started += 1
 
     def tick(self, steps=1):
-        for _ in range(steps):
+        for _ in range(self.PER_TICK * steps):
             n = self.stepped
             if n >= self.started:
                 return
@@ -953,8 +962,12 @@
             self.outcopy(n).wait()
 
 
+def scatter_ring(nz):
+    return (10, 6, 7) if nz * max(16, 128 // nz) <= 128 else (5, 2, 3)
+
+
 def piece_rows(rows, nz):
-    return min(rows, max(16, 256 // nz))
+    return min(rows, max(16, 128 // nz))
 
 
 def backward_kernel(
@@ -1453,7 +1466,7 @@
     ]
     pieces = tuple(s[0] // piece_rows(s[0], nz) for s in shards)
     n = sum(pieces)
-    slots = DpScatter.SLOTS
+    slots, _, own_slots = scatter_ring(nz)
     nb = ndp.bit_length() - 1
     pr = max(piece_rows(s[0], nz) for s in shards)
     width = max(s[1] for s in shards)
@@ -1477,7 +1490,7 @@
         pltpu.VMEM((3 + nb,) + gains.shape, F32),
         pltpu.VMEM((slots, nz, pr, width), BF16),
         pltpu.VMEM((slots, nz - 1, pr, width), BF16),
-        pltpu.VMEM((DpScatter.OWN, nz, pr, width), BF16),
+        pltpu.VMEM((own_slots, nz, pr, width), BF16),
         pltpu.VMEM((slots, pr, width), F32),
         dma((slots, nz + nb - 1)),
         dma((slots, nz + nb - 1)),

time: 747 us -> 698 us (0.934)
  Pallas kernels: 715 us -> 660 us
    pallas_call x1, Pallas kernels: 380 us -> 347 us  [forward_call(): pl.pallas_call(functools.partial(forward_kernel, (ndp, own, dim, rank, hd...]
    pallas_call x1, Pallas kernels: 334 us -> 313 us  [backward_call(): pl.pallas_call(functools.partial(backward_kernel, (ndp, own, dim, rank, h...]
where the time goes in v4:
time: 698 us; the launch traced here: 689 us
  Pallas kernels  660 us (95%)
  local copies, waits for them, and re-layouts  17.9 us (3%)
  other arithmetic  9.6 us (1%)
    pallas_call x1, Pallas kernels, forward_call(): pl.pallas_call(functools.partial(forward_kernel, (ndp, own, dim, rank, hd...  347 us
    pallas_call x1, Pallas kernels, backward_call(): pl.pallas_call(functools.partial(backward_kernel, (ndp, own, dim, rank, h...  313 us

profile of v4, /device:TPU:0, one launch (start us, length us, event | category | flops | bytes accessed | tf_op | source)
XLA Modules:
  0.0 688.8 jit_solution(5852035070353474145)
XLA Ops:
  0.7 0.1 iota.88
  0.7 0.1 iota.89
  0.8 0.7 broadcast_in_dim.73
  1.5 0.1 broadcast_in_dim.74
  1.6 0.7 broadcast_in_dim.77
  2.2 0.1 broadcast_in_dim.78
  2.3 0.7 convert_element_type.38
  3.0 0.1 broadcast_select_fusion
  3.1 0.1 select_n.50
  3.1 0.6 select_maximum_fusion.gain_sh
  3.8 0.9 convert_reduce_fusion
  4.7 0.1 broadcast_in_dim.69
  4.8 0.1 mul.64
  4.9 0.7 broadcast_compare_fusion
  5.6 0.1 broadcast_in_dim.68
  5.6 0.1 gt.15
  5.7 0.8 fusion.3
  6.5 0.1 convert_bitcast_fusion
  6.6 3.1 multiply_sine_fusion
  9.7 0.7 broadcast_in_dim.70
  10.4 0.1 reshape.146
  10.6 1.0 and_select_fusion.bias
  11.5 1.6 pad_maximum_fusion.seq_sh
  13.2 347.4 %gather_forward.1 = (bf16[1024,1024]{1,0:T(8,128)(2,1)}, bf16[2048,1024]{1,0:T(8,128)(2,1)}, bf16[2048,1408]{1,0:T(8,128)(2,1)}, bf16[2048,1408]{1,0:T(8,128)(2,...) custom-call(bf16[2,128,2048]{2,1,0:T(8,128)(2,1)} %tok.3, ...), custom_call_target="tpu_custom_call" | custom-call | tf_op jit(solution)/shard_map/gather_forward/pallas_call | solution.py:779
  360.6 312.8 %backward_scatter.1 = (f32[256,1408]{1,0:T(8,128)}, f32[256,1408]{1,0:T(8,128)}, f32[256,1408]{1,0:T(8,128)}, f32[256,1024]{1,0:T(8,128)}, f32[128,1024]{1,0:T(8...) custom-call(bf16[2,128,2048]{2,1,0:T(8,128)(2,1)} %tok.3, ...), custom_call_target="tpu_custom_call" | custom-call | tf_op jit(solution)/shard_map/backward_scatter/pallas_call | solution.py:1506
  673.4 0.0 copy-start.4
  673.4 0.0 copy-start.5
  673.5 0.9 slice_bitcast_fusion
  674.4 0.6 dynamic_slice.14
  674.9 0.6 dynamic_slice.11
  675.5 1.7 slice.23
  677.2 0.0 copy-start.3
  677.2 1.6 fusion.4
  678.8 0.8 slice.24
  679.6 0.6 dynamic-slice_bitcast_fusion
  680.2 2.3 copy.40
  682.5 0.0 copy-done.4
  682.5 0.0 copy-start.2
  682.5 1.0 copy.41
  683.4 0.0 copy-done.5
  683.4 0.0 copy-start.1
  683.4 0.8 copy.42
  684.2 0.0 copy-done.3
  684.2 1.0 copy.43
  685.2 0.0 copy-done.2
  685.2 0.0 copy-start
  685.2 1.1 copy.44
  686.3 0.0 copy-done.1
  686.3 1.1 copy.45
  687.4 0.0 copy-done
  687.4 1.1 copy.46
  (12 shorter events, 0.1 us)
Async XLA Ops:
  673.4 9.0 %copy-start.4 = (bf16[2,128,2048]{2,1,0:T(8,128)(2,1)S(1)}, bf16[2,128,2048]{2,1,0:T(8,128)(2,1)}, u32[]{:S(2)}) copy-start(bf16[2,128,2048]{2,1,0:T(8,128)(2,1)} %get-tuple-element.93) | copy-start | bytes 3145732
  673.4 10.0 %copy-start.5 = (f32[128,1024]{1,0:T(8,128)S(1)}, f32[128,1024]{1,0:T(8,128)}, u32[]{:S(2)}) copy-start(f32[128,1024]{1,0:T(8,128)} %get-tuple-element.97) | copy-start | bytes 1572868
  677.2 7.0 %copy-start.3 = (f32[256,1024]{1,0:T(8,128)S(1)}, f32[256,1024]{1,0:T(8,128)}, u32[]{:S(2)}) copy-start(f32[256,1024]{1,0:T(8,128)} %get-tuple-element.100) | copy-start | bytes 3145732
  682.5 2.7 copy-start.2
  683.4 2.9 copy-start.1
  685.2 2.2 copy-start

commit v5 on v4

--- a/solution.py
+++ b/solution.py
@@ -19,7 +19,8 @@
 VMEM = pl.BlockSpec(memory_space=pltpu.VMEM)
 NF = 4
 GATHER_ROWS = 64
-GATHER_AHEAD = 4
+GATHER_AHEAD = 5
+GATHER_FIRST = 4
 FFN_ROWS = 128
 FFN_COLS = 512
 
@@ -373,7 +374,7 @@
                 g.add(
                     src.at[pl.ds(c * step, step), cols],
                     lambda j, c=c: dst.at[pl.ds(al(j * n + c * step, step), step), cols],
-                    turn[0] % 4 == 0,
+                    turn[0] % 8 == 0,
                 )
             )
         return out
@@ -413,7 +414,7 @@
     ]
 
     p.barrier()
-    for _ in range(GATHER_AHEAD):
+    for _ in range(GATHER_FIRST):
         g.launch()
     npiece = ndp
 
@@ -656,7 +657,9 @@
             q_v[rr, up_c] = (grad_hidden * act).astype(BF16)
             return 0
 
-        lax.fori_loop(0, rows // 256, both, 0)
+        for lo in range(0, rows // 256, 2):
+            lax.fori_loop(lo, lo + 2, both, 0)
+            tick(1)
         pending = [
             pltpu.make_async_copy(src, dst.at[:, cols], ffn_ls.at[3 + n])
             for n, (src, dst) in enumerate(
@@ -683,6 +686,7 @@
                 return 0
 
             lax.fori_loop(lo, min(dim // 256, lo + half_rows), weight_grads, 0)
+            tick(1)
         saves = [
             pltpu.make_async_copy(out_v.at[:, pl.ds(0, cw)], gw_gate.at[:, cols], ffn_ls.at[6]),
             pltpu.make_async_copy(out_v.at[:, pl.ds(width, cw)], gw_up.at[:, cols], ffn_ls.at[7]),

time: 698 us -> 678 us (0.971)
  Pallas kernels: 660 us -> 640 us
    pallas_call x1, Pallas kernels: 347 us -> 327 us  [forward_call(): pl.pallas_call(functools.partial(forward_kernel, (ndp, own, dim, rank, hd...]
where the time goes in v5:
time: 678 us; the launch traced here: 669 us
  Pallas kernels  640 us (94%)
  local copies, waits for them, and re-layouts  17.9 us (3%)
  other arithmetic  9.6 us (1%)
    pallas_call x1, Pallas kernels, forward_call(): pl.pallas_call(functools.partial(forward_kernel, (ndp, own, dim, rank, hd...  327 us
    pallas_call x1, Pallas kernels, backward_call(): pl.pallas_call(functools.partial(backward_kernel, (ndp, own, dim, rank, h...  313 us

profile of v5, /device:TPU:0, one launch (start us, length us, event | category | flops | bytes accessed | tf_op | source)
XLA Modules:
  0.0 669.2 jit_solution(12502091552599969192)
XLA Ops:
  0.7 0.1 iota.88
  0.7 0.1 iota.89
  0.8 0.7 broadcast_in_dim.73
  1.5 0.1 broadcast_in_dim.74
  1.6 0.7 broadcast_in_dim.77
  2.2 0.1 broadcast_in_dim.78
  2.3 0.7 convert_element_type.38
  3.0 0.1 broadcast_select_fusion
  3.1 0.1 select_n.50
  3.1 0.6 select_maximum_fusion.gain_sh
  3.8 0.9 convert_reduce_fusion
  4.7 0.1 broadcast_in_dim.69
  4.8 0.1 mul.64
  4.9 0.7 broadcast_compare_fusion
  5.6 0.1 broadcast_in_dim.68
  5.6 0.1 gt.15
  5.7 0.8 fusion.3
  6.5 0.1 convert_bitcast_fusion
  6.6 3.1 multiply_sine_fusion
  9.7 0.7 broadcast_in_dim.70
  10.4 0.1 reshape.146
  10.6 1.0 and_select_fusion.bias
  11.5 1.6 pad_maximum_fusion.seq_sh
  13.2 327.5 %gather_forward.1 = (bf16[1024,1024]{1,0:T(8,128)(2,1)}, bf16[2048,1024]{1,0:T(8,128)(2,1)}, bf16[2048,1408]{1,0:T(8,128)(2,1)}, bf16[2048,1408]{1,0:T(8,128)(2,...) custom-call(bf16[2,128,2048]{2,1,0:T(8,128)(2,1)} %tok.3, ...), custom_call_target="tpu_custom_call" | custom-call | tf_op jit(solution)/shard_map/gather_forward/pallas_call | solution.py:783
  340.6 313.0 %backward_scatter.1 = (f32[256,1408]{1,0:T(8,128)}, f32[256,1408]{1,0:T(8,128)}, f32[256,1408]{1,0:T(8,128)}, f32[256,1024]{1,0:T(8,128)}, f32[128,1024]{1,0:T(8...) custom-call(bf16[2,128,2048]{2,1,0:T(8,128)(2,1)} %tok.3, ...), custom_call_target="tpu_custom_call" | custom-call | tf_op jit(solution)/shard_map/backward_scatter/pallas_call | solution.py:1510
  653.7 0.0 copy-start.4
  653.7 0.0 copy-start.5
  653.7 0.9 slice_bitcast_fusion
  654.6 0.6 dynamic_slice.14
  655.2 0.6 dynamic_slice.11
  655.8 1.7 slice.23
  657.4 0.0 copy-start.3
  657.4 1.6 fusion.4
  659.0 0.8 slice.24
  659.8 0.6 dynamic-slice_bitcast_fusion
  660.4 2.3 copy.40
  662.7 0.0 copy-done.4
  662.7 0.0 copy-start.2
  662.7 1.0 copy.41
  663.7 0.0 copy-done.5
  663.7 0.0 copy-start.1
  663.7 0.8 copy.42
  664.5 0.0 copy-done.3
  664.5 1.0 copy.43
  665.4 0.0 copy-done.2
  665.4 0.0 copy-start
  665.4 1.1 copy.44
  666.5 0.0 copy-done.1
  666.5 1.1 copy.45
  667.6 0.0 copy-done
  667.6 1.1 copy.46
  (12 shorter events, 0.1 us)
Async XLA Ops:
  653.7 9.0 %copy-start.4 = (bf16[2,128,2048]{2,1,0:T(8,128)(2,1)S(1)}, bf16[2,128,2048]{2,1,0:T(8,128)(2,1)}, u32[]{:S(2)}) copy-start(bf16[2,128,2048]{2,1,0:T(8,128)(2,1)} %get-tuple-element.93) | copy-start | bytes 3145732
  653.7 10.0 %copy-start.5 = (f32[128,1024]{1,0:T(8,128)S(1)}, f32[128,1024]{1,0:T(8,128)}, u32[]{:S(2)}) copy-start(f32[128,1024]{1,0:T(8,128)} %get-tuple-element.97) | copy-start | bytes 1572868
  657.4 7.0 %copy-start.3 = (f32[256,1024]{1,0:T(8,128)S(1)}, f32[256,1024]{1,0:T(8,128)}, u32[]{:S(2)}) copy-start(f32[256,1024]{1,0:T(8,128)} %get-tuple-element.100) | copy-start | bytes 3145732
  662.7 2.7 copy-start.2
  663.7 2.9 copy-start.1
  665.4 2.2 copy-start

commit v6 on v5

--- a/solution.py
+++ b/solution.py
@@ -330,6 +330,7 @@
     gw_gate,
     gw_up,
     gw_down,
+    rx_o,
     seq_v,
     gain_v,
     qb_v,
@@ -353,6 +354,8 @@
     syr,
     ls,
     ffn_ls,
+    pss,
+    prs,
 ):
     ndp, own, dim, rank, hd, heads = cfg
     rows = NF * own
@@ -627,7 +630,21 @@
     red.wait_sends()
     pending = []
     width = FFN_COLS
-    for (c0, cw), some in zip(ffn_chunks(gate_sh.shape[1]), i_ffn):
+    chunks = ffn_chunks(gate_sh.shape[1])
+    nb = len(p.bits)
+    blk = gate_sh.shape[0]
+
+    def early_copy(i):
+        mask = 1 + sum(p.bits[1 + t] for t in range(nb - 1) if i >> (nb - 2 - t) & 1)
+        return rcopy(
+            gw_gate.at[pl.ds(al(p.at(mask) * blk, blk), blk), pl.ds(0, width)],
+            rx_o.at[i],
+            pss.at[i],
+            prs.at[i],
+            p.to_dp(1),
+        )
+
+    for n_chunk, ((c0, cw), some) in enumerate(zip(chunks, i_ffn)):
         g.need(some[-1], GATHER_AHEAD)
         for i in some:
             own_copies[i].wait()
@@ -641,6 +658,9 @@
             c.start()
         for c in pending:
             c.wait()
+        if n_chunk == len(chunks) - 1:
+            for i in range(ndp // 2):
+                early_copy(i).start()
         for c in loads:
             c.wait()
         gate_c, up_c, down_c = (slice(n * width, n * width + cw) for n in range(3))
@@ -706,6 +726,9 @@
     for c in pending:
         c.wait()
     tick(2 * len(g.items))
+    for i in range(ndp // 2):
+        early_copy(i).wait_recv()
+        early_copy(i).wait_send()
     for i in order:
         if i not in early:
             g.wait_sends(i)
@@ -752,8 +775,9 @@
         full(gate),
         full(up),
         full(down),
+        sds((ndp // 2, gate.shape[0], FFN_COLS)),
     )
-    out_specs = (ANY,) * 6 + (VMEM,) + (ANY,) * 3 + (VMEM,) * 3 + (ANY,) * 6
+    out_specs = (ANY,) * 6 + (VMEM,) + (ANY,) * 3 + (VMEM,) * 3 + (ANY,) * 7
     dma = pltpu.SemaphoreType.DMA
     scratch = [
         pltpu.VMEM((seq_sh.shape[0] * ndp * NF, kvw), BF16),
@@ -779,6 +803,8 @@
         dma((2, 3, ndp)),
         dma((n_items + 10,)),
         dma((10,)),
+        dma((ndp // 2,)),
+        dma((ndp // 2,)),
     ]
     return pl.pallas_call(
         functools.partial(forward_kernel, (ndp, own, dim, rank, hd, heads)),
@@ -794,14 +820,14 @@
 
 
 class DpScatter:
-    PER_TICK = 2
-
-    def __init__(self, pos, count, first, later, own, acc, ss, rs, ls, credit):
+    PER_TICK = 1
+
+    def __init__(self, pos, count, first, later, own, acc, ss, rs, ls, credit, pls):
         self.p, self.count = pos, count
         self.n = len(pos.bits)
         self.SLOTS, self.AHEAD, self.OWN = scatter_ring(pos.ndp // 2)
         self.first, self.later, self.own, self.acc = first, later, own, acc
-        self.ss, self.rs, self.ls, self.credit = ss, rs, ls, credit
+        self.ss, self.rs, self.ls, self.credit, self.pls = ss, rs, ls, credit, pls
         self.items = []
         self.started = self.stepped = 0
 
@@ -811,11 +837,14 @@
     def width(self, stage):
         return 1 << (self.n - 1 - stage)
 
-    def add(self, src, base, out, pieces):
-        rows, cols = out.shape
+    def make(self, src, base, out, pieces, c0=0, cols=None, pre=None):
+        rows = out.shape[0]
+        cols = out.shape[1] if cols is None else cols
         r = rows // pieces
-        for c in range(pieces):
-            self.items.append((src, base, out, rows, cols, c * r, r))
+        return [(src, base, out, rows, cols, c * r, r, c0, pre) for c in range(pieces)]
+
+    def add(self, *args):
+        self.items += self.make(*args)
         self.pump()
 
     def mask(self, n, i):
@@ -823,11 +852,11 @@
         return sum(order[1 + t] for t in range(self.n - 1) if i >> (self.n - 2 - t) & 1)
 
     def block(self, n, mask):
-        src, base, out, rows, cols, r0, r = self.items[n]
-        return src.at[pl.ds(al(base + self.p.at(mask) * rows + r0, r), r)]
+        src, base, out, rows, cols, r0, r, c0, pre = self.items[n]
+        return src.at[pl.ds(al(base + self.p.at(mask) * rows + r0, r), r), pl.ds(c0, cols)]
 
     def place(self, buf, n, lo, size):
-        src, base, out, rows, cols, r0, r = self.items[n]
+        src, base, out, rows, cols, r0, r, c0, pre = self.items[n]
         return buf.at[n % self.SLOTS, pl.ds(lo, size), pl.ds(0, r), pl.ds(0, cols)]
 
     def copies(self, n, stage):
@@ -858,7 +887,7 @@
         ]
 
     def owncopy(self, n, i):
-        src, base, out, rows, cols, r0, r = self.items[n]
+        src, base, out, rows, cols, r0, r, c0, pre = self.items[n]
         s = n % self.OWN
         return pltpu.make_async_copy(
             self.block(n, self.mask(n, i)),
@@ -867,17 +896,17 @@
         )
 
     def outcopy(self, n):
-        src, base, out, rows, cols, r0, r = self.items[n]
+        src, base, out, rows, cols, r0, r, c0, pre = self.items[n]
         s = n % self.SLOTS
         return pltpu.make_async_copy(
             self.acc.at[s, pl.ds(0, r), pl.ds(0, cols)],
-            out.at[pl.ds(r0, r)],
+            out.at[pl.ds(r0, r), pl.ds(c0, cols)],
             self.ls.at[s, self.width(0)],
         )
 
     def free(self, n, stage):
         m = n + self.SLOTS
-        if m < self.count:
+        if m < self.count and not (stage == 0 and self.given(m)):
             bit = self.order(m)[stage]
             pl.semaphore_signal(
                 self.credit.at[stage, self.p.bits.index(bit)],
@@ -886,7 +915,21 @@
                 device_id_type=MESH,
             )
 
+    def given(self, n):
+        return n < len(self.items) and self.items[n][-1] is not None
+
+    def precopy(self, n, i):
+        src, base, out, rows, cols, r0, r, c0, pre = self.items[n]
+        s = n % self.SLOTS
+        return pltpu.make_async_copy(
+            pre.at[i, pl.ds(r0, r)], self.place(self.first, n, i, 1).at[0], self.pls.at[s, i]
+        )
+
     def send(self, n, stage):
+        if stage == 0 and self.given(n):
+            for i in range(self.width(0)):
+                self.precopy(n, i).start()
+            return
         bit = self.order(n)[stage]
         if n >= self.SLOTS:
             pl.semaphore_wait(self.credit.at[stage, self.p.bits.index(bit)], 1)
@@ -914,11 +957,15 @@
                     self.combine(n - stage, stage)
 
     def combine(self, n, stage):
-        src, base, out, rows, cols, r0, r = self.items[n]
+        src, base, out, rows, cols, r0, r, c0, pre = self.items[n]
         s, tile = n % self.SLOTS, 16
         w = self.width(stage)
-        for c in self.copies(n, stage):
-            c.wait_recv()
+        if stage == 0 and pre is not None:
+            for i in range(w):
+                self.precopy(n, i).wait()
+        else:
+            for c in self.copies(n, stage):
+                c.wait_recv()
         if stage == 0:
             for i in range(w):
                 self.owncopy(n, i).wait()
@@ -944,8 +991,9 @@
         if last:
             if n >= self.SLOTS:
                 self.outcopy(n - self.SLOTS).wait()
-            for c in self.copies(n, 0):
-                c.wait_send()
+            if pre is None:
+                for c in self.copies(n, 0):
+                    c.wait_send()
             add(0, 1)
             self.outcopy(n).start()
             for t in range(self.n):
@@ -994,6 +1042,7 @@
     gate_h,
     up_h,
     down_h,
+    rx_h,
     lkv_h,
     q_h,
     mixed_h,
@@ -1033,6 +1082,7 @@
     drs,
     dls,
     credit,
+    pls,
     fss,
     frs,
     gs,
@@ -1075,10 +1125,14 @@
 
     for which in (0, 1):
         tile_load(0, which).start()
-    sc = DpScatter(p, sum(pieces), first_b, later_b, own_b, acc_b, dss, drs, dls, credit)
+    sc = DpScatter(p, sum(pieces) + pieces[0], first_b, later_b, own_b, acc_b, dss, drs, dls, credit, pls)
     p.barrier()
-    sc.add(gw_gate, 0, o_gate, pieces[0])
-    sc.add(gw_up, 0, o_up, pieces[1])
+    cut = rx_h.shape[2]
+    ready = sc.make(gw_gate, 0, o_gate, pieces[0], 0, cut, rx_h)
+    fresh = sc.make(gw_up, 0, o_up, pieces[1])
+    for a, b in zip(fresh, ready):
+        sc.items += [a, b]
+    sc.add(gw_gate, 0, o_gate, pieces[0], cut, o_gate.shape[1] - cut)
     sc.add(gw_down, 0, o_down, pieces[2])
     gg_in.wait()
     gu_in.wait()
@@ -1121,12 +1175,12 @@
         red.start()
         if h > 0:
             halves[-1].mid(own)
-        sc.tick(1)
+        sc.tick(2)
         halves.append(red)
     lkv_in = local_copy(lkv_h, lkv_v)
     seq_in = local_copy(seq_h, seq_v)
     halves[-1].mid(own)
-    sc.tick(1)
+    sc.tick(4)
     for red in halves:
         red.end()
         red.wait_sends()
@@ -1151,9 +1205,9 @@
         gain_acc[0, pl.ds(wide + r, 1), :] = part_two[:, r * rank : (r + 1) * rank]
     ag = FsGather(p, lambda b: proj_v.at[pl.ds(al(b * own, own), own)], fss.at[1], frs.at[1])
     ag.start()
-    sc.tick(1)
+    sc.tick(4)
     ag.mid()
-    sc.tick(1)
+    sc.tick(2)
     out_in.wait()
     ag.end()
     ag.wait_sends()
@@ -1166,7 +1220,7 @@
         return 0
 
     lax.fori_loop(0, heads * hd // 256, back_out, 0)
-    sc.tick(1)
+    sc.tick(2)
     mixed_in.wait()
 
     def grad_out(j, _):
@@ -1175,7 +1229,7 @@
         return 0
 
     lax.fori_loop(0, dim // 256, grad_out, 0)
-    sc.tick(1)
+    sc.tick(2)
     sc.add(out_v, 0, o_out, pieces[3])
     q_in.wait()
     lkv_in.wait()
@@ -1237,7 +1291,7 @@
         for h2 in (0, 1):
             put_rows(proj_v, m, h2, kcols, own, (kv_acc[h2] * scale).astype(BF16))
             put_rows(proj_v, m, h2, vcols, own, kv_acc[2 + h2].astype(BF16))
-        sc.tick(1)
+        sc.tick(3)
     qb_in.wait()
 
     def back_latent(j, _):
@@ -1265,10 +1319,10 @@
         frs.at[2],
     )
     red2.start()
-    sc.tick(1)
+    sc.tick(2)
     sc.add(qb_v, 0, o_qb, pieces[4])
     red2.mid(own)
-    sc.tick(1)
+    sc.tick(5)
     red2.end()
     red2.wait_sends()
     own_rows = pl.ds(al(p.f * own, own), own)
@@ -1298,7 +1352,7 @@
         return 0
 
     lax.fori_loop(0, dim // 256, back_seq, 0)
-    sc.tick(1)
+    sc.tick(2)
     span = NF * sr
 
     def grad_seq(j, _):
@@ -1376,8 +1430,7 @@
         gain_acc[n + 1] = gain_acc[n] + gain_rx[n]
         if n + 1 < len(gain_steps):
             gain_steps[n + 1].start()
-        if n % 2 == 0:
-            sc.tick(1)
+        sc.tick(1)
     c0.wait_recv()
     for c in cys:
         c.wait_recv()
@@ -1413,7 +1466,7 @@
         )
 
     down_load(0).start()
-    sc.tick(1)
+    sc.tick(2)
     hid_in.wait()
 
     def ffn_out(t, _):
@@ -1440,9 +1493,9 @@
         frs.at[5],
     )
     red3.start()
-    sc.tick(1)
+    sc.tick(2)
     red3.mid(own)
-    sc.tick(2)
+    sc.tick(5)
     red3.end()
     for m in range(2):
         rr = pl.ds(m * t2, t2)
@@ -1500,6 +1553,7 @@
         dma((slots, nz + nb - 1)),
         dma((slots, nz + 1)),
         pltpu.SemaphoreType.REGULAR((nb, nb)),
+        dma((slots, nz)),
         dma((6, 4)),
         dma((6, 4)),
         dma((2 + nb,)),
@@ -1515,7 +1569,7 @@
             jax.ShapeDtypeStruct(tok.shape, BF16),
             jax.ShapeDtypeStruct(tok.shape, BF16),
         ),
-        in_specs=(VMEM,) * 9 + (ANY,) * 15,
+        in_specs=(VMEM,) * 9 + (ANY,) * 16,
         out_specs=(ANY,) * 6 + (VMEM,) * 3,
         scratch_shapes=scratch,
         compiler_params=pltpu.CompilerParams(
@@ -1588,6 +1642,7 @@
         gw_gate,
         gw_up,
         gw_down,
+        early_gate,
     ) = forward_call(
         ndp, tokens, d_output, cos, sin, bias, seq_sh, gain_sh, w_qb, w_out, w_gate, w_up, w_down
     )
@@ -1603,7 +1658,7 @@
         sin,
         bias,
         (gw_gate, gw_up, gw_down),
-        (hidden, grad_gate, grad_up, gate_all, up_all, down_all),
+        (hidden, grad_gate, grad_up, gate_all, up_all, down_all, early_gate),
         (lkv, q_all, mixed, qb_all, out_all, seq_all),
     )
 

time: 678 us -> 665 us (0.981)
  Pallas kernels: 640 us -> 627 us
    pallas_call x1, Pallas kernels: 313 us -> 297 us  [backward_call(): pl.pallas_call(functools.partial(backward_kernel, (ndp, own, dim, rank, h...]
where the time goes in v6:
time: 665 us; the launch traced here: 656 us
  Pallas kernels  627 us (94%)
  local copies, waits for them, and re-layouts  17.9 us (3%)
  other arithmetic  9.6 us (1%)
    pallas_call x1, Pallas kernels, forward_call(): pl.pallas_call(functools.partial(forward_kernel, (ndp, own, dim, rank, hd...  331 us
    pallas_call x1, Pallas kernels, backward_call(): pl.pallas_call(functools.partial(backward_kernel, (ndp, own, dim, rank, h...  297 us

profile of v6, /device:TPU:0, one launch (start us, length us, event | category | flops | bytes accessed | tf_op | source)
XLA Modules:
  0.0 656.0 jit_solution(18004017420666659684)
XLA Ops:
  0.7 0.1 iota.88
  0.7 0.1 iota.89
  0.8 0.7 broadcast_in_dim.73
  1.5 0.1 broadcast_in_dim.74
  1.6 0.7 broadcast_in_dim.77
  2.2 0.1 broadcast_in_dim.78
  2.3 0.7 convert_element_type.38
  3.0 0.1 broadcast_select_fusion
  3.1 0.1 select_n.50
  3.1 0.6 select_maximum_fusion.gain_sh
  3.8 0.9 convert_reduce_fusion
  4.7 0.1 broadcast_in_dim.69
  4.8 0.1 mul.64
  4.9 0.7 broadcast_compare_fusion
  5.6 0.1 broadcast_in_dim.68
  5.6 0.1 gt.15
  5.7 0.8 fusion.3
  6.5 0.1 convert_bitcast_fusion
  6.6 3.1 multiply_sine_fusion
  9.7 0.7 broadcast_in_dim.70
  10.4 0.1 reshape.146
  10.6 1.0 and_select_fusion.bias
  11.5 1.6 pad_maximum_fusion.seq_sh
  13.2 330.6 %gather_forward.1 = (bf16[1024,1024]{1,0:T(8,128)(2,1)}, bf16[2048,1024]{1,0:T(8,128)(2,1)}, bf16[2048,1408]{1,0:T(8,128)(2,1)}, bf16[2048,1408]{1,0:T(8,128)(2,...) custom-call(bf16[2,128,2048]{2,1,0:T(8,128)(2,1)} %tok.3, ...), custom_call_target="tpu_custom_call" | custom-call | tf_op jit(solution)/shard_map/gather_forward/pallas_call | solution.py:809
  343.7 296.7 %backward_scatter.1 = (f32[256,1408]{1,0:T(8,128)}, f32[256,1408]{1,0:T(8,128)}, f32[256,1408]{1,0:T(8,128)}, f32[256,1024]{1,0:T(8,128)}, f32[128,1024]{1,0:T(8...) custom-call(bf16[2,128,2048]{2,1,0:T(8,128)(2,1)} %tok.3, ...), custom_call_target="tpu_custom_call" | custom-call | tf_op jit(solution)/shard_map/backward_scatter/pallas_call | solution.py:1564
  640.4 0.0 copy-start.4
  640.4 0.0 copy-start.5
  640.5 0.9 slice_bitcast_fusion
  641.4 0.6 dynamic_slice.14
  641.9 0.6 dynamic_slice.11
  642.5 1.7 slice.23
  644.2 0.0 copy-start.3
  644.2 1.6 fusion.4
  645.8 0.8 slice.24
  646.6 0.6 dynamic-slice_bitcast_fusion
  647.2 2.3 copy.40
  649.5 0.0 copy-done.4
  649.5 0.0 copy-start.2
  649.5 1.0 copy.41
  650.4 0.0 copy-done.5
  650.4 0.0 copy-start.1
  650.4 0.8 copy.42
  651.2 0.0 copy-done.3
  651.2 1.0 copy.43
  652.2 0.0 copy-done.2
  652.2 0.0 copy-start
  652.2 1.1 copy.44
  653.3 0.0 copy-done.1
  653.3 1.1 copy.45
  654.4 0.0 copy-done
  654.4 1.1 copy.46
  (12 shorter events, 0.1 us)
Async XLA Ops:
  640.4 9.0 %copy-start.4 = (bf16[2,128,2048]{2,1,0:T(8,128)(2,1)S(1)}, bf16[2,128,2048]{2,1,0:T(8,128)(2,1)}, u32[]{:S(2)}) copy-start(bf16[2,128,2048]{2,1,0:T(8,128)(2,1)} %get-tuple-element.95) | copy-start | bytes 3145732
  640.4 10.0 %copy-start.5 = (f32[128,1024]{1,0:T(8,128)S(1)}, f32[128,1024]{1,0:T(8,128)}, u32[]{:S(2)}) copy-start(f32[128,1024]{1,0:T(8,128)} %get-tuple-element.99) | copy-start | bytes 1572868
  644.2 7.0 %copy-start.3 = (f32[256,1024]{1,0:T(8,128)S(1)}, f32[256,1024]{1,0:T(8,128)}, u32[]{:S(2)}) copy-start(f32[256,1024]{1,0:T(8,128)} %get-tuple-element.102) | copy-start | bytes 3145732
  649.5 2.7 copy-start.2
  650.4 2.9 copy-start.1
  652.2 2.2 copy-start

commit v7 on v6

--- a/solution.py
+++ b/solution.py
@@ -1291,7 +1291,7 @@
         for h2 in (0, 1):
             put_rows(proj_v, m, h2, kcols, own, (kv_acc[h2] * scale).astype(BF16))
             put_rows(proj_v, m, h2, vcols, own, kv_acc[2 + h2].astype(BF16))
-        sc.tick(3)
+        sc.tick(4)
     qb_in.wait()
 
     def back_latent(j, _):

time: 665 us -> 672 us (1.011)
  no operation moved by 1% of the time
where the time goes in v7:
time: 672 us; the launch traced here: 661 us
  Pallas kernels  632 us (94%)
  local copies, waits for them, and re-layouts  17.9 us (3%)
  other arithmetic  9.6 us (1%)
    pallas_call x1, Pallas kernels, forward_call(): pl.pallas_call(functools.partial(forward_kernel, (ndp, own, dim, rank, hd...  331 us
    pallas_call x1, Pallas kernels, backward_call(): pl.pallas_call(functools.partial(backward_kernel, (ndp, own, dim, rank, h...  301 us

profile of v7, /device:TPU:0, one launch (start us, length us, event | category | flops | bytes accessed | tf_op | source)
XLA Modules:
  0.0 660.6 jit_solution(11103254033902388058)
XLA Ops:
  0.7 0.1 iota.88
  0.7 0.1 iota.89
  0.8 0.7 broadcast_in_dim.73
  1.5 0.1 broadcast_in_dim.74
  1.6 0.7 broadcast_in_dim.77
  2.2 0.1 broadcast_in_dim.78
  2.3 0.7 convert_element_type.38
  3.0 0.1 broadcast_select_fusion
  3.1 0.1 select_n.50
  3.1 0.6 select_maximum_fusion.gain_sh
  3.8 0.9 convert_reduce_fusion
  4.7 0.1 broadcast_in_dim.69
  4.8 0.1 mul.64
  4.9 0.7 broadcast_compare_fusion
  5.6 0.1 broadcast_in_dim.68
  5.6 0.1 gt.15
  5.7 0.8 fusion.3
  6.5 0.1 convert_bitcast_fusion
  6.6 3.1 multiply_sine_fusion
  9.7 0.7 broadcast_in_dim.70
  10.4 0.1 reshape.146
  10.6 1.0 and_select_fusion.bias
  11.5 1.6 pad_maximum_fusion.seq_sh
  13.2 330.6 %gather_forward.1 = (bf16[1024,1024]{1,0:T(8,128)(2,1)}, bf16[2048,1024]{1,0:T(8,128)(2,1)}, bf16[2048,1408]{1,0:T(8,128)(2,1)}, bf16[2048,1408]{1,0:T(8,128)(2,...) custom-call(bf16[2,128,2048]{2,1,0:T(8,128)(2,1)} %tok.3, ...), custom_call_target="tpu_custom_call" | custom-call | tf_op jit(solution)/shard_map/gather_forward/pallas_call | solution.py:809
  343.7 301.3 %backward_scatter.1 = (f32[256,1408]{1,0:T(8,128)}, f32[256,1408]{1,0:T(8,128)}, f32[256,1408]{1,0:T(8,128)}, f32[256,1024]{1,0:T(8,128)}, f32[128,1024]{1,0:T(8...) custom-call(bf16[2,128,2048]{2,1,0:T(8,128)(2,1)} %tok.3, ...), custom_call_target="tpu_custom_call" | custom-call | tf_op jit(solution)/shard_map/backward_scatter/pallas_call | solution.py:1564
  645.0 0.0 copy-start.4
  645.0 0.0 copy-start.5
  645.1 0.9 slice_bitcast_fusion
  646.0 0.6 dynamic_slice.14
  646.6 0.6 dynamic_slice.11
  647.1 1.7 slice.23
  648.8 0.0 copy-start.3
  648.8 1.6 fusion.4
  650.4 0.8 slice.24
  651.2 0.6 dynamic-slice_bitcast_fusion
  651.8 2.3 copy.40
  654.1 0.0 copy-done.4
  654.1 0.0 copy-start.2
  654.1 1.0 copy.41
  655.0 0.0 copy-done.5
  655.0 0.0 copy-start.1
  655.0 0.8 copy.42
  655.8 0.0 copy-done.3
  655.8 1.0 copy.43
  656.8 0.0 copy-done.2
  656.8 0.0 copy-start
  656.8 1.1 copy.44
  657.9 0.0 copy-done.1
  657.9 1.1 copy.45
  659.0 0.0 copy-done
  659.0 1.1 copy.46
  (12 shorter events, 0.1 us)
Async XLA Ops:
  645.0 9.0 %copy-start.4 = (bf16[2,128,2048]{2,1,0:T(8,128)(2,1)S(1)}, bf16[2,128,2048]{2,1,0:T(8,128)(2,1)}, u32[]{:S(2)}) copy-start(bf16[2,128,2048]{2,1,0:T(8,128)(2,1)} %get-tuple-element.95) | copy-start | bytes 3145732
  645.0 10.0 %copy-start.5 = (f32[128,1024]{1,0:T(8,128)S(1)}, f32[128,1024]{1,0:T(8,128)}, u32[]{:S(2)}) copy-start(f32[128,1024]{1,0:T(8,128)} %get-tuple-element.99) | copy-start | bytes 1572868
  648.8 7.0 %copy-start.3 = (f32[256,1024]{1,0:T(8,128)S(1)}, f32[256,1024]{1,0:T(8,128)}, u32[]{:S(2)}) copy-start(f32[256,1024]{1,0:T(8,128)} %get-tuple-element.102) | copy-start | bytes 3145732
  654.1 2.7 copy-start.2
  655.0 2.9 copy-start.1
  656.8 2.2 copy-start
